TPU v7x, 128 devices: a whole 4x4x4 slice. The times are simulated.
128 devices in a mesh: row: 8 (over x_lo, y), col: 16 (over z, x_hi, core).
Axes of the slice: x: 4 (x_hi: 2, x_lo: 2; x = x_hi * 2 + x_lo), y: 4, z: 4, core: 2. Of those that a mesh axis runs over, the one named last changes fastest.
Arguments:
- features: bfloat16 [65536, 256], P(('col', 'row')), may hold values from -6 to 6
- weight: bfloat16 [256, 256], replicated, may hold values from -0.375 to 0.375
- tile_values: bfloat16 [65536, 128, 128], P(('row', 'col')), may hold values from -0.046875 to 0.046875
- tile_row: int32 [65536], P(('row', 'col')), may hold values from 0 to 63, as said below
- tile_col: int32 [65536], P(('row', 'col')), may hold values from 0 to 31, as said below
- tile_count: int32 [8, 16], P('row', 'col'), may hold values from 128 to 512, as said below
- cotangent: bfloat16 [65536, 256], P(('row', 'col')), may hold values from -6 to 6
Outputs:
- activated: bfloat16 [65536, 256], P(('row', 'col'))
- grad_features: bfloat16 [65536, 256], P(('col', 'row'))
- grad_weight: float32 [256, 256], replicated
Inputs may be any that keep to these rules, and one draw needn't show every extreme that they name: `tile_count`: 512 on at least one device in every draw. Within each device's slots the pairs (tile_row, tile_col) are distinct. Within each device's slots the pairs (tile_row, tile_col) are distinct.
All inputs are finite; a program needn't handle non-finite values.
Results may differ from a plain program's by a relative error of at most 0.024.
Values may be sent and summed in bfloat16 or wider, within the bound.
A program may use at most 128 MiB of HBM per device.

v0:
```python
import math

import jax
import jax.numpy as jnp
from jax import lax
from jax.sharding import PartitionSpec as P


def silu_slope(values):
    sigma = jax.nn.sigmoid(values)
    return sigma * (1.0 + values * (1.0 - sigma))


def tile_products(tile_values, fetch_index, place_index, live_mask, source, out_tiles, forward):
    slots = tile_values.shape[0]
    tile_size = tile_values.shape[1]
    hidden = source.shape[-1]
    source_tiles = source.shape[0]
    source_flat = source.reshape(source_tiles, tile_size * hidden)
    group_size = math.gcd(slots, 64)
    turn_count = slots // group_size
    source_ids = jnp.arange(source_tiles, dtype=jnp.int32)
    out_ids = jnp.arange(out_tiles, dtype=jnp.int32)

    def step(running, step_index):
        offset = step_index * group_size
        blocks = lax.dynamic_slice_in_dim(tile_values, offset, group_size, 0)
        take = lax.dynamic_slice_in_dim(fetch_index, offset, group_size, 0)
        place = lax.dynamic_slice_in_dim(place_index, offset, group_size, 0)
        live_part = lax.dynamic_slice_in_dim(live_mask, offset, group_size, 0)
        take_onehot = (take[:, None] == source_ids[None, :]).astype(jnp.bfloat16)
        fetched = jnp.dot(take_onehot, source_flat, preferred_element_type=jnp.float32)
        fetched = fetched.astype(jnp.bfloat16).reshape(group_size, tile_size, hidden)
        if forward:
            product = jnp.einsum(
                "sab,sbf->saf", blocks, fetched, preferred_element_type=jnp.float32
            )
        else:
            product = jnp.einsum(
                "sab,saf->sbf", blocks, fetched, preferred_element_type=jnp.float32
            )
        place_onehot = (place[:, None] == out_ids[None, :]).astype(jnp.float32) * live_part[:, None]
        added = lax.dot_general(
            place_onehot,
            product.reshape(group_size, tile_size * hidden),
            (((0,), (0,)), ((), ())),
            precision=lax.Precision.HIGHEST,
            preferred_element_type=jnp.float32,
        )
        return (running + added, None)

    start_value = jnp.zeros((out_tiles, tile_size * hidden), jnp.float32)
    result = lax.scan(step, start_value, jnp.arange(turn_count, dtype=jnp.int32))[0]
    return result.reshape(out_tiles * tile_size, hidden)


def body(features, weight, tile_values, tile_row, tile_col, tile_count, cotangent):
    row_count = lax.axis_size("row")
    col_count = lax.axis_size("col")
    node_dev = features.shape[0]
    hidden = features.shape[1]
    tile_size = tile_values.shape[1]
    slots = tile_values.shape[0]
    row_tiles = node_dev * col_count // tile_size
    col_tiles = node_dev * row_count // tile_size
    live_mask = (jnp.arange(slots, dtype=jnp.int32) < tile_count[0, 0]).astype(jnp.float32)
    projected = jnp.dot(features, weight, preferred_element_type=jnp.float32).astype(jnp.bfloat16)
    panel_rows = lax.all_gather(projected, "row", axis=0, tiled=True).reshape(
        col_tiles, tile_size, hidden
    )
    forward_part = tile_products(
        tile_values, tile_col, tile_row, live_mask, panel_rows, row_tiles, True
    )
    forward_part = forward_part.astype(jnp.bfloat16)
    summed = lax.psum_scatter(forward_part, "col", scatter_dimension=0, tiled=True).astype(
        jnp.float32
    )
    activated = jax.nn.silu(summed).astype(jnp.bfloat16)
    slope = (cotangent.astype(jnp.float32) * silu_slope(summed)).astype(jnp.bfloat16)
    slope_full = lax.all_gather(slope, "col", axis=0, tiled=True)
    slope_tiles = slope_full.reshape(row_tiles, tile_size, hidden)
    column_part = tile_products(
        tile_values, tile_row, tile_col, live_mask, slope_tiles, col_tiles, False
    )
    column_part = column_part.astype(jnp.bfloat16)
    grad_nodes = (
        lax.psum_scatter(column_part, "row", scatter_dimension=0, tiled=True)
        .astype(jnp.float32)
        .astype(jnp.bfloat16)
    )
    grad_features = lax.dot_general(
        grad_nodes, weight, (((1,), (1,)), ((), ())), preferred_element_type=jnp.float32
    ).astype(jnp.bfloat16)
    weight_term = lax.dot_general(
        features, grad_nodes, (((0,), (0,)), ((), ())), preferred_element_type=jnp.float32
    )
    grad_weight = lax.psum(weight_term, ("row", "col"))
    return (activated, grad_features, grad_weight)


def solution(mesh):
    placed = (
        P(("col", "row"), None),
        P(),
        P(("row", "col"), None, None),
        P(("row", "col")),
        P(("row", "col")),
        P("row", "col"),
        P(("row", "col"), None),
    )
    return jax.shard_map(
        body,
        mesh=mesh,
        in_specs=placed,
        out_specs=(P(("row", "col"), None), P(("col", "row"), None), P()),
        check_vma=False,
    )
```

profile of v0, /device:TPU:1, one launch (start us, length us, event | category | flops | bytes accessed | tf_op | source)
XLA Modules:
  0.0 843.4 jit_solution(16008225680619883002)
XLA Ops:
  10.7 39.1 %all-gather.3.cloned.1.call-done = bf16[4096,256]{1,0:T(8,128)(2,1)} async-done(((bf16[512,256]{1,0:T(8,128)(2,1)}), bf16[4096,256]{1,0:T(8,128)(2,1)}) %all-gather.3.cloned.1.call-update) | async-done | bytes 2097168 | tf_op jit(solution)/shard_map/all_gather | solution.py:68
  52.7 223.3 %while.22 = (s32[]{:T(128)}, f32[64,32768]{1,0:T(8,128)}, s32[8]{0:T(128)S(1)}, s32[512]{0:T(512)S(1)}, f32[512]{0:T(512)S(1)}, /*index=5*/bf16[512,128,128]{2,1...) while((s32[]{:T(128)}, f32[64,32768]{1,0:T(8,128)}, ...), condition=%wide.region_1.2_spmd.clone, body=%wide.region_0.1_spmd.clone.sunk | while | flops 2288003072 | bytes 71305672 | solution.py:53
  59.3 8.0 copy.22
  67.4 12.1 %convolution_add_fusion.4 = f32[64,32768]{1,0:T(8,128)} fusion(f32[64,32768]{1,0:T(8,128)} %bitcast.61, f32[64,32768]{1,0:T(8,128)} %get-tuple-element.327, pred[]{:T(512)S(6)} %compare.6, f32[64]{0:T(128)S(1)} %dynamic_slice.58, s32[64]{0:T(128)S(1)} %dynamic_slice.59), kind=kOutput, calls=%fused_computation.4.clone.1 | convolution fusion | flops 1614815232 | bytes 25166336 | tf_op jit(solution)/shard_map/while/body/eval_jaxpr/dot_general | solution.py:43
  86.1 8.0 copy.22
  94.2 13.4 %convolution_add_fusion.4 = f32[64,32768]{1,0:T(8,128)} fusion(f32[64,32768]{1,0:T(8,128)} %bitcast.61, f32[64,32768]{1,0:T(8,128)} %get-tuple-element.327, pred[]{:T(512)S(6)} %compare.6, f32[64]{0:T(128)S(1)} %dynamic_slice.58, s32[64]{0:T(128)S(1)} %dynamic_slice.59), kind=kOutput, calls=%fused_computation.4.clone.1 | convolution fusion | flops 1614815232 | bytes 25166336 | tf_op jit(solution)/shard_map/while/body/eval_jaxpr/dot_general | solution.py:43
  114.1 8.0 copy.22
  122.2 13.4 %convolution_add_fusion.4 = f32[64,32768]{1,0:T(8,128)} fusion(f32[64,32768]{1,0:T(8,128)} %bitcast.61, f32[64,32768]{1,0:T(8,128)} %get-tuple-element.327, pred[]{:T(512)S(6)} %compare.6, f32[64]{0:T(128)S(1)} %dynamic_slice.58, s32[64]{0:T(128)S(1)} %dynamic_slice.59), kind=kOutput, calls=%fused_computation.4.clone.1 | convolution fusion | flops 1614815232 | bytes 25166336 | tf_op jit(solution)/shard_map/while/body/eval_jaxpr/dot_general | solution.py:43
  142.2 8.0 copy.22
  150.3 13.4 %convolution_add_fusion.4 = f32[64,32768]{1,0:T(8,128)} fusion(f32[64,32768]{1,0:T(8,128)} %bitcast.61, f32[64,32768]{1,0:T(8,128)} %get-tuple-element.327, pred[]{:T(512)S(6)} %compare.6, f32[64]{0:T(128)S(1)} %dynamic_slice.58, s32[64]{0:T(128)S(1)} %dynamic_slice.59), kind=kOutput, calls=%fused_computation.4.clone.1 | convolution fusion | flops 1614815232 | bytes 25166336 | tf_op jit(solution)/shard_map/while/body/eval_jaxpr/dot_general | solution.py:43
  170.3 8.0 copy.22
  178.4 13.4 %convolution_add_fusion.4 = f32[64,32768]{1,0:T(8,128)} fusion(f32[64,32768]{1,0:T(8,128)} %bitcast.61, f32[64,32768]{1,0:T(8,128)} %get-tuple-element.327, pred[]{:T(512)S(6)} %compare.6, f32[64]{0:T(128)S(1)} %dynamic_slice.58, s32[64]{0:T(128)S(1)} %dynamic_slice.59), kind=kOutput, calls=%fused_computation.4.clone.1 | convolution fusion | flops 1614815232 | bytes 25166336 | tf_op jit(solution)/shard_map/while/body/eval_jaxpr/dot_general | solution.py:43
  198.3 8.0 copy.22
  206.4 13.4 %convolution_add_fusion.4 = f32[64,32768]{1,0:T(8,128)} fusion(f32[64,32768]{1,0:T(8,128)} %bitcast.61, f32[64,32768]{1,0:T(8,128)} %get-tuple-element.327, pred[]{:T(512)S(6)} %compare.6, f32[64]{0:T(128)S(1)} %dynamic_slice.58, s32[64]{0:T(128)S(1)} %dynamic_slice.59), kind=kOutput, calls=%fused_computation.4.clone.1 | convolution fusion | flops 1614815232 | bytes 25166336 | tf_op jit(solution)/shard_map/while/body/eval_jaxpr/dot_general | solution.py:43
  226.4 8.0 copy.22
  234.5 13.4 %convolution_add_fusion.4 = f32[64,32768]{1,0:T(8,128)} fusion(f32[64,32768]{1,0:T(8,128)} %bitcast.61, f32[64,32768]{1,0:T(8,128)} %get-tuple-element.327, pred[]{:T(512)S(6)} %compare.6, f32[64]{0:T(128)S(1)} %dynamic_slice.58, s32[64]{0:T(128)S(1)} %dynamic_slice.59), kind=kOutput, calls=%fused_computation.4.clone.1 | convolution fusion | flops 1614815232 | bytes 25166336 | tf_op jit(solution)/shard_map/while/body/eval_jaxpr/dot_general | solution.py:43
  254.5 8.0 copy.22
  262.6 13.4 %convolution_add_fusion.4 = f32[64,32768]{1,0:T(8,128)} fusion(f32[64,32768]{1,0:T(8,128)} %bitcast.61, f32[64,32768]{1,0:T(8,128)} %get-tuple-element.327, pred[]{:T(512)S(6)} %compare.6, f32[64]{0:T(128)S(1)} %dynamic_slice.58, s32[64]{0:T(128)S(1)} %dynamic_slice.59), kind=kOutput, calls=%fused_computation.4.clone.1 | convolution fusion | flops 1614815232 | bytes 25166336 | tf_op jit(solution)/shard_map/while/body/eval_jaxpr/dot_general | solution.py:43
  276.0 5.7 convert_element_type.47
  281.7 7.4 convert_element_type.48
  289.2 83.9 %reduce-scatter.3.cloned.1.call-done = bf16[512,256]{1,0:T(8,128)(2,1)} async-done(((bf16[8192,256]{1,0:T(8,128)(2,1)}), bf16[512,256]{1,0:T(8,128)(2,1)}) %reduce-scatter.3.cloned.1.call-update) | async-done | bytes 262160 | tf_op jit(solution)/shard_map/reduce_scatter | solution.py:75
  375.2 57.3 %all-gather.5.cloned.1.call-done = bf16[8192,256]{1,0:T(8,128)(2,1)} async-done(((bf16[512,256]{1,0:T(8,128)(2,1)}), bf16[8192,256]{1,0:T(8,128)(2,1)}) %all-gather.5.cloned.1.call-update) | async-done | bytes 4194320 | tf_op jit(solution)/shard_map/all_gather | solution.py:80
  432.5 7.4 reshape_reshape.7
  439.9 204.1 %while.23 = (s32[]{:T(128)}, f32[32,32768]{1,0:T(8,128)}, s32[8]{0:T(128)S(1)}, s32[512]{0:T(512)S(1)}, f32[512]{0:T(512)S(1)}, /*index=5*/bf16[512,128,128]{2,1...) while((s32[]{:T(128)}, f32[32,32768]{1,0:T(8,128)}, ...), condition=%wide.region_4.5_spmd.clone, body=%wide.region_3.4_spmd.clone.sunk | while | flops 1614815232 | bytes 65014216 | solution.py:53
  441.2 3.5 convolution_convert_fusion.7
  448.7 8.0 copy.24
  456.8 8.0 convolution_add_fusion.5
  466.1 3.5 convolution_convert_fusion.7
  473.6 8.0 copy.24
  481.7 8.7 %convolution_add_fusion.5 = f32[32,32768]{1,0:T(8,128)} fusion(f32[64,32768]{1,0:T(8,128)} %bitcast.58, f32[32,32768]{1,0:T(8,128)} %get-tuple-element.363, pred[]{:T(512)S(6)} %compare.7, f32[64]{0:T(128)S(1)} %dynamic_slice.63, s32[64]{0:T(128)S(1)} %dynamic_slice.64), kind=kOutput, calls=%fused_computation.18.clone.1 | convolution fusion | flops 807407616 | bytes 16777728 | tf_op jit(solution)/shard_map/while/body/eval_jaxpr/dot_general | solution.py:43
  499.2 8.0 copy.24
  507.3 8.7 %convolution_add_fusion.5 = f32[32,32768]{1,0:T(8,128)} fusion(f32[64,32768]{1,0:T(8,128)} %bitcast.58, f32[32,32768]{1,0:T(8,128)} %get-tuple-element.363, pred[]{:T(512)S(6)} %compare.7, f32[64]{0:T(128)S(1)} %dynamic_slice.63, s32[64]{0:T(128)S(1)} %dynamic_slice.64), kind=kOutput, calls=%fused_computation.18.clone.1 | convolution fusion | flops 807407616 | bytes 16777728 | tf_op jit(solution)/shard_map/while/body/eval_jaxpr/dot_general | solution.py:43
  517.3 3.5 convolution_convert_fusion.7
  524.8 8.0 copy.24
  532.9 8.7 %convolution_add_fusion.5 = f32[32,32768]{1,0:T(8,128)} fusion(f32[64,32768]{1,0:T(8,128)} %bitcast.58, f32[32,32768]{1,0:T(8,128)} %get-tuple-element.363, pred[]{:T(512)S(6)} %compare.7, f32[64]{0:T(128)S(1)} %dynamic_slice.63, s32[64]{0:T(128)S(1)} %dynamic_slice.64), kind=kOutput, calls=%fused_computation.18.clone.1 | convolution fusion | flops 807407616 | bytes 16777728 | tf_op jit(solution)/shard_map/while/body/eval_jaxpr/dot_general | solution.py:43
  550.4 8.0 copy.24
  558.5 8.7 %convolution_add_fusion.5 = f32[32,32768]{1,0:T(8,128)} fusion(f32[64,32768]{1,0:T(8,128)} %bitcast.58, f32[32,32768]{1,0:T(8,128)} %get-tuple-element.363, pred[]{:T(512)S(6)} %compare.7, f32[64]{0:T(128)S(1)} %dynamic_slice.63, s32[64]{0:T(128)S(1)} %dynamic_slice.64), kind=kOutput, calls=%fused_computation.18.clone.1 | convolution fusion | flops 807407616 | bytes 16777728 | tf_op jit(solution)/shard_map/while/body/eval_jaxpr/dot_general | solution.py:43
  568.5 3.5 convolution_convert_fusion.7
  576.0 8.0 copy.24
  584.1 8.7 %convolution_add_fusion.5 = f32[32,32768]{1,0:T(8,128)} fusion(f32[64,32768]{1,0:T(8,128)} %bitcast.58, f32[32,32768]{1,0:T(8,128)} %get-tuple-element.363, pred[]{:T(512)S(6)} %compare.7, f32[64]{0:T(128)S(1)} %dynamic_slice.63, s32[64]{0:T(128)S(1)} %dynamic_slice.64), kind=kOutput, calls=%fused_computation.18.clone.1 | convolution fusion | flops 807407616 | bytes 16777728 | tf_op jit(solution)/shard_map/while/body/eval_jaxpr/dot_general | solution.py:43
  594.1 3.5 convolution_convert_fusion.7
  601.6 8.0 copy.24
  609.7 8.7 %convolution_add_fusion.5 = f32[32,32768]{1,0:T(8,128)} fusion(f32[64,32768]{1,0:T(8,128)} %bitcast.58, f32[32,32768]{1,0:T(8,128)} %get-tuple-element.363, pred[]{:T(512)S(6)} %compare.7, f32[64]{0:T(128)S(1)} %dynamic_slice.63, s32[64]{0:T(128)S(1)} %dynamic_slice.64), kind=kOutput, calls=%fused_computation.18.clone.1 | convolution fusion | flops 807407616 | bytes 16777728 | tf_op jit(solution)/shard_map/while/body/eval_jaxpr/dot_general | solution.py:43
  619.7 3.5 convolution_convert_fusion.7
  627.2 8.0 copy.24
  635.3 8.7 %convolution_add_fusion.5 = f32[32,32768]{1,0:T(8,128)} fusion(f32[64,32768]{1,0:T(8,128)} %bitcast.58, f32[32,32768]{1,0:T(8,128)} %get-tuple-element.363, pred[]{:T(512)S(6)} %compare.7, f32[64]{0:T(128)S(1)} %dynamic_slice.63, s32[64]{0:T(128)S(1)} %dynamic_slice.64), kind=kOutput, calls=%fused_computation.18.clone.1 | convolution fusion | flops 807407616 | bytes 16777728 | tf_op jit(solution)/shard_map/while/body/eval_jaxpr/dot_general | solution.py:43
  648.8 35.1 %reduce-scatter.5.cloned.1.call-done = bf16[512,256]{1,0:T(8,128)(2,1)} async-done(((bf16[4096,256]{1,0:T(8,128)(2,1)}), bf16[512,256]{1,0:T(8,128)(2,1)}) %reduce-scatter.5.cloned.1.call-update) | async-done | bytes 262160 | tf_op jit(solution)/shard_map/reduce_scatter | solution.py:87
  687.8 147.3 %all-reduce.2.cloned.1.call-done = f32[256,256]{0,1:T(8,128)} async-done(((f32[256,256]{0,1:T(8,128)}), f32[256,256]{0,1:T(8,128)}) %all-reduce.2.cloned.1.call-update) | async-done | bytes 262160 | tf_op jit(solution)/shard_map/psum | solution.py:97
  (139 shorter events, 112.1 us)
Async XLA Ops:
  7.2 1.0 copy-start
  7.2 45.5 %copy-start.3 = (s32[512]{0:T(512)S(1)}, s32[512]{0:T(512)}, u32[]{:S(2)}) copy-start(s32[512]{0:T(512)} %param.14) | copy-start | bytes 6148
  7.2 45.5 %copy-start.4 = (s32[512]{0:T(512)S(1)}, s32[512]{0:T(512)}, u32[]{:S(2)}) copy-start(s32[512]{0:T(512)} %param.15) | copy-start | bytes 6148
  7.2 42.6 %all-gather.3.cloned.1.call-start = ((), (), s32[]{:S(2)}) async-start(), calls=%async_computation.2 | async-start | bytes 2359296 | tf_op jit(solution)/shard_map/all_gather | solution.py:68
  10.0 363.2 %reduce-scatter.3.cloned.1.call-start = ((), (), s32[]{:S(2)}) async-start(), calls=%async_computation.3 | async-start | bytes 4456448 | tf_op jit(solution)/shard_map/reduce_scatter | solution.py:75
  289.1 84.0 %copy-start.2 = (bf16[512,256]{1,0:T(8,128)(2,1)S(1)}, bf16[512,256]{1,0:T(8,128)(2,1)}, u32[]{:S(2)}) copy-start(bf16[512,256]{1,0:T(8,128)(2,1)} %param.17) | copy-start | bytes 786436
  289.2 143.4 %all-gather.5.cloned.1.call-start = ((), (), s32[]{:S(2)}) async-start(), calls=%async_computation.4 | async-start | bytes 4456448 | tf_op jit(solution)/shard_map/all_gather | solution.py:80
  375.2 308.7 %reduce-scatter.5.cloned.1.call-start = ((), (), s32[]{:S(2)}) async-start(), calls=%async_computation.5 | async-start | bytes 2359296 | tf_op jit(solution)/shard_map/reduce_scatter | solution.py:87
  646.4 39.5 %copy-start.1 = (bf16[256,256]{1,0:T(8,128)(2,1)S(1)}, bf16[256,256]{1,0:T(8,128)(2,1)}, u32[]{:S(2)}) copy-start(bf16[256,256]{1,0:T(8,128)(2,1)} %param.12) | copy-start | bytes 393220
  648.8 186.3 %all-reduce.2.cloned.1.call-start = ((), (), s32[]{:S(2)}) async-start(), calls=%async_computation.6 | async-start | bytes 524288 | tf_op jit(solution)/shard_map/psum | solution.py:97
Sparse Core Ops, SparseCore 0:
  10.3 39.4 all-gather.2
  289.3 83.8 reduce-scatter.2
  376.5 55.9 all-gather.4
  648.9 34.9 reduce-scatter.4
  689.8 145.2 all-reduce.1
where the time goes:
time: 845 us; the launch traced here: 843 us
  waiting for transfers between devices  363 us (43%)
  matrix products  264 us (31%)
  local copies, waits for them, and re-layouts  180 us (21%)
  between operations  14.5 us (2%)
  loops' own time  10.8 us (1%)
  other arithmetic  10.1 us (1%)
    dot_general x16, matrix products, step(): lax.dot_general(place_onehot, product.reshape(group_size, tile_size * hid...  175 us
    psum x1, waiting for transfers between devices, body(): grad_weight = lax.psum(weight_term, ('row', 'col'))  147 us
    while x32, local copies, waits for them, and re-layouts  145 us
    reduce_scatter x1, waiting for transfers between devices, body(): lax.psum_scatter(forward_part, 'col', scatter_dimension=0, tiled=True)  83.9 us
    all_gather x1, waiting for transfers between devices, body(): slope_full = lax.all_gather(slope, 'col', axis=0, tiled=True)  57.3 us
    all_gather x1, waiting for transfers between devices, body(): lax.all_gather(projected, 'row', axis=0, tiled=True)  39.1 us
    dot_general x16, matrix products, step(): jnp.dot(take_onehot, source_flat, preferred_element_type=jnp.float32)  38.1 us
    reduce_scatter x1, waiting for transfers between devices, body(): lax.psum_scatter(column_part, 'row', scatter_dimension=0, tiled=True)  35.1 us
  transfers between devices with their start and end apart: 5, of which 5 were waited for; matrix products, arithmetic and copies ran while one was open for 0% of the time, Pallas kernels for 0%

commit v1 on v0

v1 whole, which is shorter than its diff:
```python
import functools

import jax
import jax.numpy as jnp
from jax import lax
from jax.experimental import pallas as pl
from jax.experimental.pallas import tpu as pltpu
from jax.sharding import PartitionSpec as P


GROUP = 32
CHUNK = 256


def silu_slope(values):
    sigma = jax.nn.sigmoid(values)
    return sigma * (1.0 + values * (1.0 - sigma))


def tile_kernel(count_ref, place_ref, fetch_ref, tiles_ref, src_ref, out_ref, acc_ref, *, forward):
    step = pl.program_id(0)
    tile = tiles_ref.shape[1]
    group = tiles_ref.shape[0]
    out_rows = acc_ref.shape[0]

    @pl.when(step == 0)
    def _():
        def zero(k, carry):
            rows = pl.ds(pl.multiple_of(k * CHUNK, CHUNK), CHUNK)
            acc_ref[rows, :] = jnp.zeros((CHUNK, acc_ref.shape[1]), jnp.float32)
            return carry

        lax.fori_loop(0, out_rows // CHUNK, zero, 0)

    base = step * group
    live = jnp.clip(count_ref[0] - base, 0, group)

    def body(j, carry):
        slot = base + j
        src_rows = pl.ds(pl.multiple_of(fetch_ref[slot] * tile, tile), tile)
        dst_rows = pl.ds(pl.multiple_of(place_ref[slot] * tile, tile), tile)
        block = tiles_ref[j]
        src = src_ref[src_rows, :]
        if forward:
            prod = jnp.dot(block, src, preferred_element_type=jnp.float32)
        else:
            prod = lax.dot_general(
                block, src, (((0,), (0,)), ((), ())), preferred_element_type=jnp.float32
            )
        acc_ref[dst_rows, :] += prod
        return carry

    lax.fori_loop(0, live, body, 0)

    @pl.when(step == pl.num_programs(0) - 1)
    def _():
        def emit(k, carry):
            rows = pl.ds(pl.multiple_of(k * CHUNK, CHUNK), CHUNK)
            out_ref[rows, :] = acc_ref[rows, :].astype(out_ref.dtype)
            return carry

        lax.fori_loop(0, out_rows // CHUNK, emit, 0)


def tile_products(tile_values, fetch_index, place_index, count, source, out_tiles, forward):
    slots, tile, _ = tile_values.shape
    hidden = source.shape[-1]
    src_rows = source.shape[0]
    out_rows = out_tiles * tile
    group = GROUP
    steps = slots // group

    def tiles_map(i, count_ref, place_ref, fetch_ref):
        last = jnp.maximum(count_ref[0] - 1, 0) // group
        return (jnp.minimum(i, last), 0, 0)

    grid_spec = pltpu.PrefetchScalarGridSpec(
        num_scalar_prefetch=3,
        grid=(steps,),
        in_specs=[
            pl.BlockSpec((group, tile, tile), tiles_map),
            pl.BlockSpec((src_rows, hidden), lambda i, *_: (0, 0)),
        ],
        out_specs=pl.BlockSpec((out_rows, hidden), lambda i, *_: (0, 0)),
        scratch_shapes=[pltpu.VMEM((out_rows, hidden), jnp.float32)],
    )
    flops = 2 * slots * tile * tile * hidden
    return pl.pallas_call(
        functools.partial(tile_kernel, forward=forward),
        grid_spec=grid_spec,
        out_shape=jax.ShapeDtypeStruct((out_rows, hidden), jnp.bfloat16),
        compiler_params=pltpu.CompilerParams(
            dimension_semantics=("arbitrary",), vmem_limit_bytes=48 * 1024 * 1024
        ),
        cost_estimate=pl.CostEstimate(
            flops=flops,
            bytes_accessed=slots * tile * tile * 2 + src_rows * hidden * 2 + out_rows * hidden * 2,
            transcendentals=0,
        ),
    )(count, place_index, fetch_index, tile_values, source)


def body(features, weight, tile_values, tile_row, tile_col, tile_count, cotangent):
    row_count = lax.axis_size("row")
    col_count = lax.axis_size("col")
    node_dev = features.shape[0]
    tile_size = tile_values.shape[1]
    row_tiles = node_dev * col_count // tile_size
    col_tiles = node_dev * row_count // tile_size
    count = tile_count.reshape(1)
    projected = jnp.dot(features, weight, preferred_element_type=jnp.float32).astype(jnp.bfloat16)
    panel_rows = lax.all_gather(projected, "row", axis=0, tiled=True)
    forward_part = tile_products(
        tile_values, tile_col, tile_row, count, panel_rows, row_tiles, True
    )
    summed = lax.psum_scatter(forward_part, "col", scatter_dimension=0, tiled=True).astype(
        jnp.float32
    )
    activated = jax.nn.silu(summed).astype(jnp.bfloat16)
    slope = (cotangent.astype(jnp.float32) * silu_slope(summed)).astype(jnp.bfloat16)
    slope_full = lax.all_gather(slope, "col", axis=0, tiled=True)
    column_part = tile_products(
        tile_values, tile_row, tile_col, count, slope_full, col_tiles, False
    )
    grad_nodes = (
        lax.psum_scatter(column_part, "row", scatter_dimension=0, tiled=True)
        .astype(jnp.float32)
        .astype(jnp.bfloat16)
    )
    grad_features = lax.dot_general(
        grad_nodes, weight, (((1,), (1,)), ((), ())), preferred_element_type=jnp.float32
    ).astype(jnp.bfloat16)
    weight_term = lax.dot_general(
        features, grad_nodes, (((0,), (0,)), ((), ())), preferred_element_type=jnp.float32
    )
    grad_weight = lax.psum(weight_term, ("row", "col"))
    return (activated, grad_features, grad_weight)


def solution(mesh):
    placed = (
        P(("col", "row"), None),
        P(),
        P(("row", "col"), None, None),
        P(("row", "col")),
        P(("row", "col")),
        P("row", "col"),
        P(("row", "col"), None),
    )
    return jax.shard_map(
        body,
        mesh=mesh,
        in_specs=placed,
        out_specs=(P(("row", "col"), None), P(("col", "row"), None), P()),
        check_vma=False,
    )
```

time: 845 us -> 576 us (0.68)
  matrix products: 264 us -> 5.67 us
  local copies, waits for them, and re-layouts: 180 us -> 5.65 us
  Pallas kernels: 0 us -> 163 us
  waiting for transfers between devices: 363 us -> 384 us
  loops' own time: 10.8 us -> 0 us
    dot_general x48 -> x0, matrix products: 259 us -> none  [the longest x16 175 us: step(): lax.dot_general(place_onehot, product.reshape(group_size, tile_size * hid...]
    pallas_call x0 -> x2, Pallas kernels: none -> 163 us  [tile_products(): pl.pallas_call(functools.partial(tile_kernel, forward=forward), grid_spec...]
    while x32 -> x0, local copies, waits for them, and re-layouts: 145 us -> none
    reduce_scatter x1, waiting for transfers between devices: 35.1 us -> 49.1 us  [body(): lax.psum_scatter(column_part, 'row', scatter_dimension=0, tiled=True)]
    dynamic_slice x64 -> x0, local copies, waits for them, and re-layouts: 12.9 us -> none  [the longest x16 9.32 us: tile_products(): lax.scan(step, start_value, jnp.arange(turn_count, dtype=jnp.int32))[0]]
    another operation x2 -> x0, loops' own time: 10.8 us -> none  [tile_products(): lax.scan(step, start_value, jnp.arange(turn_count, dtype=jnp.int32))[0]]
    another operation x2 -> x0, local copies, waits for them, and re-layouts: 10.2 us -> none  [tile_products(): source_flat = source.reshape(source_tiles, tile_size * hidden)]
    convert_element_type x2 -> x0, local copies, waits for them, and re-layouts: 9.8 us -> none  [the longest x1 7.44 us: body(): forward_part = forward_part.astype(jnp.bfloat16)]
where the time goes in v1:
time: 576 us; the launch traced here: 575 us
  waiting for transfers between devices  384 us (67%)
  Pallas kernels  163 us (28%)
  between operations  14.4 us (2%)
    pallas_call x2, Pallas kernels, tile_products(): pl.pallas_call(functools.partial(tile_kernel, forward=forward), grid_spec...  163 us
    psum x1, waiting for transfers between devices, body(): grad_weight = lax.psum(weight_term, ('row', 'col'))  148 us
    reduce_scatter x1, waiting for transfers between devices, body(): lax.psum_scatter(forward_part, 'col', scatter_dimension=0, tiled=True)  91.1 us
    all_gather x1, waiting for transfers between devices, body(): slope_full = lax.all_gather(slope, 'col', axis=0, tiled=True)  57.3 us
    reduce_scatter x1, waiting for transfers between devices, body(): lax.psum_scatter(column_part, 'row', scatter_dimension=0, tiled=True)  49.1 us
    all_gather x1, waiting for transfers between devices, body(): panel_rows = lax.all_gather(projected, 'row', axis=0, tiled=True)  39.1 us
  transfers between devices with their start and end apart: 5, of which 5 were waited for; matrix products, arithmetic and copies ran while one was open for 0% of the time, Pallas kernels for 0%

profile of v1, /device:TPU:1, one launch (start us, length us, event | category | flops | bytes accessed | tf_op | source)
XLA Modules:
  0.0 575.3 jit_solution(12326846144410468598)
XLA Ops:
  7.2 0.0 copy-start
  7.2 0.0 all-gather.3.cloned.1.call-start
  7.2 0.9 copy-done
  8.1 1.8 convolution_convert_fusion.1
  10.0 0.0 all-gather.3.cloned.1.call-update
  10.0 0.0 reduce-scatter.3.cloned.1.call-start
  10.7 39.1 %all-gather.3.cloned.1.call-done.src_ref = bf16[4096,256]{1,0:T(8,128)(2,1)} async-done(((bf16[512,256]{1,0:T(8,128)(2,1)}), bf16[4096,256]{1,0:T(8,128)(2,1)}) %all-gather.3.cloned.1.call-update) | async-done | bytes 2097168 | tf_op jit(solution)/shard_map/all_gather | solution.py:112
  49.7 0.0 copy-start.1
  49.7 1.6 copy-done.1
  51.3 0.0 copy-start.2
  51.3 0.7 copy-done.2
  52.0 0.0 copy-start.4
  52.0 0.7 copy-done.4
  52.7 71.1 %shard_map.94 = bf16[8192,256]{1,0:T(8,128)(2,1)} custom-call(s32[1]{0:T(128)} %bitcast.9.count_ref, s32[512]{0:T(512)S(1)} %copy-done.2, s32[512]{0:T(512)S(1)} %copy-done.4, bf16[512,128,128]{2,1,0:T(8,128)(2,1)} %tiles_ref.3, bf16[4096,256]{1,0:T(8,128)(2,1)S(1)} %copy-done.1), custom_call_target="tpu_custom_call" | custom-call | flops 4294967296 | bytes 23068672 | tf_op jit(solution)/shard_map/pallas_call | solution.py:88
  123.8 0.0 copy-start.7
  123.8 0.0 copy-start.3
  123.8 0.0 copy-start.5
  123.8 0.0 reduce-scatter.3.cloned.1.call-update
  123.8 0.0 all-gather.5.cloned.1.call-start
  123.8 91.1 %reduce-scatter.3.cloned.1.call-done = bf16[512,256]{1,0:T(8,128)(2,1)} async-done(((bf16[8192,256]{1,0:T(8,128)(2,1)}), bf16[512,256]{1,0:T(8,128)(2,1)}) %reduce-scatter.3.cloned.1.call-update) | async-done | bytes 262160 | tf_op jit(solution)/shard_map/reduce_scatter | solution.py:116
  215.0 0.0 copy-done.7
  215.0 2.0 fusion.7
  217.0 0.0 all-gather.5.cloned.1.call-update
  217.0 0.0 reduce-scatter.5.cloned.1.call-start
  217.0 57.3 %all-gather.5.cloned.1.call-done.src_ref = bf16[8192,256]{1,0:T(8,128)(2,1)} async-done(((bf16[512,256]{1,0:T(8,128)(2,1)}), bf16[8192,256]{1,0:T(8,128)(2,1)}) %all-gather.5.cloned.1.call-update) | async-done | bytes 4194320 | tf_op jit(solution)/shard_map/all_gather | solution.py:121
  274.4 0.0 copy-done.3
  274.4 0.0 copy-done.5
  274.4 0.0 copy-start.6
  274.4 92.1 %shard_map.95 = bf16[4096,256]{1,0:T(8,128)(2,1)} custom-call(s32[1]{0:T(128)} %bitcast.10.count_ref, s32[512]{0:T(512)S(1)} %copy-done.5, s32[512]{0:T(512)S(1)} %copy-done.3, bf16[512,128,128]{2,1,0:T(8,128)(2,1)} %tiles_ref.3, bf16[8192,256]{1,0:T(8,128)(2,1)} %all-gather.5.cloned.1.call-done.src_ref), custom_call_target="tpu_custom_call" | custom-call | flops 4294967296 | bytes 23068672 | tf_op jit(solution)/shard_map/pallas_call | solution.py:88
  366.5 0.0 reduce-scatter.5.cloned.1.call-update
  366.5 0.0 all-reduce.2.cloned.1.call-start
  366.5 49.1 %reduce-scatter.5.cloned.1.call-done = bf16[512,256]{1,0:T(8,128)(2,1)} async-done(((bf16[4096,256]{1,0:T(8,128)(2,1)}), bf16[512,256]{1,0:T(8,128)(2,1)}) %reduce-scatter.5.cloned.1.call-update) | async-done | bytes 262160 | tf_op jit(solution)/shard_map/reduce_scatter | solution.py:126
  415.6 1.9 convolution_bitcast_fusion
  417.5 0.0 all-reduce.2.cloned.1.call-update
  417.5 0.0 copy-done.6
  417.6 1.9 convolution_convert_fusion
  419.5 147.6 %all-reduce.2.cloned.1.call-done = f32[256,256]{0,1:T(8,128)} async-done(((f32[256,256]{0,1:T(8,128)}), f32[256,256]{0,1:T(8,128)}) %all-reduce.2.cloned.1.call-update) | async-done | bytes 262160 | tf_op jit(solution)/shard_map/psum | solution.py:136
  567.0 1.8 copy.10
Async XLA Ops:
  7.2 1.0 copy-start
  7.2 42.6 %all-gather.3.cloned.1.call-start = ((), (), s32[]{:S(2)}) async-start(), calls=%async_computation.2 | async-start | bytes 2359296 | tf_op jit(solution)/shard_map/all_gather | solution.py:112
  10.0 205.0 %reduce-scatter.3.cloned.1.call-start = ((), (), s32[]{:S(2)}) async-start(), calls=%async_computation.3 | async-start | bytes 4456448 | tf_op jit(solution)/shard_map/reduce_scatter | solution.py:116
  49.7 1.6 copy-start.1
  51.3 0.7 copy-start.2
  52.0 0.7 copy-start.4
  123.8 91.2 %copy-start.7 = (bf16[512,256]{1,0:T(8,128)(2,1)S(1)}, bf16[512,256]{1,0:T(8,128)(2,1)}, u32[]{:S(2)}) copy-start(bf16[512,256]{1,0:T(8,128)(2,1)} %param.13) | copy-start | bytes 786436
  123.8 150.6 %copy-start.3 = (s32[512]{0:T(512)S(1)}, s32[512]{0:T(512)}, u32[]{:S(2)}) copy-start(s32[512]{0:T(512)} %fetch_ref.3) | copy-start | bytes 6148
  123.8 150.6 %copy-start.5 = (s32[512]{0:T(512)S(1)}, s32[512]{0:T(512)}, u32[]{:S(2)}) copy-start(s32[512]{0:T(512)} %place_ref.3) | copy-start | bytes 6148
  123.8 150.6 %all-gather.5.cloned.1.call-start = ((), (), s32[]{:S(2)}) async-start(), calls=%async_computation.4 | async-start | bytes 4456448 | tf_op jit(solution)/shard_map/all_gather | solution.py:121
  217.0 198.6 %reduce-scatter.5.cloned.1.call-start = ((), (), s32[]{:S(2)}) async-start(), calls=%async_computation.5 | async-start | bytes 2359296 | tf_op jit(solution)/shard_map/reduce_scatter | solution.py:126
  274.4 143.2 %copy-start.6 = (bf16[256,256]{1,0:T(8,128)(2,1)S(1)}, bf16[256,256]{1,0:T(8,128)(2,1)}, u32[]{:S(2)}) copy-start(bf16[256,256]{1,0:T(8,128)(2,1)} %param.8) | copy-start | bytes 393220
  366.5 200.5 %all-reduce.2.cloned.1.call-start = ((), (), s32[]{:S(2)}) async-start(), calls=%async_computation.6 | async-start | bytes 524288 | tf_op jit(solution)/shard_map/psum | solution.py:136
Sparse Core Ops, SparseCore 0:
  10.2 39.4 all-gather.2
  123.9 91.0 reduce-scatter.2
  218.3 55.9 all-gather.4
  366.6 48.9 reduce-scatter.4
  421.5 145.4 all-reduce.1

commit v2 on v1

--- a/solution.py
+++ b/solution.py
@@ -10,6 +10,7 @@
 
 GROUP = 32
 CHUNK = 256
+UNROLL = 4
 
 
 def silu_slope(values):
@@ -35,22 +36,34 @@
     base = step * group
     live = jnp.clip(count_ref[0] - base, 0, group)
 
-    def body(j, carry):
-        slot = base + j
+    def product(slot, j):
         src_rows = pl.ds(pl.multiple_of(fetch_ref[slot] * tile, tile), tile)
-        dst_rows = pl.ds(pl.multiple_of(place_ref[slot] * tile, tile), tile)
         block = tiles_ref[j]
         src = src_ref[src_rows, :]
         if forward:
-            prod = jnp.dot(block, src, preferred_element_type=jnp.float32)
-        else:
-            prod = lax.dot_general(
-                block, src, (((0,), (0,)), ((), ())), preferred_element_type=jnp.float32
-            )
+            return jnp.dot(block, src, preferred_element_type=jnp.float32)
+        return lax.dot_general(
+            block, src, (((0,), (0,)), ((), ())), preferred_element_type=jnp.float32
+        )
+
+    def add(slot, prod):
+        dst_rows = pl.ds(pl.multiple_of(place_ref[slot] * tile, tile), tile)
         acc_ref[dst_rows, :] += prod
+
+    def many(k, carry):
+        j0 = k * UNROLL
+        prods = [product(base + j0 + u, j0 + u) for u in range(UNROLL)]
+        for u in range(UNROLL):
+            add(base + j0 + u, prods[u])
         return carry
 
-    lax.fori_loop(0, live, body, 0)
+    def one(j, carry):
+        add(base + j, product(base + j, j))
+        return carry
+
+    full = live // UNROLL
+    lax.fori_loop(0, full, many, 0)
+    lax.fori_loop(full * UNROLL, live, one, 0)
 
     @pl.when(step == pl.num_programs(0) - 1)
     def _():

time: 576 us -> 462 us (0.80)
  Pallas kernels: 163 us -> 64.4 us
  waiting for transfers between devices: 384 us -> 370 us
    pallas_call x2, Pallas kernels: 163 us -> 64.4 us  [tile_products(): pl.pallas_call(functools.partial(tile_kernel, forward=forward), grid_spec...]
    reduce_scatter x1, waiting for transfers between devices: 49.1 us -> 39.7 us  [body(): lax.psum_scatter(column_part, 'row', scatter_dimension=0, tiled=True)]
where the time goes in v2:
time: 462 us
  waiting for transfers between devices  370 us (80%)
  Pallas kernels  64.4 us (14%)
  between operations  14.4 us (3%)
  matrix products  5.67 us (1%)
  local copies, waits for them, and re-layouts  5.65 us (1%)
    psum x1, waiting for transfers between devices, body(): grad_weight = lax.psum(weight_term, ('row', 'col'))  147 us
    reduce_scatter x1, waiting for transfers between devices, body(): lax.psum_scatter(forward_part, 'col', scatter_dimension=0, tiled=True)  86.2 us
    pallas_call x2, Pallas kernels, tile_products(): pl.pallas_call(functools.partial(tile_kernel, forward=forward), grid_spec...  64.4 us
    all_gather x1, waiting for transfers between devices, body(): slope_full = lax.all_gather(slope, 'col', axis=0, tiled=True)  57.3 us
    reduce_scatter x1, waiting for transfers between devices, body(): lax.psum_scatter(column_part, 'row', scatter_dimension=0, tiled=True)  39.7 us
    all_gather x1, waiting for transfers between devices, body(): panel_rows = lax.all_gather(projected, 'row', axis=0, tiled=True)  39.1 us
  transfers between devices with their start and end apart: 5, of which 5 were waited for; matrix products, arithmetic and copies ran while one was open for 0% of the time, Pallas kernels for 0%

profile of v2, /device:TPU:1, one launch (start us, length us, event | category | flops | bytes accessed | tf_op | source)
XLA Modules:
  0.0 462.0 jit_solution(11713521572465103885)
XLA Ops:
  7.2 0.0 copy-start
  7.2 0.0 all-gather.3.cloned.1.call-start
  7.2 0.9 copy-done
  8.1 1.8 convolution_convert_fusion.1
  10.0 0.0 all-gather.3.cloned.1.call-update
  10.0 0.0 reduce-scatter.3.cloned.1.call-start
  10.7 39.1 %all-gather.3.cloned.1.call-done.src_ref = bf16[4096,256]{1,0:T(8,128)(2,1)} async-done(((bf16[512,256]{1,0:T(8,128)(2,1)}), bf16[4096,256]{1,0:T(8,128)(2,1)}) %all-gather.3.cloned.1.call-update) | async-done | bytes 2097168 | tf_op jit(solution)/shard_map/all_gather | solution.py:125
  49.7 0.0 copy-start.1
  49.7 1.6 copy-done.1
  51.3 0.0 copy-start.2
  51.3 0.7 copy-done.2
  52.0 0.0 copy-start.4
  52.0 0.7 copy-done.4
  52.7 30.2 %shard_map.94 = bf16[8192,256]{1,0:T(8,128)(2,1)} custom-call(s32[1]{0:T(128)} %bitcast.9.count_ref, s32[512]{0:T(512)S(1)} %copy-done.2, s32[512]{0:T(512)S(1)} %copy-done.4, bf16[512,128,128]{2,1,0:T(8,128)(2,1)} %tiles_ref.3, bf16[4096,256]{1,0:T(8,128)(2,1)S(1)} %copy-done.1), custom_call_target="tpu_custom_call" | custom-call | flops 4294967296 | bytes 23068672 | tf_op jit(solution)/shard_map/pallas_call | solution.py:101
  82.9 0.0 copy-start.7
  82.9 0.0 copy-start.3
  82.9 0.0 copy-start.5
  82.9 0.0 reduce-scatter.3.cloned.1.call-update
  82.9 0.0 all-gather.5.cloned.1.call-start
  83.0 86.2 %reduce-scatter.3.cloned.1.call-done = bf16[512,256]{1,0:T(8,128)(2,1)} async-done(((bf16[8192,256]{1,0:T(8,128)(2,1)}), bf16[512,256]{1,0:T(8,128)(2,1)}) %reduce-scatter.3.cloned.1.call-update) | async-done | bytes 262160 | tf_op jit(solution)/shard_map/reduce_scatter | solution.py:129
  169.2 0.0 copy-done.7
  169.2 2.0 fusion.7
  171.2 0.0 all-gather.5.cloned.1.call-update
  171.2 0.0 reduce-scatter.5.cloned.1.call-start
  171.2 57.3 %all-gather.5.cloned.1.call-done.src_ref = bf16[8192,256]{1,0:T(8,128)(2,1)} async-done(((bf16[512,256]{1,0:T(8,128)(2,1)}), bf16[8192,256]{1,0:T(8,128)(2,1)}) %all-gather.5.cloned.1.call-update) | async-done | bytes 4194320 | tf_op jit(solution)/shard_map/all_gather | solution.py:134
  228.6 0.0 copy-done.3
  228.6 0.0 copy-done.5
  228.6 0.0 copy-start.6
  228.6 34.2 %shard_map.95 = bf16[4096,256]{1,0:T(8,128)(2,1)} custom-call(s32[1]{0:T(128)} %bitcast.10.count_ref, s32[512]{0:T(512)S(1)} %copy-done.5, s32[512]{0:T(512)S(1)} %copy-done.3, bf16[512,128,128]{2,1,0:T(8,128)(2,1)} %tiles_ref.3, bf16[8192,256]{1,0:T(8,128)(2,1)} %all-gather.5.cloned.1.call-done.src_ref), custom_call_target="tpu_custom_call" | custom-call | flops 4294967296 | bytes 23068672 | tf_op jit(solution)/shard_map/pallas_call | solution.py:101
  262.8 0.0 reduce-scatter.5.cloned.1.call-update
  262.8 0.0 all-reduce.2.cloned.1.call-start
  262.8 39.7 %reduce-scatter.5.cloned.1.call-done = bf16[512,256]{1,0:T(8,128)(2,1)} async-done(((bf16[4096,256]{1,0:T(8,128)(2,1)}), bf16[512,256]{1,0:T(8,128)(2,1)}) %reduce-scatter.5.cloned.1.call-update) | async-done | bytes 262160 | tf_op jit(solution)/shard_map/reduce_scatter | solution.py:139
  302.5 1.9 convolution_bitcast_fusion
  304.4 0.0 all-reduce.2.cloned.1.call-update
  304.4 0.0 copy-done.6
  304.4 1.9 convolution_convert_fusion
  306.4 147.3 %all-reduce.2.cloned.1.call-done = f32[256,256]{0,1:T(8,128)} async-done(((f32[256,256]{0,1:T(8,128)}), f32[256,256]{0,1:T(8,128)}) %all-reduce.2.cloned.1.call-update) | async-done | bytes 262160 | tf_op jit(solution)/shard_map/psum | solution.py:149
  453.7 1.8 copy.10
Async XLA Ops:
  7.2 1.0 copy-start
  7.2 42.6 %all-gather.3.cloned.1.call-start = ((), (), s32[]{:S(2)}) async-start(), calls=%async_computation.2 | async-start | bytes 2359296 | tf_op jit(solution)/shard_map/all_gather | solution.py:125
  10.0 159.2 %reduce-scatter.3.cloned.1.call-start = ((), (), s32[]{:S(2)}) async-start(), calls=%async_computation.3 | async-start | bytes 4456448 | tf_op jit(solution)/shard_map/reduce_scatter | solution.py:129
  49.7 1.6 copy-start.1
  51.3 0.7 copy-start.2
  52.0 0.7 copy-start.4
  82.9 86.3 %copy-start.7 = (bf16[512,256]{1,0:T(8,128)(2,1)S(1)}, bf16[512,256]{1,0:T(8,128)(2,1)}, u32[]{:S(2)}) copy-start(bf16[512,256]{1,0:T(8,128)(2,1)} %param.13) | copy-start | bytes 786436
  82.9 145.7 %copy-start.3 = (s32[512]{0:T(512)S(1)}, s32[512]{0:T(512)}, u32[]{:S(2)}) copy-start(s32[512]{0:T(512)} %fetch_ref.3) | copy-start | bytes 6148
  82.9 145.7 %copy-start.5 = (s32[512]{0:T(512)S(1)}, s32[512]{0:T(512)}, u32[]{:S(2)}) copy-start(s32[512]{0:T(512)} %place_ref.3) | copy-start | bytes 6148
  82.9 145.6 %all-gather.5.cloned.1.call-start = ((), (), s32[]{:S(2)}) async-start(), calls=%async_computation.4 | async-start | bytes 4456448 | tf_op jit(solution)/shard_map/all_gather | solution.py:134
  171.2 131.3 %reduce-scatter.5.cloned.1.call-start = ((), (), s32[]{:S(2)}) async-start(), calls=%async_computation.5 | async-start | bytes 2359296 | tf_op jit(solution)/shard_map/reduce_scatter | solution.py:139
  228.6 75.9 %copy-start.6 = (bf16[256,256]{1,0:T(8,128)(2,1)S(1)}, bf16[256,256]{1,0:T(8,128)(2,1)}, u32[]{:S(2)}) copy-start(bf16[256,256]{1,0:T(8,128)(2,1)} %param.8) | copy-start | bytes 393220
  262.8 190.9 %all-reduce.2.cloned.1.call-start = ((), (), s32[]{:S(2)}) async-start(), calls=%async_computation.6 | async-start | bytes 524288 | tf_op jit(solution)/shard_map/psum | solution.py:149
Sparse Core Ops, SparseCore 0:
  10.2 39.4 all-gather.2
  83.1 86.0 reduce-scatter.2
  172.5 56.0 all-gather.4
  262.9 39.5 reduce-scatter.4
  308.4 145.2 all-reduce.1

commit v3 on v2

--- a/solution.py
+++ b/solution.py
@@ -113,6 +113,16 @@
     )(count, place_index, fetch_index, tile_values, source)
 
 
+def gather_rows(values, axes, parts):
+    copies = jnp.broadcast_to(values[None], (parts,) + values.shape)
+    return lax.all_to_all(copies, axes, 0, 0, tiled=True).reshape(-1, values.shape[-1])
+
+
+def scatter_sum(values, axes, parts):
+    pieces = lax.all_to_all(values.reshape(parts, -1, values.shape[-1]), axes, 0, 0, tiled=False)
+    return pieces.astype(jnp.float32).sum(0)
+
+
 def body(features, weight, tile_values, tile_row, tile_col, tile_count, cotangent):
     row_count = lax.axis_size("row")
     col_count = lax.axis_size("col")
@@ -122,31 +132,27 @@
     col_tiles = node_dev * row_count // tile_size
     count = tile_count.reshape(1)
     projected = jnp.dot(features, weight, preferred_element_type=jnp.float32).astype(jnp.bfloat16)
-    panel_rows = lax.all_gather(projected, "row", axis=0, tiled=True)
+    panel_rows = gather_rows(projected, "row", row_count)
     forward_part = tile_products(
         tile_values, tile_col, tile_row, count, panel_rows, row_tiles, True
     )
-    summed = lax.psum_scatter(forward_part, "col", scatter_dimension=0, tiled=True).astype(
-        jnp.float32
-    )
+    summed = scatter_sum(forward_part, "col", col_count)
     activated = jax.nn.silu(summed).astype(jnp.bfloat16)
     slope = (cotangent.astype(jnp.float32) * silu_slope(summed)).astype(jnp.bfloat16)
-    slope_full = lax.all_gather(slope, "col", axis=0, tiled=True)
+    slope_full = gather_rows(slope, "col", col_count)
     column_part = tile_products(
         tile_values, tile_row, tile_col, count, slope_full, col_tiles, False
     )
-    grad_nodes = (
-        lax.psum_scatter(column_part, "row", scatter_dimension=0, tiled=True)
-        .astype(jnp.float32)
-        .astype(jnp.bfloat16)
-    )
+    grad_nodes = scatter_sum(column_part, "row", row_count).astype(jnp.bfloat16)
     grad_features = lax.dot_general(
         grad_nodes, weight, (((1,), (1,)), ((), ())), preferred_element_type=jnp.float32
     ).astype(jnp.bfloat16)
     weight_term = lax.dot_general(
         features, grad_nodes, (((0,), (0,)), ((), ())), preferred_element_type=jnp.float32
     )
-    grad_weight = lax.psum(weight_term, ("row", "col"))
+    devices = row_count * col_count
+    weight_piece = scatter_sum(weight_term, ("row", "col"), devices)
+    grad_weight = gather_rows(weight_piece, ("row", "col"), devices)
     return (activated, grad_features, grad_weight)
 
 

time: 462 us -> 285 us (0.62)
  waiting for transfers between devices: 370 us -> 35.7 us
  blocking collectives: 0 us -> 180 us
  Pallas kernels: 64.4 us -> 48.4 us
  between operations: 14.4 us -> 1.38 us
  starting transfers between devices: 0.21 us -> 10.2 us
    all_to_all x0 -> x4, blocking collectives: none -> 180 us  [the longest x3 125 us: scatter_sum(): lax.all_to_all(values.reshape(parts, -1, values.shape[-1]), axes, 0, 0, t...]
    psum x1 -> x0, waiting for transfers between devices: 147 us -> none  [body(): grad_weight = lax.psum(weight_term, ('row', 'col'))]
    reduce_scatter x2 -> x0, waiting for transfers between devices: 126 us -> none  [the longest x1 86.2 us: body(): lax.psum_scatter(forward_part, 'col', scatter_dimension=0, tiled=True)]
    all_gather x2 -> x0, waiting for transfers between devices: 96.4 us -> none  [the longest x1 57.3 us: body(): slope_full = lax.all_gather(slope, 'col', axis=0, tiled=True)]
    all_to_all x0 -> x2, waiting for transfers between devices: none -> 35.7 us  [gather_rows(): lax.all_to_all(copies, axes, 0, 0, tiled=True).reshape(-1, values.shape[-1])]
    pallas_call x2, Pallas kernels: 64.4 us -> 48.4 us  [tile_products(): pl.pallas_call(functools.partial(tile_kernel, forward=forward), grid_spec...]
    all_to_all x0 -> x2, starting transfers between devices: none -> 10.2 us  [gather_rows(): lax.all_to_all(copies, axes, 0, 0, tiled=True).reshape(-1, values.shape[-1])]
  transfers between devices with their start and end apart: 5 -> 2, of which waited for: 5 -> 2; matrix products, arithmetic and copies ran while one was open for 0% -> 0% of each run, Pallas kernels for 0% -> 0%
where the time goes in v3:
time: 285 us
  blocking collectives  180 us (63%)
  Pallas kernels  48.4 us (17%)
  waiting for transfers between devices  35.7 us (13%)
  starting transfers between devices  10.2 us (4%)
  local copies, waits for them, and re-layouts  4.99 us (2%)
    all_to_all x3, blocking collectives, scatter_sum(): lax.all_to_all(values.reshape(parts, -1, values.shape[-1]), axes, 0, 0, t...  125 us
    all_to_all x1, blocking collectives, gather_rows(): lax.all_to_all(copies, axes, 0, 0, tiled=True).reshape(-1, values.shape[-1])  55 us
    pallas_call x2, Pallas kernels, tile_products(): pl.pallas_call(functools.partial(tile_kernel, forward=forward), grid_spec...  48.4 us
    all_to_all x2, waiting for transfers between devices, gather_rows(): lax.all_to_all(copies, axes, 0, 0, tiled=True).reshape(-1, values.shape[-1])  35.7 us
    all_to_all x2, starting transfers between devices, gather_rows(): lax.all_to_all(copies, axes, 0, 0, tiled=True).reshape(-1, values.shape[-1])  10.2 us
  transfers between devices with their start and end apart: 2, of which 2 were waited for; matrix products, arithmetic and copies ran while one was open for 0% of the time, Pallas kernels for 0%

profile of v3, /device:TPU:1, one launch (start us, length us, event | category | flops | bytes accessed | tf_op | source)
XLA Modules:
  0.0 285.0 jit_solution(1094438244745250597)
XLA Ops:
  0.6 0.0 copy-start
  0.6 0.0 copy-start.2
  0.7 0.0 copy-start.1
  0.7 0.9 copy-done
  1.6 1.1 convolution_convert_fusion.1
  2.7 1.5 broadcast_in_dim.6
  4.2 5.9 %all-to-all-start = ((bf16[8,512,256]{2,1,0:T(8,128)(2,1)}), bf16[8,512,256]{2,1,0:T(8,128)(2,1)S(1)}, u32[]{:S(2)}, u32[]{:S(2)}) async-start(bf16[8,512,256]{2,1,0:T(8,128)(2,1)} %broadcast_in_dim.6), calls=%async_computation | async-start | bytes 4194304 | tf_op jit(solution)/shard_map/all_to_all | solution.py:118
  10.8 25.5 %all-to-all-done = bf16[8,512,256]{2,1,0:T(8,128)(2,1)S(1)} async-done(((bf16[8,512,256]{2,1,0:T(8,128)(2,1)}), bf16[8,512,256]{2,1,0:T(8,128)(2,1)S(1)}, u32[]{:S(2)}, u32[]{:S(2)}) %all-to-all-start) | async-done | bytes 2097184 | tf_op jit(solution)/shard_map/all_to_all | solution.py:118
  36.3 0.0 copy-done.2
  36.3 0.0 copy-done.1
  36.3 23.4 %shard_map.94 = bf16[8192,256]{1,0:T(8,128)(2,1)} custom-call(s32[1]{0:T(128)} %bitcast.13.count_ref, s32[512]{0:T(512)S(1)} %copy-done.1, s32[512]{0:T(512)S(1)} %copy-done.2, bf16[512,128,128]{2,1,0:T(8,128)(2,1)} %tiles_ref.3, bf16[4096,256]{1,0:T(8,128)(2,1)S(1)} %bitcast.15), custom_call_target="tpu_custom_call" | custom-call | flops 4294967296 | bytes 23068672 | tf_op jit(solution)/shard_map/pallas_call | solution.py:101
  59.7 65.2 %all_to_all.30 = bf16[16,512,256]{2,1,0:T(8,128)(2,1)S(1)} all-to-all(bf16[16,512,256]{2,1,0:T(8,128)(2,1)} %bitcast.18), channel_id=1, replica_groups=mesh['row'=8,'col'=16] {'col'}, dimensions={0} | all-to-all | bytes 8388608 | tf_op jit(solution)/shard_map/all_to_all | solution.py:122
  124.9 0.0 copy-start.4
  124.9 0.6 convert_reduce_fusion
  125.5 0.4 copy-done.4
  125.9 0.9 multiply_convert_fusion
  126.8 0.4 broadcast_in_dim.7
  127.2 55.0 %all_to_all.31 = bf16[16,512,256]{2,1,0:T(8,128)(2,1)} all-to-all(bf16[16,512,256]{2,1,0:T(8,128)(2,1)S(1)} %broadcast_in_dim.7), channel_id=1, replica_groups=mesh['row'=8,'col'=16] {'col'}, dimensions={0} | all-to-all | bytes 8388608 | tf_op jit(solution)/shard_map/all_to_all | solution.py:118
  182.3 25.0 %shard_map.95 = bf16[4096,256]{1,0:T(8,128)(2,1)S(1)} custom-call(s32[1]{0:T(128)} %bitcast.14.count_ref, s32[512]{0:T(512)S(1)} %copy-done.2, s32[512]{0:T(512)S(1)} %copy-done.1, bf16[512,128,128]{2,1,0:T(8,128)(2,1)} %tiles_ref.3, bf16[8192,256]{1,0:T(8,128)(2,1)} %bitcast.17), custom_call_target="tpu_custom_call" | custom-call | flops 4294967296 | bytes 23068672 | tf_op jit(solution)/shard_map/pallas_call | solution.py:101
  207.2 0.0 copy-start.3
  207.2 41.8 %all_to_all.32 = bf16[8,512,256]{2,1,0:T(8,128)(2,1)S(1)} all-to-all(bf16[8,512,256]{2,1,0:T(8,128)(2,1)S(1)} %bitcast.16), channel_id=1, replica_groups=mesh['row'=8,'col'=16] {'row'}, dimensions={0} | all-to-all | bytes 4194304 | tf_op jit(solution)/shard_map/all_to_all | solution.py:122
  249.0 0.4 reduce_sum.31
  249.4 0.3 convolution_bitcast_fusion
  249.7 0.1 reshape.35
  249.8 17.9 %all_to_all.33 = f32[128,2,256]{2,1,0:T(2,128)S(1)} all-to-all(f32[128,2,256]{2,1,0:T(2,128)S(1)} %reshape.35), channel_id=1, replica_groups=mesh['row'=8,'col'=16] {'row','col'}, dimensions={0} | all-to-all | bytes 524288 | tf_op jit(solution)/shard_map/all_to_all | solution.py:122
  267.7 0.1 reduce_sum.32
  267.9 0.8 broadcast_in_dim.8
  268.6 4.2 %all-to-all-start.5 = ((f32[128,2,256]{2,1,0:T(2,128)}), f32[128,2,256]{2,1,0:T(2,128)S(1)}, u32[]{:S(2)}, u32[]{:S(2)}) async-start(f32[128,2,256]{2,1,0:T(2,128)} %broadcast_in_dim.8), calls=%async_computation.5 | async-start | bytes 524288 | tf_op jit(solution)/shard_map/all_to_all | solution.py:118
  272.9 0.0 copy-done.3
  272.9 1.0 convolution_convert_fusion
  273.9 10.2 %all-to-all-done.5 = f32[128,2,256]{2,1,0:T(2,128)S(1)} async-done(((f32[128,2,256]{2,1,0:T(2,128)}), f32[128,2,256]{2,1,0:T(2,128)S(1)}, u32[]{:S(2)}, u32[]{:S(2)}) %all-to-all-start.5) | async-done | bytes 262176 | tf_op jit(solution)/shard_map/all_to_all | solution.py:118
  284.1 0.9 reshape.36
Async XLA Ops:
  0.6 1.0 copy-start
  0.6 35.6 %copy-start.2 = (s32[512]{0:T(512)S(1)}, s32[512]{0:T(512)}, u32[]{:S(2)}) copy-start(s32[512]{0:T(512)} %place_ref.3) | copy-start | bytes 6148
  0.7 35.6 %copy-start.1 = (s32[512]{0:T(512)S(1)}, s32[512]{0:T(512)}, u32[]{:S(2)}) copy-start(s32[512]{0:T(512)} %fetch_ref.3) | copy-start | bytes 6148
  4.2 32.1 %all-to-all-start = ((bf16[8,512,256]{2,1,0:T(8,128)(2,1)}), bf16[8,512,256]{2,1,0:T(8,128)(2,1)S(1)}, u32[]{:S(2)}, u32[]{:S(2)}) async-start(bf16[8,512,256]{2,1,0:T(8,128)(2,1)} %broadcast_in_dim.6), calls=%async_computation | async-start | bytes 4194304 | tf_op jit(solution)/shard_map/all_to_all | solution.py:118
  124.9 1.0 copy-start.4
  207.2 65.7 %copy-start.3 = (bf16[256,256]{1,0:T(8,128)(2,1)S(1)}, bf16[256,256]{1,0:T(8,128)(2,1)}, u32[]{:S(2)}) copy-start(bf16[256,256]{1,0:T(8,128)(2,1)} %param.8) | copy-start | bytes 393220
  268.6 15.5 %all-to-all-start.5 = ((f32[128,2,256]{2,1,0:T(2,128)}), f32[128,2,256]{2,1,0:T(2,128)S(1)}, u32[]{:S(2)}, u32[]{:S(2)}) async-start(f32[128,2,256]{2,1,0:T(2,128)} %broadcast_in_dim.8), calls=%async_computation.5 | async-start | bytes 524288 | tf_op jit(solution)/shard_map/all_to_all | solution.py:118

commit v4 on v3

--- a/solution.py
+++ b/solution.py
@@ -11,6 +11,7 @@
 GROUP = 32
 CHUNK = 256
 UNROLL = 4
+SPLIT = 2
 
 
 def silu_slope(values):
@@ -75,9 +76,9 @@
         lax.fori_loop(0, out_rows // CHUNK, emit, 0)
 
 
-def tile_products(tile_values, fetch_index, place_index, count, source, out_tiles, forward):
+def tile_products(tile_values, fetch_index, place_index, count, source, out_tiles, forward, part=0, hidden=None):
     slots, tile, _ = tile_values.shape
-    hidden = source.shape[-1]
+    hidden = source.shape[-1] if hidden is None else hidden
     src_rows = source.shape[0]
     out_rows = out_tiles * tile
     group = GROUP
@@ -92,7 +93,7 @@
         grid=(steps,),
         in_specs=[
             pl.BlockSpec((group, tile, tile), tiles_map),
-            pl.BlockSpec((src_rows, hidden), lambda i, *_: (0, 0)),
+            pl.BlockSpec((src_rows, hidden), lambda i, *_: (0, part)),
         ],
         out_specs=pl.BlockSpec((out_rows, hidden), lambda i, *_: (0, 0)),
         scratch_shapes=[pltpu.VMEM((out_rows, hidden), jnp.float32)],
@@ -127,23 +128,31 @@
     row_count = lax.axis_size("row")
     col_count = lax.axis_size("col")
     node_dev = features.shape[0]
+    hidden = features.shape[1]
     tile_size = tile_values.shape[1]
     row_tiles = node_dev * col_count // tile_size
     col_tiles = node_dev * row_count // tile_size
     count = tile_count.reshape(1)
+    width = hidden // SPLIT
     projected = jnp.dot(features, weight, preferred_element_type=jnp.float32).astype(jnp.bfloat16)
     panel_rows = gather_rows(projected, "row", row_count)
-    forward_part = tile_products(
-        tile_values, tile_col, tile_row, count, panel_rows, row_tiles, True
-    )
-    summed = scatter_sum(forward_part, "col", col_count)
-    activated = jax.nn.silu(summed).astype(jnp.bfloat16)
-    slope = (cotangent.astype(jnp.float32) * silu_slope(summed)).astype(jnp.bfloat16)
-    slope_full = gather_rows(slope, "col", col_count)
-    column_part = tile_products(
-        tile_values, tile_row, tile_col, count, slope_full, col_tiles, False
-    )
-    grad_nodes = scatter_sum(column_part, "row", row_count).astype(jnp.bfloat16)
+    activated_parts = []
+    grad_parts = []
+    for part in range(SPLIT):
+        forward_part = tile_products(
+            tile_values, tile_col, tile_row, count, panel_rows, row_tiles, True, part, width
+        )
+        summed = scatter_sum(forward_part, "col", col_count)
+        activated_parts.append(jax.nn.silu(summed).astype(jnp.bfloat16))
+        cot = cotangent[:, part * width:(part + 1) * width].astype(jnp.float32)
+        slope = (cot * silu_slope(summed)).astype(jnp.bfloat16)
+        slope_full = gather_rows(slope, "col", col_count)
+        column_part = tile_products(
+            tile_values, tile_row, tile_col, count, slope_full, col_tiles, False
+        )
+        grad_parts.append(scatter_sum(column_part, "row", row_count))
+    activated = jnp.concatenate(activated_parts, axis=1)
+    grad_nodes = jnp.concatenate(grad_parts, axis=1).astype(jnp.bfloat16)
     grad_features = lax.dot_general(
         grad_nodes, weight, (((1,), (1,)), ((), ())), preferred_element_type=jnp.float32
     ).astype(jnp.bfloat16)

time: 285 us -> 302 us (1.060)
  blocking collectives: 180 us -> 64.2 us
  waiting for transfers between devices: 35.7 us -> 83.6 us
  Pallas kernels: 48.4 us -> 86.4 us
  starting transfers between devices: 10.2 us -> 47.8 us
  local copies, waits for them, and re-layouts: 4.99 us -> 10.6 us
    all_to_all x3 -> x1, blocking collectives: 125 us -> 31.9 us  [scatter_sum(): lax.all_to_all(values.reshape(parts, -1, values.shape[-1]), axes, 0, 0, t...]
    all_to_all x0 -> x4, waiting for transfers between devices: none -> 45 us  [scatter_sum(): lax.all_to_all(values.reshape(parts, -1, values.shape[-1]), axes, 0, 0, t...]
    pallas_call x2 -> x4, Pallas kernels: 48.4 us -> 86.4 us  [tile_products(): pl.pallas_call(functools.partial(tile_kernel, forward=forward), grid_spec...]
    all_to_all x0 -> x4, starting transfers between devices: none -> 32.8 us  [scatter_sum(): lax.all_to_all(values.reshape(parts, -1, values.shape[-1]), axes, 0, 0, t...]
    all_to_all x1, blocking collectives: 55 us -> 32.3 us  [gather_rows(): lax.all_to_all(copies, axes, 0, 0, tiled=True).reshape(-1, values.shape[-1])]
    all_to_all x2 -> x3, starting transfers between devices: 10.2 us -> 15 us  [gather_rows(): lax.all_to_all(copies, axes, 0, 0, tiled=True).reshape(-1, values.shape[-1])]
    unnamed x10 -> x18, local copies, waits for them, and re-layouts: 1.31 us -> 5.18 us
    all_to_all x2 -> x3, waiting for transfers between devices: 35.7 us -> 38.6 us  [gather_rows(): lax.all_to_all(copies, axes, 0, 0, tiled=True).reshape(-1, values.shape[-1])]
  transfers between devices with their start and end apart: 2 -> 7, of which waited for: 2 -> 6; matrix products, arithmetic and copies ran while one was open for 0% -> 1% of each run, Pallas kernels for 0% -> 22%
where the time goes in v4:
time: 302 us; the launch traced here: 301 us
  Pallas kernels  86.4 us (29%)
  waiting for transfers between devices  83.6 us (28%)
  blocking collectives  64.2 us (21%)
  starting transfers between devices  47.8 us (16%)
  local copies, waits for them, and re-layouts  10.6 us (4%)
  other arithmetic  4.32 us (1%)
    pallas_call x4, Pallas kernels, tile_products(): pl.pallas_call(functools.partial(tile_kernel, forward=forward), grid_spec...  86.4 us
    all_to_all x4, waiting for transfers between devices, scatter_sum(): lax.all_to_all(values.reshape(parts, -1, values.shape[-1]), axes, 0, 0, t...  45 us
    all_to_all x3, waiting for transfers between devices, gather_rows(): lax.all_to_all(copies, axes, 0, 0, tiled=True).reshape(-1, values.shape[-1])  38.6 us
    all_to_all x4, starting transfers between devices, scatter_sum(): lax.all_to_all(values.reshape(parts, -1, values.shape[-1]), axes, 0, 0, t...  32.8 us
    all_to_all x1, blocking collectives, gather_rows(): lax.all_to_all(copies, axes, 0, 0, tiled=True).reshape(-1, values.shape[-1])  32.3 us
    all_to_all x1, blocking collectives, scatter_sum(): lax.all_to_all(values.reshape(parts, -1, values.shape[-1]), axes, 0, 0, t...  31.9 us
    all_to_all x3, starting transfers between devices, gather_rows(): lax.all_to_all(copies, axes, 0, 0, tiled=True).reshape(-1, values.shape[-1])  15 us
  transfers between devices with their start and end apart: 7, of which 6 were waited for; matrix products, arithmetic and copies ran while one was open for 1% of the time, Pallas kernels for 22%

profile of v4, /device:TPU:1, one launch (start us, length us, event | category | flops | bytes accessed | tf_op | source)
XLA Modules:
  0.0 300.7 jit_solution(11311115242234383560)
XLA Ops:
  0.6 0.0 copy-start
  0.6 0.9 copy-done
  1.6 1.1 convolution_convert_fusion.1
  2.7 1.5 broadcast_in_dim.8
  4.2 6.1 %all-to-all-start = ((bf16[8,512,256]{2,1,0:T(8,128)(2,1)}), bf16[8,512,256]{2,1,0:T(8,128)(2,1)S(1)}, u32[]{:S(2)}, u32[]{:S(2)}) async-start(bf16[8,512,256]{2,1,0:T(8,128)(2,1)} %broadcast_in_dim.8), calls=%async_computation | async-start | bytes 4194304 | tf_op jit(solution)/shard_map/all_to_all | solution.py:119
  10.9 25.5 %all-to-all-done = bf16[8,512,256]{2,1,0:T(8,128)(2,1)S(1)} async-done(((bf16[8,512,256]{2,1,0:T(8,128)(2,1)}), bf16[8,512,256]{2,1,0:T(8,128)(2,1)S(1)}, u32[]{:S(2)}, u32[]{:S(2)}) %all-to-all-start) | async-done | bytes 2097184 | tf_op jit(solution)/shard_map/all_to_all | solution.py:119
  36.4 0.0 copy-done.4
  36.4 0.0 copy-done.5
  36.4 19.8 %shard_map.95 = bf16[8192,128]{1,0:T(8,128)(2,1)S(1)} custom-call(s32[1]{0:T(128)} %bitcast.15.count_ref, s32[512]{0:T(512)S(1)} %copy-done.4, s32[512]{0:T(512)S(1)} %copy-done.5, bf16[512,128,128]{2,1,0:T(8,128)(2,1)} %tiles_ref.7, bf16[4096,256]{1,0:T(8,128)(2,1)S(1)} %bitcast.18), custom_call_target="tpu_custom_call" | custom-call | flops 2147483648 | bytes 19922944 | tf_op jit(solution)/shard_map/pallas_call | solution.py:102
  56.3 0.0 copy-start.3
  56.3 1.3 copy-done.3
  57.6 15.1 %all-to-all-start.2 = ((bf16[16,512,128]{2,1,0:T(8,128)(2,1)}), bf16[16,512,128]{2,1,0:T(8,128)(2,1)}, u32[]{:S(2)}, u32[]{:S(2)}) async-start(bf16[16,512,128]{2,1,0:T(8,128)(2,1)} %bitcast.23), calls=%async_computation.2 | async-start | bytes 4194304 | tf_op jit(solution)/shard_map/all_to_all | solution.py:123
  72.7 19.8 %shard_map.94 = bf16[8192,128]{1,0:T(8,128)(2,1)S(1)} custom-call(s32[1]{0:T(128)} %bitcast.14.count_ref, s32[512]{0:T(512)S(1)} %copy-done.4, s32[512]{0:T(512)S(1)} %copy-done.5, bf16[512,128,128]{2,1,0:T(8,128)(2,1)} %tiles_ref.7, bf16[4096,256]{1,0:T(8,128)(2,1)S(1)} %bitcast.19), custom_call_target="tpu_custom_call" | custom-call | flops 2147483648 | bytes 19922944 | tf_op jit(solution)/shard_map/pallas_call | solution.py:102
  92.5 0.0 copy-start.1
  92.5 1.3 copy-done.1
  93.9 7.4 %all-to-all-done.2 = bf16[16,512,128]{2,1,0:T(8,128)(2,1)} async-done(((bf16[16,512,128]{2,1,0:T(8,128)(2,1)}), bf16[16,512,128]{2,1,0:T(8,128)(2,1)}, u32[]{:S(2)}, u32[]{:S(2)}) %all-to-all-start.2) | async-done | bytes 2097184 | tf_op jit(solution)/shard_map/all_to_all | solution.py:123
  101.3 6.8 %all-to-all-start.1 = ((bf16[16,512,128]{2,1,0:T(8,128)(2,1)}), bf16[16,512,128]{2,1,0:T(8,128)(2,1)S(1)}, u32[]{:S(2)}, u32[]{:S(2)}) async-start(bf16[16,512,128]{2,1,0:T(8,128)(2,1)} %bitcast.21), calls=%async_computation.1 | async-start | bytes 4194304 | tf_op jit(solution)/shard_map/all_to_all | solution.py:123
  108.0 1.9 convert_reduce_fusion
  110.0 26.5 %all-to-all-done.1 = bf16[16,512,128]{2,1,0:T(8,128)(2,1)S(1)} async-done(((bf16[16,512,128]{2,1,0:T(8,128)(2,1)}), bf16[16,512,128]{2,1,0:T(8,128)(2,1)S(1)}, u32[]{:S(2)}, u32[]{:S(2)}) %all-to-all-start.1) | async-done | bytes 2097184 | tf_op jit(solution)/shard_map/all_to_all | solution.py:123
  136.5 0.3 convert_reduce_fusion.1
  136.8 0.9 multiply_convert_fusion.1
  137.7 0.4 broadcast_in_dim.9
  138.1 32.3 %all_to_all.45 = bf16[16,512,128]{2,1,0:T(8,128)(2,1)} all-to-all(bf16[16,512,128]{2,1,0:T(8,128)(2,1)S(1)} %broadcast_in_dim.9), channel_id=1, replica_groups=mesh['row'=8,'col'=16] {'col'}, dimensions={0} | all-to-all | bytes 4194304 | tf_op jit(solution)/shard_map/all_to_all | solution.py:119
  170.4 1.7 broadcast_in_dim.10
  172.2 4.7 %all-to-all-start.5 = ((bf16[16,512,128]{2,1,0:T(8,128)(2,1)}), bf16[16,512,128]{2,1,0:T(8,128)(2,1)S(1)}, u32[]{:S(2)}, u32[]{:S(2)}) async-start(bf16[16,512,128]{2,1,0:T(8,128)(2,1)} %broadcast_in_dim.10), calls=%async_computation.5 | async-start | bytes 4194304 | tf_op jit(solution)/shard_map/all_to_all | solution.py:119
  176.9 1.6 copy-done.2
  178.5 23.4 %shard_map.96 = bf16[4096,128]{1,0:T(8,128)(2,1)} custom-call(s32[1]{0:T(128)} %bitcast.16.count_ref, s32[512]{0:T(512)S(1)} %copy-done.5, s32[512]{0:T(512)S(1)} %copy-done.4, bf16[512,128,128]{2,1,0:T(8,128)(2,1)} %tiles_ref.7, bf16[8192,128]{1,0:T(8,128)(2,1)S(1)} %bitcast.22), custom_call_target="tpu_custom_call" | custom-call | flops 2147483648 | bytes 19922944 | tf_op jit(solution)/shard_map/pallas_call | solution.py:102
  201.8 3.6 %all-to-all-done.5 = bf16[16,512,128]{2,1,0:T(8,128)(2,1)S(1)} async-done(((bf16[16,512,128]{2,1,0:T(8,128)(2,1)}), bf16[16,512,128]{2,1,0:T(8,128)(2,1)S(1)}, u32[]{:S(2)}, u32[]{:S(2)}) %all-to-all-start.5) | async-done | bytes 2097184 | tf_op jit(solution)/shard_map/all_to_all | solution.py:119
  205.4 3.6 %all-to-all-start.4 = ((bf16[8,512,128]{2,1,0:T(8,128)(2,1)}), bf16[8,512,128]{2,1,0:T(8,128)(2,1)S(1)}, u32[]{:S(2)}, u32[]{:S(2)}) async-start(bf16[8,512,128]{2,1,0:T(8,128)(2,1)} %bitcast.5), calls=%async_computation.4 | async-start | bytes 2097152 | tf_op jit(solution)/shard_map/all_to_all | solution.py:123
  209.0 23.4 %shard_map.97 = bf16[4096,128]{1,0:T(8,128)(2,1)} custom-call(s32[1]{0:T(128)} %bitcast.17.count_ref, s32[512]{0:T(512)S(1)} %copy-done.5, s32[512]{0:T(512)S(1)} %copy-done.4, bf16[512,128,128]{2,1,0:T(8,128)(2,1)} %tiles_ref.7, bf16[8192,128]{1,0:T(8,128)(2,1)S(1)} %bitcast.20), custom_call_target="tpu_custom_call" | custom-call | flops 2147483648 | bytes 19922944 | tf_op jit(solution)/shard_map/pallas_call | solution.py:102
  232.4 0.0 all-to-all-done.4
  232.4 7.3 %all-to-all-start.6 = ((bf16[8,512,128]{2,1,0:T(8,128)(2,1)}), bf16[8,512,128]{2,1,0:T(8,128)(2,1)S(1)}, u32[]{:S(2)}, u32[]{:S(2)}) async-start(bf16[8,512,128]{2,1,0:T(8,128)(2,1)} %bitcast.7), calls=%async_computation.6 | async-start | bytes 2097152 | tf_op jit(solution)/shard_map/all_to_all | solution.py:123
  239.7 0.1 reduce
  239.9 0.0 copy-start.6
  239.9 0.0 copy-start.8
  239.9 11.1 %all-to-all-done.6 = bf16[8,512,128]{2,1,0:T(8,128)(2,1)S(1)} async-done(((bf16[8,512,128]{2,1,0:T(8,128)(2,1)}), bf16[8,512,128]{2,1,0:T(8,128)(2,1)S(1)}, u32[]{:S(2)}, u32[]{:S(2)}) %all-to-all-start.6) | async-done | bytes 1048608 | tf_op jit(solution)/shard_map/all_to_all | solution.py:123
  251.0 0.1 reduce.1
  251.1 0.3 convolution_bitcast_fusion
  251.4 0.1 reshape.48
  251.6 31.9 %all_to_all.46 = f32[128,2,256]{2,1,0:T(2,128)S(1)} all-to-all(f32[128,2,256]{2,1,0:T(2,128)S(1)} %reshape.48), channel_id=1, replica_groups=mesh['row'=8,'col'=16] {'row','col'}, dimensions={0} | all-to-all | bytes 524288 | tf_op jit(solution)/shard_map/all_to_all | solution.py:123
  283.5 0.1 reduce_sum.49
  283.6 0.8 broadcast_in_dim.11
  284.4 4.2 %all-to-all-start.8 = ((f32[128,2,256]{2,1,0:T(2,128)}), f32[128,2,256]{2,1,0:T(2,128)S(1)}, u32[]{:S(2)}, u32[]{:S(2)}) async-start(f32[128,2,256]{2,1,0:T(2,128)} %broadcast_in_dim.11), calls=%async_computation.8 | async-start | bytes 524288 | tf_op jit(solution)/shard_map/all_to_all | solution.py:119
  288.6 0.7 pad_maximum_fusion
  289.4 0.0 copy-done.8
  289.4 1.0 convolution_convert_fusion
  290.3 9.5 %all-to-all-done.8 = f32[128,2,256]{2,1,0:T(2,128)S(1)} async-done(((f32[128,2,256]{2,1,0:T(2,128)}), f32[128,2,256]{2,1,0:T(2,128)S(1)}, u32[]{:S(2)}, u32[]{:S(2)}) %all-to-all-start.8) | async-done | bytes 262176 | tf_op jit(solution)/shard_map/all_to_all | solution.py:119
  299.8 0.9 reshape.49
  (6 shorter events, 0.0 us)
Async XLA Ops:
  0.6 1.0 copy-start
  4.2 32.2 %copy-start.4 = (s32[512]{0:T(512)S(1)}, s32[512]{0:T(512)}, u32[]{:S(2)}) copy-start(s32[512]{0:T(512)} %fetch_ref.7) | copy-start | bytes 6148
  4.2 32.2 %copy-start.5 = (s32[512]{0:T(512)S(1)}, s32[512]{0:T(512)}, u32[]{:S(2)}) copy-start(s32[512]{0:T(512)} %place_ref.7) | copy-start | bytes 6148
  4.2 32.2 %all-to-all-start = ((bf16[8,512,256]{2,1,0:T(8,128)(2,1)}), bf16[8,512,256]{2,1,0:T(8,128)(2,1)S(1)}, u32[]{:S(2)}, u32[]{:S(2)}) async-start(bf16[8,512,256]{2,1,0:T(8,128)(2,1)} %broadcast_in_dim.8), calls=%async_computation | async-start | bytes 4194304 | tf_op jit(solution)/shard_map/all_to_all | solution.py:119
  56.3 1.3 copy-start.3
  57.6 43.7 %all-to-all-start.2 = ((bf16[16,512,128]{2,1,0:T(8,128)(2,1)}), bf16[16,512,128]{2,1,0:T(8,128)(2,1)}, u32[]{:S(2)}, u32[]{:S(2)}) async-start(bf16[16,512,128]{2,1,0:T(8,128)(2,1)} %bitcast.23), calls=%async_computation.2 | async-start | bytes 4194304 | tf_op jit(solution)/shard_map/all_to_all | solution.py:123
  92.5 1.3 copy-start.1
  101.3 35.2 %all-to-all-start.1 = ((bf16[16,512,128]{2,1,0:T(8,128)(2,1)}), bf16[16,512,128]{2,1,0:T(8,128)(2,1)S(1)}, u32[]{:S(2)}, u32[]{:S(2)}) async-start(bf16[16,512,128]{2,1,0:T(8,128)(2,1)} %bitcast.21), calls=%async_computation.1 | async-start | bytes 4194304 | tf_op jit(solution)/shard_map/all_to_all | solution.py:123
  108.0 28.8 %copy-start.7 = (bf16[512,256]{1,0:T(8,128)(2,1)S(1)}, bf16[512,256]{1,0:T(8,128)(2,1)}, u32[]{:S(2)}) copy-start(bf16[512,256]{1,0:T(8,128)(2,1)} %param.13) | copy-start | bytes 786436
  172.2 33.2 %all-to-all-start.5 = ((bf16[16,512,128]{2,1,0:T(8,128)(2,1)}), bf16[16,512,128]{2,1,0:T(8,128)(2,1)S(1)}, u32[]{:S(2)}, u32[]{:S(2)}) async-start(bf16[16,512,128]{2,1,0:T(8,128)(2,1)} %broadcast_in_dim.10), calls=%async_computation.5 | async-start | bytes 4194304 | tf_op jit(solution)/shard_map/all_to_all | solution.py:119
  176.9 1.6 copy-start.2
  205.4 26.9 %all-to-all-start.4 = ((bf16[8,512,128]{2,1,0:T(8,128)(2,1)}), bf16[8,512,128]{2,1,0:T(8,128)(2,1)S(1)}, u32[]{:S(2)}, u32[]{:S(2)}) async-start(bf16[8,512,128]{2,1,0:T(8,128)(2,1)} %bitcast.5), calls=%async_computation.4 | async-start | bytes 2097152 | tf_op jit(solution)/shard_map/all_to_all | solution.py:123
  232.4 18.6 %all-to-all-start.6 = ((bf16[8,512,128]{2,1,0:T(8,128)(2,1)}), bf16[8,512,128]{2,1,0:T(8,128)(2,1)S(1)}, u32[]{:S(2)}, u32[]{:S(2)}) async-start(bf16[8,512,128]{2,1,0:T(8,128)(2,1)} %bitcast.7), calls=%async_computation.6 | async-start | bytes 2097152 | tf_op jit(solution)/shard_map/all_to_all | solution.py:123
  239.9 48.8 %copy-start.6 = (bf16[512,128]{1,0:T(8,128)(2,1)S(1)}, bf16[512,128]{1,0:T(8,128)(2,1)}, u32[]{:S(2)}) copy-start(bf16[512,128]{1,0:T(8,128)(2,1)} %get-tuple-element.6) | copy-start | bytes 393220
  239.9 49.5 %copy-start.8 = (bf16[256,256]{1,0:T(8,128)(2,1)S(1)}, bf16[256,256]{1,0:T(8,128)(2,1)}, u32[]{:S(2)}) copy-start(bf16[256,256]{1,0:T(8,128)(2,1)} %param.8) | copy-start | bytes 393220
  284.4 15.5 %all-to-all-start.8 = ((f32[128,2,256]{2,1,0:T(2,128)}), f32[128,2,256]{2,1,0:T(2,128)S(1)}, u32[]{:S(2)}, u32[]{:S(2)}) async-start(f32[128,2,256]{2,1,0:T(2,128)} %broadcast_in_dim.11), calls=%async_computation.8 | async-start | bytes 524288 | tf_op jit(solution)/shard_map/all_to_all | solution.py:119

commit v5 on v3

--- a/solution.py
+++ b/solution.py
@@ -5,7 +5,7 @@
 from jax import lax
 from jax.experimental import pallas as pl
 from jax.experimental.pallas import tpu as pltpu
-from jax.sharding import PartitionSpec as P
+from jax.sharding import Mesh, PartitionSpec as P
 
 
 GROUP = 32
@@ -125,9 +125,13 @@
 
 def body(features, weight, tile_values, tile_row, tile_col, tile_count, cotangent):
     row_count = lax.axis_size("row")
-    col_count = lax.axis_size("col")
+    pair_count = lax.axis_size("colhi")
+    core_count = lax.axis_size("core")
+    col_count = pair_count * core_count
     node_dev = features.shape[0]
+    hidden = features.shape[1]
     tile_size = tile_values.shape[1]
+    per_dev = node_dev // tile_size
     row_tiles = node_dev * col_count // tile_size
     col_tiles = node_dev * row_count // tile_size
     count = tile_count.reshape(1)
@@ -136,12 +140,22 @@
     forward_part = tile_products(
         tile_values, tile_col, tile_row, count, panel_rows, row_tiles, True
     )
-    summed = scatter_sum(forward_part, "col", col_count)
+    by_core = forward_part.reshape(pair_count, core_count, node_dev, hidden)
+    on_chip = lax.all_to_all(by_core, "core", 1, 1, tiled=False)
+    chip_sum = on_chip.astype(jnp.float32).sum(1).astype(jnp.bfloat16)
+    summed = scatter_sum(chip_sum, "colhi", pair_count)
     activated = jax.nn.silu(summed).astype(jnp.bfloat16)
     slope = (cotangent.astype(jnp.float32) * silu_slope(summed)).astype(jnp.bfloat16)
-    slope_full = gather_rows(slope, "col", col_count)
+    slope_pairs = gather_rows(slope, "colhi", pair_count)
+    slope_full = gather_rows(slope_pairs, "core", core_count)
+    owner = tile_row // per_dev
+    slope_index = (
+        (owner % core_count) * (pair_count * per_dev)
+        + (owner // core_count) * per_dev
+        + tile_row % per_dev
+    )
     column_part = tile_products(
-        tile_values, tile_row, tile_col, count, slope_full, col_tiles, False
+        tile_values, slope_index, tile_col, count, slope_full, col_tiles, False
     )
     grad_nodes = scatter_sum(column_part, "row", row_count).astype(jnp.bfloat16)
     grad_features = lax.dot_general(
@@ -150,26 +164,30 @@
     weight_term = lax.dot_general(
         features, grad_nodes, (((0,), (0,)), ((), ())), preferred_element_type=jnp.float32
     )
+    everyone = ("row", "colhi", "core")
     devices = row_count * col_count
-    weight_piece = scatter_sum(weight_term, ("row", "col"), devices)
-    grad_weight = gather_rows(weight_piece, ("row", "col"), devices)
+    weight_piece = scatter_sum(weight_term, everyone, devices)
+    grad_weight = gather_rows(weight_piece, everyone, devices)
     return (activated, grad_features, grad_weight)
 
 
 def solution(mesh):
+    rows, cols = mesh.devices.shape
+    fine = Mesh(mesh.devices.reshape(rows, cols // 2, 2), ("row", "colhi", "core"))
+    col = ("colhi", "core")
     placed = (
-        P(("col", "row"), None),
+        P((*col, "row"), None),
         P(),
-        P(("row", "col"), None, None),
-        P(("row", "col")),
-        P(("row", "col")),
-        P("row", "col"),
-        P(("row", "col"), None),
+        P(("row", *col), None, None),
+        P(("row", *col)),
+        P(("row", *col)),
+        P("row", col),
+        P(("row", *col), None),
     )
     return jax.shard_map(
         body,
-        mesh=mesh,
+        mesh=fine,
         in_specs=placed,
-        out_specs=(P(("row", "col"), None), P(("col", "row"), None), P()),
+        out_specs=(P(("row", *col), None), P((*col, "row"), None), P()),
         check_vma=False,
     )

time: 285 us -> 264 us (0.926)
  blocking collectives: 180 us -> 103 us
  waiting for transfers between devices: 35.7 us -> 62.3 us
  Pallas kernels: 48.4 us -> 65.4 us
  local copies, waits for them, and re-layouts: 4.99 us -> 9.12 us
  starting transfers between devices: 10.2 us -> 13.9 us
  other arithmetic: 2.07 us -> 5.03 us
    all_to_all x1, blocking collectives: 55 us -> 10.6 us  [gather_rows(): lax.all_to_all(copies, axes, 0, 0, tiled=True).reshape(-1, values.shape[-1])]
    all_to_all x3, blocking collectives: 125 us -> 85 us  [scatter_sum(): lax.all_to_all(values.reshape(parts, -1, values.shape[-1]), axes, 0, 0, t...]
    all_to_all x2 -> x3, waiting for transfers between devices: 35.7 us -> 62.3 us  [gather_rows(): lax.all_to_all(copies, axes, 0, 0, tiled=True).reshape(-1, values.shape[-1])]
    pallas_call x2, Pallas kernels: 48.4 us -> 65.4 us  [tile_products(): pl.pallas_call(functools.partial(tile_kernel, forward=forward), grid_spec...]
    all_to_all x0 -> x1, blocking collectives: none -> 7.77 us  [body(): on_chip = lax.all_to_all(by_core, 'core', 1, 1, tiled=False)]
    all_to_all x2 -> x3, starting transfers between devices: 10.2 us -> 13.9 us  [gather_rows(): lax.all_to_all(copies, axes, 0, 0, tiled=True).reshape(-1, values.shape[-1])]
    reduce_sum x0 -> x1, other arithmetic: none -> 3.23 us  [body(): chip_sum = on_chip.astype(jnp.float32).sum(1).astype(jnp.bfloat16)]
  transfers between devices with their start and end apart: 2 -> 3, of which waited for: 2 -> 3; matrix products, arithmetic and copies ran while one was open for 0% -> 0% of each run, Pallas kernels for 0% -> 0%
where the time goes in v5:
time: 264 us; the launch traced here: 263 us
  blocking collectives  103 us (39%)
  Pallas kernels  65.4 us (25%)
  waiting for transfers between devices  62.3 us (24%)
  starting transfers between devices  13.9 us (5%)
  local copies, waits for them, and re-layouts  9.12 us (3%)
  other arithmetic  5.03 us (2%)
    all_to_all x3, blocking collectives, scatter_sum(): lax.all_to_all(values.reshape(parts, -1, values.shape[-1]), axes, 0, 0, t...  85 us
    pallas_call x2, Pallas kernels, tile_products(): pl.pallas_call(functools.partial(tile_kernel, forward=forward), grid_spec...  65.4 us
    all_to_all x3, waiting for transfers between devices, gather_rows(): lax.all_to_all(copies, axes, 0, 0, tiled=True).reshape(-1, values.shape[-1])  62.3 us
    all_to_all x3, starting transfers between devices, gather_rows(): lax.all_to_all(copies, axes, 0, 0, tiled=True).reshape(-1, values.shape[-1])  13.9 us
    all_to_all x1, blocking collectives, gather_rows(): lax.all_to_all(copies, axes, 0, 0, tiled=True).reshape(-1, values.shape[-1])  10.6 us
    all_to_all x1, blocking collectives, body(): on_chip = lax.all_to_all(by_core, 'core', 1, 1, tiled=False)  7.77 us
  transfers between devices with their start and end apart: 3, of which 3 were waited for; matrix products, arithmetic and copies ran while one was open for 0% of the time, Pallas kernels for 0%

profile of v5, /device:TPU:1, one launch (start us, length us, event | category | flops | bytes accessed | tf_op | source)
XLA Modules:
  0.0 262.9 jit_solution(114729212586990648)
XLA Ops:
  0.6 0.0 copy-start
  0.6 0.9 copy-done
  1.6 1.1 convolution_convert_fusion.1
  2.7 1.5 broadcast_in_dim.10
  4.2 0.0 copy-start.1
  4.2 0.0 copy-start.2
  4.2 6.1 %all-to-all-start = ((bf16[8,512,256]{2,1,0:T(8,128)(2,1)}), bf16[8,512,256]{2,1,0:T(8,128)(2,1)S(1)}, u32[]{:S(2)}, u32[]{:S(2)}) async-start(bf16[8,512,256]{2,1,0:T(8,128)(2,1)} %broadcast_in_dim.10), calls=%async_computation | async-start | bytes 4194304 | tf_op jit(solution)/shard_map/all_to_all | solution.py:118
  10.9 25.5 %all-to-all-done = bf16[8,512,256]{2,1,0:T(8,128)(2,1)S(1)} async-done(((bf16[8,512,256]{2,1,0:T(8,128)(2,1)}), bf16[8,512,256]{2,1,0:T(8,128)(2,1)S(1)}, u32[]{:S(2)}, u32[]{:S(2)}) %all-to-all-start) | async-done | bytes 2097184 | tf_op jit(solution)/shard_map/all_to_all | solution.py:118
  36.4 0.0 copy-done.1
  36.4 0.0 copy-done.2
  36.4 31.4 %shard_map.94 = bf16[8192,256]{1,0:T(8,128)(2,1)} custom-call(s32[1]{0:T(128)} %bitcast.14.count_ref, s32[512]{0:T(512)S(1)} %copy-done.2, s32[512]{0:T(512)S(1)} %copy-done.1, bf16[512,128,128]{2,1,0:T(8,128)(2,1)} %tiles_ref.3, bf16[4096,256]{1,0:T(8,128)(2,1)S(1)} %bitcast.16), custom_call_target="tpu_custom_call" | custom-call | flops 4294967296 | bytes 23068672 | tf_op jit(solution)/shard_map/pallas_call | solution.py:101
  67.8 2.5 copy.11
  70.3 7.8 %all_to_all.40 = bf16[8,2,512,256]{3,2,0,1:T(8,128)(2,1)} all-to-all(bf16[8,2,512,256]{3,2,0,1:T(8,128)(2,1)S(1)} %copy.11), channel_id=1, replica_groups=mesh['row'=8,'colhi'=8,'core'=2] {'core'}, dimensions={1} | all-to-all | bytes 8388608 | tf_op jit(solution)/shard_map/all_to_all | solution.py:144
  78.1 3.2 %reduce_sum.42 = bf16[8,512,256]{2,1,0:T(8,128)(2,1)S(1)} reduce(bf16[8,2,512,256]{3,2,0,1:T(8,128)(2,1)} %all_to_all.40, bf16[]{:T(256)} %constant.47.clone.1), dimensions={1}, to_apply=%region_0.0 | reduce | flops 1048576 | bytes 6291458 | tf_op jit(solution)/shard_map/reduce_sum | solution.py:145
  81.3 38.3 %all_to_all.41 = bf16[8,512,256]{2,1,0:T(8,128)(2,1)S(1)} all-to-all(bf16[8,512,256]{2,1,0:T(8,128)(2,1)S(1)} %reduce_sum.42), channel_id=1, replica_groups=mesh['row'=8,'colhi'=8,'core'=2] {'colhi'}, dimensions={0} | all-to-all | bytes 4194304 | tf_op jit(solution)/shard_map/all_to_all | solution.py:122
  119.6 0.0 copy-start.4
  119.6 0.3 convert_reduce_fusion
  119.9 0.7 copy-done.4
  120.6 0.9 multiply_convert_fusion
  121.5 1.5 broadcast_in_dim.11
  123.0 3.6 %all-to-all-start.3 = ((bf16[8,512,256]{2,1,0:T(8,128)(2,1)}), bf16[8,512,256]{2,1,0:T(8,128)(2,1)S(1)}, u32[]{:S(2)}, u32[]{:S(2)}) async-start(bf16[8,512,256]{2,1,0:T(8,128)(2,1)} %broadcast_in_dim.11), calls=%async_computation.3 | async-start | bytes 4194304 | tf_op jit(solution)/shard_map/all_to_all | solution.py:118
  126.7 26.6 %all-to-all-done.3 = bf16[8,512,256]{2,1,0:T(8,128)(2,1)S(1)} async-done(((bf16[8,512,256]{2,1,0:T(8,128)(2,1)}), bf16[8,512,256]{2,1,0:T(8,128)(2,1)S(1)}, u32[]{:S(2)}, u32[]{:S(2)}) %all-to-all-start.3) | async-done | bytes 2097184 | tf_op jit(solution)/shard_map/all_to_all | solution.py:118
  153.2 0.3 broadcast_in_dim.13
  153.5 10.6 %all_to_all.42 = bf16[2,4096,256]{2,1,0:T(8,128)(2,1)} all-to-all(bf16[2,4096,256]{2,1,0:T(8,128)(2,1)S(1)} %broadcast_in_dim.13), channel_id=1, replica_groups=mesh['row'=8,'colhi'=8,'core'=2] {'core'}, dimensions={0} | all-to-all | bytes 8388608 | tf_op jit(solution)/shard_map/all_to_all | solution.py:118
  164.1 34.0 %shard_map.95 = bf16[4096,256]{1,0:T(8,128)(2,1)S(1)} custom-call(s32[1]{0:T(128)} %bitcast.15.count_ref, s32[512]{0:T(512)S(1)} %copy-done.1, s32[512]{0:T(512)S(1)} %fusion.2.fetch_ref, bf16[512,128,128]{2,1,0:T(8,128)(2,1)} %tiles_ref.3, bf16[8192,256]{1,0:T(8,128)(2,1)} %bitcast.18), custom_call_target="tpu_custom_call" | custom-call | flops 4294967296 | bytes 23068672 | tf_op jit(solution)/shard_map/pallas_call | solution.py:101
  198.1 31.5 %all_to_all.43 = bf16[8,512,256]{2,1,0:T(8,128)(2,1)S(1)} all-to-all(bf16[8,512,256]{2,1,0:T(8,128)(2,1)S(1)} %bitcast.17), channel_id=1, replica_groups=mesh['row'=8,'colhi'=8,'core'=2] {'row'}, dimensions={0} | all-to-all | bytes 4194304 | tf_op jit(solution)/shard_map/all_to_all | solution.py:122
  229.6 0.0 copy-start.3
  229.6 0.4 reduce_sum.44
  230.0 0.3 convolution_bitcast_fusion
  230.3 0.1 reshape.36
  230.4 15.1 %all_to_all.44 = f32[128,2,256]{2,1,0:T(2,128)S(1)} all-to-all(f32[128,2,256]{2,1,0:T(2,128)S(1)} %reshape.36), channel_id=1, replica_groups=mesh['row'=8,'colhi'=8,'core'=2] {'row','colhi','core'}, dimensions={0} | all-to-all | bytes 524288 | tf_op jit(solution)/shard_map/all_to_all | solution.py:122
  245.6 0.1 reduce_sum.45
  245.7 0.8 broadcast_in_dim.14
  246.5 4.2 %all-to-all-start.7 = ((f32[128,2,256]{2,1,0:T(2,128)}), f32[128,2,256]{2,1,0:T(2,128)S(1)}, u32[]{:S(2)}, u32[]{:S(2)}) async-start(f32[128,2,256]{2,1,0:T(2,128)} %broadcast_in_dim.14), calls=%async_computation.7 | async-start | bytes 524288 | tf_op jit(solution)/shard_map/all_to_all | solution.py:118
  250.8 0.0 copy-done.3
  250.8 1.0 convolution_convert_fusion
  251.7 10.2 %all-to-all-done.7 = f32[128,2,256]{2,1,0:T(2,128)S(1)} async-done(((f32[128,2,256]{2,1,0:T(2,128)}), f32[128,2,256]{2,1,0:T(2,128)S(1)}, u32[]{:S(2)}, u32[]{:S(2)}) %all-to-all-start.7) | async-done | bytes 262176 | tf_op jit(solution)/shard_map/all_to_all | solution.py:118
  262.0 0.9 reshape.37
  (1 shorter events, 0.0 us)
Async XLA Ops:
  0.6 1.0 copy-start
  4.2 32.2 %copy-start.1 = (s32[512]{0:T(512)S(1)}, s32[512]{0:T(512)}, u32[]{:S(2)}) copy-start(s32[512]{0:T(512)} %place_ref.3) | copy-start | bytes 6148
  4.2 32.2 %copy-start.2 = (s32[512]{0:T(512)S(1)}, s32[512]{0:T(512)}, u32[]{:S(2)}) copy-start(s32[512]{0:T(512)} %place_ref.2) | copy-start | bytes 6148
  4.2 32.2 %all-to-all-start = ((bf16[8,512,256]{2,1,0:T(8,128)(2,1)}), bf16[8,512,256]{2,1,0:T(8,128)(2,1)S(1)}, u32[]{:S(2)}, u32[]{:S(2)}) async-start(bf16[8,512,256]{2,1,0:T(8,128)(2,1)} %broadcast_in_dim.10), calls=%async_computation | async-start | bytes 4194304 | tf_op jit(solution)/shard_map/all_to_all | solution.py:118
  119.6 1.0 copy-start.4
  123.0 30.2 %all-to-all-start.3 = ((bf16[8,512,256]{2,1,0:T(8,128)(2,1)}), bf16[8,512,256]{2,1,0:T(8,128)(2,1)S(1)}, u32[]{:S(2)}, u32[]{:S(2)}) async-start(bf16[8,512,256]{2,1,0:T(8,128)(2,1)} %broadcast_in_dim.11), calls=%async_computation.3 | async-start | bytes 4194304 | tf_op jit(solution)/shard_map/all_to_all | solution.py:118
  229.6 21.1 %copy-start.3 = (bf16[256,256]{1,0:T(8,128)(2,1)S(1)}, bf16[256,256]{1,0:T(8,128)(2,1)}, u32[]{:S(2)}) copy-start(bf16[256,256]{1,0:T(8,128)(2,1)} %param.8) | copy-start | bytes 393220
  246.5 15.5 %all-to-all-start.7 = ((f32[128,2,256]{2,1,0:T(2,128)}), f32[128,2,256]{2,1,0:T(2,128)S(1)}, u32[]{:S(2)}, u32[]{:S(2)}) async-start(f32[128,2,256]{2,1,0:T(2,128)} %broadcast_in_dim.14), calls=%async_computation.7 | async-start | bytes 524288 | tf_op jit(solution)/shard_map/all_to_all | solution.py:118

commit v6 on v5

--- a/solution.py
+++ b/solution.py
@@ -140,17 +140,21 @@
     forward_part = tile_products(
         tile_values, tile_col, tile_row, count, panel_rows, row_tiles, True
     )
+    core = lax.axis_index("core")
+    swap = [(0, 1), (1, 0)]
     by_core = forward_part.reshape(pair_count, core_count, node_dev, hidden)
-    on_chip = lax.all_to_all(by_core, "core", 1, 1, tiled=False)
-    chip_sum = on_chip.astype(jnp.float32).sum(1).astype(jnp.bfloat16)
+    keep = lax.dynamic_index_in_dim(by_core, core, 1, keepdims=False)
+    give = lax.dynamic_index_in_dim(by_core, 1 - core, 1, keepdims=False)
+    got = lax.ppermute(give, "core", swap)
+    chip_sum = (keep.astype(jnp.float32) + got.astype(jnp.float32)).astype(jnp.bfloat16)
     summed = scatter_sum(chip_sum, "colhi", pair_count)
     activated = jax.nn.silu(summed).astype(jnp.bfloat16)
     slope = (cotangent.astype(jnp.float32) * silu_slope(summed)).astype(jnp.bfloat16)
     slope_pairs = gather_rows(slope, "colhi", pair_count)
-    slope_full = gather_rows(slope_pairs, "core", core_count)
+    slope_full = jnp.concatenate([slope_pairs, lax.ppermute(slope_pairs, "core", swap)], axis=0)
     owner = tile_row // per_dev
     slope_index = (
-        (owner % core_count) * (pair_count * per_dev)
+        (owner % core_count != core).astype(jnp.int32) * (pair_count * per_dev)
         + (owner // core_count) * per_dev
         + tile_row % per_dev
     )

time: 264 us -> 253 us (0.958)
  blocking collectives: 103 us -> 145 us
  Pallas kernels: 65.4 us -> 31.5 us
  waiting for transfers between devices: 62.3 us -> 43.5 us
    pallas_call x2, Pallas kernels: 65.4 us -> 31.5 us  [tile_products(): pl.pallas_call(functools.partial(tile_kernel, forward=forward), grid_spec...]
    all_to_all x3, blocking collectives: 85 us -> 115 us  [scatter_sum(): lax.all_to_all(values.reshape(parts, -1, values.shape[-1]), axes, 0, 0, t...]
    all_to_all x3 -> x2, waiting for transfers between devices: 62.3 us -> 35.7 us  [gather_rows(): lax.all_to_all(copies, axes, 0, 0, tiled=True).reshape(-1, values.shape[-1])]
    all_to_all x1, blocking collectives: 10.6 us -> 29.9 us  [gather_rows(): lax.all_to_all(copies, axes, 0, 0, tiled=True).reshape(-1, values.shape[-1])]
    all_to_all x1 -> x0, blocking collectives: 7.77 us -> none  [body(): on_chip = lax.all_to_all(by_core, 'core', 1, 1, tiled=False)]
    ppermute x0 -> x2, waiting for transfers between devices: none -> 7.76 us  [the longest x1 4 us: body(): got = lax.ppermute(give, 'core', swap)]
    ppermute x0 -> x2, starting transfers between devices: none -> 4.21 us  [the longest x1 2.38 us: body(): lax.ppermute(slope_pairs, 'core', swap)]
    all_to_all x3 -> x2, starting transfers between devices: 13.9 us -> 10.3 us  [gather_rows(): lax.all_to_all(copies, axes, 0, 0, tiled=True).reshape(-1, values.shape[-1])]
  transfers between devices with their start and end apart: 3 -> 4, of which waited for: 3 -> 4; matrix products, arithmetic and copies ran while one was open for 0% -> 0% of each run, Pallas kernels for 0% -> 0%
where the time goes in v6:
time: 253 us; the launch traced here: 252 us
  blocking collectives  145 us (57%)
  waiting for transfers between devices  43.5 us (17%)
  Pallas kernels  31.5 us (12%)
  starting transfers between devices  14.5 us (6%)
  local copies, waits for them, and re-layouts  8.06 us (3%)
  other arithmetic  6.16 us (2%)
    all_to_all x3, blocking collectives, scatter_sum(): lax.all_to_all(values.reshape(parts, -1, values.shape[-1]), axes, 0, 0, t...  115 us
    all_to_all x2, waiting for transfers between devices, gather_rows(): lax.all_to_all(copies, axes, 0, 0, tiled=True).reshape(-1, values.shape[-1])  35.7 us
    pallas_call x2, Pallas kernels, tile_products(): pl.pallas_call(functools.partial(tile_kernel, forward=forward), grid_spec...  31.5 us
    all_to_all x1, blocking collectives, gather_rows(): lax.all_to_all(copies, axes, 0, 0, tiled=True).reshape(-1, values.shape[-1])  29.9 us
    all_to_all x2, starting transfers between devices, gather_rows(): lax.all_to_all(copies, axes, 0, 0, tiled=True).reshape(-1, values.shape[-1])  10.3 us
  transfers between devices with their start and end apart: 4, of which 4 were waited for; matrix products, arithmetic and copies ran while one was open for 0% of the time, Pallas kernels for 0%

profile of v6, /device:TPU:1, one launch (start us, length us, event | category | flops | bytes accessed | tf_op | source)
XLA Modules:
  0.0 252.1 jit_solution(3345994373852732982)
XLA Ops:
  0.6 0.0 copy-start
  0.6 0.9 copy-done
  1.6 1.1 convolution_convert_fusion.1
  2.7 1.5 broadcast_in_dim.6
  4.2 0.0 copy-start.1
  4.2 0.0 copy-start.2
  4.2 6.1 %all-to-all-start = ((bf16[8,512,256]{2,1,0:T(8,128)(2,1)}), bf16[8,512,256]{2,1,0:T(8,128)(2,1)S(1)}, u32[]{:S(2)}, u32[]{:S(2)}) async-start(bf16[8,512,256]{2,1,0:T(8,128)(2,1)} %broadcast_in_dim.6), calls=%async_computation | async-start | bytes 4194304 | tf_op jit(solution)/shard_map/all_to_all | solution.py:118
  10.9 25.5 %all-to-all-done = bf16[8,512,256]{2,1,0:T(8,128)(2,1)S(1)} async-done(((bf16[8,512,256]{2,1,0:T(8,128)(2,1)}), bf16[8,512,256]{2,1,0:T(8,128)(2,1)S(1)}, u32[]{:S(2)}, u32[]{:S(2)}) %all-to-all-start) | async-done | bytes 2097184 | tf_op jit(solution)/shard_map/all_to_all | solution.py:118
  36.4 0.0 copy-done.1
  36.4 0.0 copy-done.2
  36.4 15.6 %shard_map.94 = bf16[8192,256]{1,0:T(8,128)(2,1)} custom-call(s32[1]{0:T(128)} %bitcast.18.count_ref, s32[512]{0:T(512)S(1)} %copy-done.2, s32[512]{0:T(512)S(1)} %copy-done.1, bf16[512,128,128]{2,1,0:T(8,128)(2,1)} %tiles_ref.3, bf16[4096,256]{1,0:T(8,128)(2,1)S(1)} %bitcast.20), custom_call_target="tpu_custom_call" | custom-call | flops 4294967296 | bytes 23068672 | tf_op jit(solution)/shard_map/pallas_call | solution.py:101
  52.0 3.0 %dynamic-slice_bitcast_fusion = bf16[8,512,256]{2,1,0:T(8,128)(2,1)} fusion(bf16[8,2,512,256]{3,2,1,0:T(8,128)(2,1)} %bitcast.22, s32[]{:T(128)S(6)} %select_n.27), kind=kLoop, calls=%fused_computation.4 | loop fusion | bytes 4194308 | tf_op jit(solution)/shard_map/jit(dynamic_index_in_dim)/squeeze | solution.py:147
  55.1 1.8 collective-permute-start
  56.9 4.0 %collective-permute-done = bf16[8,512,256]{2,1,0:T(8,128)(2,1)S(1)} collective-permute-done((bf16[8,512,256]{2,1,0:T(8,128)(2,1)}, bf16[8,512,256]{2,1,0:T(8,128)(2,1)S(1)}, u32[]{:S(2)}, u32[]{:S(2)}) %collective-permute-start) | collective-permute-done | bytes 2097184 | tf_op jit(solution)/shard_map/ppermute | solution.py:148
  60.9 2.1 fusion
  63.1 48.9 %all_to_all.30 = bf16[8,512,256]{2,1,0:T(8,128)(2,1)S(1)} all-to-all(bf16[8,512,256]{2,1,0:T(8,128)(2,1)S(1)} %fusion), channel_id=1, replica_groups=mesh['row'=8,'colhi'=8,'core'=2] {'colhi'}, dimensions={0} | all-to-all | bytes 4194304 | tf_op jit(solution)/shard_map/all_to_all | solution.py:122
  112.0 0.0 copy-start.4
  112.0 0.3 convert_reduce_fusion
  112.3 0.7 copy-done.4
  112.9 0.9 multiply_convert_fusion
  113.9 0.1 broadcast_in_dim.7
  114.0 29.9 %all_to_all.31 = bf16[8,512,256]{2,1,0:T(8,128)(2,1)S(1)} all-to-all(bf16[8,512,256]{2,1,0:T(8,128)(2,1)S(1)} %broadcast_in_dim.7), channel_id=1, replica_groups=mesh['row'=8,'colhi'=8,'core'=2] {'colhi'}, dimensions={0} | all-to-all | bytes 4194304 | tf_op jit(solution)/shard_map/all_to_all | solution.py:118
  143.9 2.4 collective-permute-start.1
  146.3 3.8 %collective-permute-done.1 = bf16[4096,256]{1,0:T(8,128)(2,1)S(1)} collective-permute-done((bf16[4096,256]{1,0:T(8,128)(2,1)S(1)}, bf16[4096,256]{1,0:T(8,128)(2,1)S(1)}, u32[]{:S(2)}, u32[]{:S(2)}) %collective-permute-start.1) | collective-permute-done | bytes 2097184 | tf_op jit(solution)/shard_map/ppermute | solution.py:154
  150.1 2.2 pad_maximum_fusion.src_ref
  152.3 15.9 %shard_map.95 = bf16[4096,256]{1,0:T(8,128)(2,1)S(1)} custom-call(s32[1]{0:T(128)} %bitcast.19.count_ref, s32[512]{0:T(512)S(1)} %copy-done.1, s32[512]{0:T(512)S(1)} %fusion.4.fetch_ref, bf16[512,128,128]{2,1,0:T(8,128)(2,1)} %tiles_ref.3, bf16[8192,256]{1,0:T(8,128)(2,1)} %pad_maximum_fusion.src_ref), custom_call_target="tpu_custom_call" | custom-call | flops 4294967296 | bytes 23068672 | tf_op jit(solution)/shard_map/pallas_call | solution.py:101
  168.2 37.9 %all_to_all.32 = bf16[8,512,256]{2,1,0:T(8,128)(2,1)S(1)} all-to-all(bf16[8,512,256]{2,1,0:T(8,128)(2,1)S(1)} %bitcast.21), channel_id=1, replica_groups=mesh['row'=8,'colhi'=8,'core'=2] {'row'}, dimensions={0} | all-to-all | bytes 4194304 | tf_op jit(solution)/shard_map/all_to_all | solution.py:122
  206.0 0.0 copy-start.3
  206.1 0.4 reduce_sum.31
  206.4 0.3 convolution_bitcast_fusion
  206.7 0.1 reshape.37
  206.9 27.9 %all_to_all.33 = f32[128,2,256]{2,1,0:T(2,128)S(1)} all-to-all(f32[128,2,256]{2,1,0:T(2,128)S(1)} %reshape.37), channel_id=1, replica_groups=mesh['row'=8,'colhi'=8,'core'=2] {'row','colhi','core'}, dimensions={0} | all-to-all | bytes 524288 | tf_op jit(solution)/shard_map/all_to_all | solution.py:122
  234.8 0.1 reduce_sum.32
  235.0 0.8 broadcast_in_dim.8
  235.7 4.2 %all-to-all-start.5 = ((f32[128,2,256]{2,1,0:T(2,128)}), f32[128,2,256]{2,1,0:T(2,128)S(1)}, u32[]{:S(2)}, u32[]{:S(2)}) async-start(f32[128,2,256]{2,1,0:T(2,128)} %broadcast_in_dim.8), calls=%async_computation.5 | async-start | bytes 524288 | tf_op jit(solution)/shard_map/all_to_all | solution.py:118
  240.0 0.0 copy-done.3
  240.0 1.0 convolution_convert_fusion
  241.0 10.2 %all-to-all-done.5 = f32[128,2,256]{2,1,0:T(2,128)S(1)} async-done(((f32[128,2,256]{2,1,0:T(2,128)}), f32[128,2,256]{2,1,0:T(2,128)S(1)}, u32[]{:S(2)}, u32[]{:S(2)}) %all-to-all-start.5) | async-done | bytes 262176 | tf_op jit(solution)/shard_map/all_to_all | solution.py:118
  251.2 0.9 reshape.38
  (1 shorter events, 0.0 us)
Async XLA Ops:
  0.6 1.0 copy-start
  4.2 32.2 %copy-start.1 = (s32[512]{0:T(512)S(1)}, s32[512]{0:T(512)}, u32[]{:S(2)}) copy-start(s32[512]{0:T(512)} %place_ref.3) | copy-start | bytes 6148
  4.2 32.2 %copy-start.2 = (s32[512]{0:T(512)S(1)}, s32[512]{0:T(512)}, u32[]{:S(2)}) copy-start(s32[512]{0:T(512)} %place_ref.2) | copy-start | bytes 6148
  4.2 32.2 %all-to-all-start = ((bf16[8,512,256]{2,1,0:T(8,128)(2,1)}), bf16[8,512,256]{2,1,0:T(8,128)(2,1)S(1)}, u32[]{:S(2)}, u32[]{:S(2)}) async-start(bf16[8,512,256]{2,1,0:T(8,128)(2,1)} %broadcast_in_dim.6), calls=%async_computation | async-start | bytes 4194304 | tf_op jit(solution)/shard_map/all_to_all | solution.py:118
  55.1 5.8 %collective-permute-start = (bf16[8,512,256]{2,1,0:T(8,128)(2,1)}, bf16[8,512,256]{2,1,0:T(8,128)(2,1)S(1)}, u32[]{:S(2)}, u32[]{:S(2)}) collective-permute-start(bf16[8,512,256]{2,1,0:T(8,128)(2,1)} %dynamic-slice_bitcast_fusion), channel_id=1, source_target_pairs={{0,1},{1,0},{2,3},{3,2},{4,5},{5,4},{6,7},{7,6},{8,9},{9,8},{10,11... | collective-permute-start | bytes 6291464 | tf_op jit(solution)/shard_map/ppermute | solution.py:148
  112.0 1.0 copy-start.4
  143.9 6.2 %collective-permute-start.1 = (bf16[4096,256]{1,0:T(8,128)(2,1)S(1)}, bf16[4096,256]{1,0:T(8,128)(2,1)S(1)}, u32[]{:S(2)}, u32[]{:S(2)}) collective-permute-start(bf16[4096,256]{1,0:T(8,128)(2,1)S(1)} %bitcast.24), channel_id=1, source_target_pairs={{0,1},{1,0},{2,3},{3,2},{4,5},{5,4},{6,7},{7,6},{8,9},{9,8},{10,11... | collective-permute-start | bytes 6291464 | tf_op jit(solution)/shard_map/ppermute | solution.py:154
  206.0 33.9 %copy-start.3 = (bf16[256,256]{1,0:T(8,128)(2,1)S(1)}, bf16[256,256]{1,0:T(8,128)(2,1)}, u32[]{:S(2)}) copy-start(bf16[256,256]{1,0:T(8,128)(2,1)} %param.8) | copy-start | bytes 393220
  235.7 15.5 %all-to-all-start.5 = ((f32[128,2,256]{2,1,0:T(2,128)}), f32[128,2,256]{2,1,0:T(2,128)S(1)}, u32[]{:S(2)}, u32[]{:S(2)}) async-start(f32[128,2,256]{2,1,0:T(2,128)} %broadcast_in_dim.8), calls=%async_computation.5 | async-start | bytes 524288 | tf_op jit(solution)/shard_map/all_to_all | solution.py:118

commit v7 on v6

--- a/solution.py
+++ b/solution.py
@@ -8,9 +8,9 @@
 from jax.sharding import Mesh, PartitionSpec as P
 
 
-GROUP = 32
+GROUP = 64
 CHUNK = 256
-UNROLL = 4
+UNROLL = (32, 8, 1)
 
 
 def silu_slope(values):
@@ -50,20 +50,21 @@
         dst_rows = pl.ds(pl.multiple_of(place_ref[slot] * tile, tile), tile)
         acc_ref[dst_rows, :] += prod
 
-    def many(k, carry):
-        j0 = k * UNROLL
-        prods = [product(base + j0 + u, j0 + u) for u in range(UNROLL)]
-        for u in range(UNROLL):
-            add(base + j0 + u, prods[u])
-        return carry
+    def run(start, stop, width):
+        def chunk(k, carry):
+            j0 = start + k * width
+            prods = [product(base + j0 + u, j0 + u) for u in range(width)]
+            for u in range(width):
+                add(base + j0 + u, prods[u])
+            return carry
 
-    def one(j, carry):
-        add(base + j, product(base + j, j))
-        return carry
+        chunks = (stop - start) // width
+        lax.fori_loop(0, chunks, chunk, 0)
+        return start + chunks * width
 
-    full = live // UNROLL
-    lax.fori_loop(0, full, many, 0)
-    lax.fori_loop(full * UNROLL, live, one, 0)
+    done = 0
+    for width in UNROLL:
+        done = run(done, live, width)
 
     @pl.when(step == pl.num_programs(0) - 1)
     def _():

time: 253 us -> 220 us (0.87)
  blocking collectives: 145 us -> 115 us
    all_to_all x3, blocking collectives: 115 us -> 85.4 us  [scatter_sum(): lax.all_to_all(values.reshape(parts, -1, values.shape[-1]), axes, 0, 0, t...]
where the time goes in v7:
time: 220 us; the launch traced here: 219 us
  blocking collectives  115 us (52%)
  waiting for transfers between devices  43.9 us (20%)
  Pallas kernels  29.2 us (13%)
  starting transfers between devices  12.7 us (6%)
  local copies, waits for them, and re-layouts  8.06 us (4%)
  other arithmetic  6.16 us (3%)
  matrix products  2.38 us (1%)
    all_to_all x3, blocking collectives, scatter_sum(): lax.all_to_all(values.reshape(parts, -1, values.shape[-1]), axes, 0, 0, t...  85.4 us
    all_to_all x2, waiting for transfers between devices, gather_rows(): lax.all_to_all(copies, axes, 0, 0, tiled=True).reshape(-1, values.shape[-1])  35.7 us
    all_to_all x1, blocking collectives, gather_rows(): lax.all_to_all(copies, axes, 0, 0, tiled=True).reshape(-1, values.shape[-1])  29.9 us
    pallas_call x2, Pallas kernels, tile_products(): pl.pallas_call(functools.partial(tile_kernel, forward=forward), grid_spec...  29.2 us
    all_to_all x2, starting transfers between devices, gather_rows(): lax.all_to_all(copies, axes, 0, 0, tiled=True).reshape(-1, values.shape[-1])  10.3 us
  transfers between devices with their start and end apart: 4, of which 4 were waited for; matrix products, arithmetic and copies ran while one was open for 0% of the time, Pallas kernels for 0%

profile of v7, /device:TPU:1, one launch (start us, length us, event | category | flops | bytes accessed | tf_op | source)
XLA Modules:
  0.0 219.1 jit_solution(17335209560081255085)
XLA Ops:
  0.6 0.0 copy-start
  0.6 0.9 copy-done
  1.6 1.1 convolution_convert_fusion.1
  2.7 1.5 broadcast_in_dim.6
  4.2 0.0 copy-start.1
  4.2 0.0 copy-start.2
  4.2 6.1 %all-to-all-start = ((bf16[8,512,256]{2,1,0:T(8,128)(2,1)}), bf16[8,512,256]{2,1,0:T(8,128)(2,1)S(1)}, u32[]{:S(2)}, u32[]{:S(2)}) async-start(bf16[8,512,256]{2,1,0:T(8,128)(2,1)} %broadcast_in_dim.6), calls=%async_computation | async-start | bytes 4194304 | tf_op jit(solution)/shard_map/all_to_all | solution.py:119
  10.9 25.5 %all-to-all-done = bf16[8,512,256]{2,1,0:T(8,128)(2,1)S(1)} async-done(((bf16[8,512,256]{2,1,0:T(8,128)(2,1)}), bf16[8,512,256]{2,1,0:T(8,128)(2,1)S(1)}, u32[]{:S(2)}, u32[]{:S(2)}) %all-to-all-start) | async-done | bytes 2097184 | tf_op jit(solution)/shard_map/all_to_all | solution.py:119
  36.4 0.0 copy-done.1
  36.4 0.0 copy-done.2
  36.4 15.1 %shard_map.94 = bf16[8192,256]{1,0:T(8,128)(2,1)} custom-call(s32[1]{0:T(128)} %bitcast.18.count_ref, s32[512]{0:T(512)S(1)} %copy-done.2, s32[512]{0:T(512)S(1)} %copy-done.1, bf16[512,128,128]{2,1,0:T(8,128)(2,1)} %tiles_ref.3, bf16[4096,256]{1,0:T(8,128)(2,1)S(1)} %bitcast.20), custom_call_target="tpu_custom_call" | custom-call | flops 4294967296 | bytes 23068672 | tf_op jit(solution)/shard_map/pallas_call | solution.py:102
  51.5 3.0 %dynamic-slice_bitcast_fusion = bf16[8,512,256]{2,1,0:T(8,128)(2,1)} fusion(bf16[8,2,512,256]{3,2,1,0:T(8,128)(2,1)} %bitcast.22, s32[]{:T(128)S(6)} %select_n.27), kind=kLoop, calls=%fused_computation.4 | loop fusion | bytes 4194308 | tf_op jit(solution)/shard_map/jit(dynamic_index_in_dim)/squeeze | solution.py:148
  54.5 0.0 collective-permute-start
  54.5 4.4 %collective-permute-done = bf16[8,512,256]{2,1,0:T(8,128)(2,1)S(1)} collective-permute-done((bf16[8,512,256]{2,1,0:T(8,128)(2,1)}, bf16[8,512,256]{2,1,0:T(8,128)(2,1)S(1)}, u32[]{:S(2)}, u32[]{:S(2)}) %collective-permute-start) | collective-permute-done | bytes 2097184 | tf_op jit(solution)/shard_map/ppermute | solution.py:149
  58.9 2.1 fusion
  61.0 35.6 %all_to_all.30 = bf16[8,512,256]{2,1,0:T(8,128)(2,1)S(1)} all-to-all(bf16[8,512,256]{2,1,0:T(8,128)(2,1)S(1)} %fusion), channel_id=1, replica_groups=mesh['row'=8,'colhi'=8,'core'=2] {'colhi'}, dimensions={0} | all-to-all | bytes 4194304 | tf_op jit(solution)/shard_map/all_to_all | solution.py:123
  96.6 0.0 copy-start.4
  96.6 0.3 convert_reduce_fusion
  96.9 0.7 copy-done.4
  97.6 0.9 multiply_convert_fusion
  98.5 0.1 broadcast_in_dim.7
  98.7 29.9 %all_to_all.31 = bf16[8,512,256]{2,1,0:T(8,128)(2,1)S(1)} all-to-all(bf16[8,512,256]{2,1,0:T(8,128)(2,1)S(1)} %broadcast_in_dim.7), channel_id=1, replica_groups=mesh['row'=8,'colhi'=8,'core'=2] {'colhi'}, dimensions={0} | all-to-all | bytes 4194304 | tf_op jit(solution)/shard_map/all_to_all | solution.py:119
  128.6 2.4 %collective-permute-start.1 = (bf16[4096,256]{1,0:T(8,128)(2,1)S(1)}, bf16[4096,256]{1,0:T(8,128)(2,1)S(1)}, u32[]{:S(2)}, u32[]{:S(2)}) collective-permute-start(bf16[4096,256]{1,0:T(8,128)(2,1)S(1)} %bitcast.24), channel_id=1, source_target_pairs={{0,1},{1,0},{2,3},{3,2},{4,5},{5,4},{6,7},{7,6},{8,9},{9,8},{10,11... | collective-permute-start | bytes 6291464 | tf_op jit(solution)/shard_map/ppermute | solution.py:155
  131.0 3.8 %collective-permute-done.1 = bf16[4096,256]{1,0:T(8,128)(2,1)S(1)} collective-permute-done((bf16[4096,256]{1,0:T(8,128)(2,1)S(1)}, bf16[4096,256]{1,0:T(8,128)(2,1)S(1)}, u32[]{:S(2)}, u32[]{:S(2)}) %collective-permute-start.1) | collective-permute-done | bytes 2097184 | tf_op jit(solution)/shard_map/ppermute | solution.py:155
  134.8 2.2 %pad_maximum_fusion.src_ref = bf16[8192,256]{1,0:T(8,128)(2,1)} fusion(bf16[4096,256]{1,0:T(8,128)(2,1)S(1)} %collective-permute-done.1, bf16[4096,256]{1,0:T(8,128)(2,1)S(1)} %bitcast.25), kind=kLoop, calls=%fused_computation | loop fusion | flops 8388608 | bytes 8388608 | tf_op jit(solution)/shard_map/concatenate | solution.py:155
  137.0 14.2 %shard_map.95 = bf16[4096,256]{1,0:T(8,128)(2,1)S(1)} custom-call(s32[1]{0:T(128)} %bitcast.19.count_ref, s32[512]{0:T(512)S(1)} %copy-done.1, s32[512]{0:T(512)S(1)} %fusion.4.fetch_ref, bf16[512,128,128]{2,1,0:T(8,128)(2,1)} %tiles_ref.3, bf16[8192,256]{1,0:T(8,128)(2,1)} %pad_maximum_fusion.src_ref), custom_call_target="tpu_custom_call" | custom-call | flops 4294967296 | bytes 23068672 | tf_op jit(solution)/shard_map/pallas_call | solution.py:102
  151.2 32.2 %all_to_all.32 = bf16[8,512,256]{2,1,0:T(8,128)(2,1)S(1)} all-to-all(bf16[8,512,256]{2,1,0:T(8,128)(2,1)S(1)} %bitcast.21), channel_id=1, replica_groups=mesh['row'=8,'colhi'=8,'core'=2] {'row'}, dimensions={0} | all-to-all | bytes 4194304 | tf_op jit(solution)/shard_map/all_to_all | solution.py:123
  183.4 0.0 copy-start.3
  183.4 0.4 reduce_sum.31
  183.8 0.3 convolution_bitcast_fusion
  184.1 0.1 reshape.37
  184.2 17.6 %all_to_all.33 = f32[128,2,256]{2,1,0:T(2,128)S(1)} all-to-all(f32[128,2,256]{2,1,0:T(2,128)S(1)} %reshape.37), channel_id=1, replica_groups=mesh['row'=8,'colhi'=8,'core'=2] {'row','colhi','core'}, dimensions={0} | all-to-all | bytes 524288 | tf_op jit(solution)/shard_map/all_to_all | solution.py:123
  201.8 0.1 reduce_sum.32
  202.0 0.8 broadcast_in_dim.8
  202.7 4.2 %all-to-all-start.5 = ((f32[128,2,256]{2,1,0:T(2,128)}), f32[128,2,256]{2,1,0:T(2,128)S(1)}, u32[]{:S(2)}, u32[]{:S(2)}) async-start(f32[128,2,256]{2,1,0:T(2,128)} %broadcast_in_dim.8), calls=%async_computation.5 | async-start | bytes 524288 | tf_op jit(solution)/shard_map/all_to_all | solution.py:119
  207.0 0.0 copy-done.3
  207.0 1.0 convolution_convert_fusion
  208.0 10.2 %all-to-all-done.5 = f32[128,2,256]{2,1,0:T(2,128)S(1)} async-done(((f32[128,2,256]{2,1,0:T(2,128)}), f32[128,2,256]{2,1,0:T(2,128)S(1)}, u32[]{:S(2)}, u32[]{:S(2)}) %all-to-all-start.5) | async-done | bytes 262176 | tf_op jit(solution)/shard_map/all_to_all | solution.py:119
  218.2 0.9 reshape.38
  (1 shorter events, 0.0 us)
Async XLA Ops:
  0.6 1.0 copy-start
  4.2 32.2 %copy-start.1 = (s32[512]{0:T(512)S(1)}, s32[512]{0:T(512)}, u32[]{:S(2)}) copy-start(s32[512]{0:T(512)} %place_ref.3) | copy-start | bytes 6148
  4.2 32.2 %copy-start.2 = (s32[512]{0:T(512)S(1)}, s32[512]{0:T(512)}, u32[]{:S(2)}) copy-start(s32[512]{0:T(512)} %place_ref.2) | copy-start | bytes 6148
  4.2 32.2 %all-to-all-start = ((bf16[8,512,256]{2,1,0:T(8,128)(2,1)}), bf16[8,512,256]{2,1,0:T(8,128)(2,1)S(1)}, u32[]{:S(2)}, u32[]{:S(2)}) async-start(bf16[8,512,256]{2,1,0:T(8,128)(2,1)} %broadcast_in_dim.6), calls=%async_computation | async-start | bytes 4194304 | tf_op jit(solution)/shard_map/all_to_all | solution.py:119
  54.5 4.4 %collective-permute-start = (bf16[8,512,256]{2,1,0:T(8,128)(2,1)}, bf16[8,512,256]{2,1,0:T(8,128)(2,1)S(1)}, u32[]{:S(2)}, u32[]{:S(2)}) collective-permute-start(bf16[8,512,256]{2,1,0:T(8,128)(2,1)} %dynamic-slice_bitcast_fusion), channel_id=1, source_target_pairs={{0,1},{1,0},{2,3},{3,2},{4,5},{5,4},{6,7},{7,6},{8,9},{9,8},{10,11... | collective-permute-start | bytes 6291464 | tf_op jit(solution)/shard_map/ppermute | solution.py:149
  96.6 1.0 copy-start.4
  128.6 6.2 %collective-permute-start.1 = (bf16[4096,256]{1,0:T(8,128)(2,1)S(1)}, bf16[4096,256]{1,0:T(8,128)(2,1)S(1)}, u32[]{:S(2)}, u32[]{:S(2)}) collective-permute-start(bf16[4096,256]{1,0:T(8,128)(2,1)S(1)} %bitcast.24), channel_id=1, source_target_pairs={{0,1},{1,0},{2,3},{3,2},{4,5},{5,4},{6,7},{7,6},{8,9},{9,8},{10,11... | collective-permute-start | bytes 6291464 | tf_op jit(solution)/shard_map/ppermute | solution.py:155
  183.4 23.6 %copy-start.3 = (bf16[256,256]{1,0:T(8,128)(2,1)S(1)}, bf16[256,256]{1,0:T(8,128)(2,1)}, u32[]{:S(2)}) copy-start(bf16[256,256]{1,0:T(8,128)(2,1)} %param.8) | copy-start | bytes 393220
  202.7 15.5 %all-to-all-start.5 = ((f32[128,2,256]{2,1,0:T(2,128)}), f32[128,2,256]{2,1,0:T(2,128)S(1)}, u32[]{:S(2)}, u32[]{:S(2)}) async-start(f32[128,2,256]{2,1,0:T(2,128)} %broadcast_in_dim.8), calls=%async_computation.5 | async-start | bytes 524288 | tf_op jit(solution)/shard_map/all_to_all | solution.py:119

commit v8 on v7

--- a/solution.py
+++ b/solution.py
@@ -112,6 +112,69 @@
             transcendentals=0,
         ),
     )(count, place_index, fetch_index, tile_values, source)
+
+
+MESH = pl.DeviceIdType.MESH
+AXES = ("row", "colhi", "core")
+
+
+def exchange_kernel(src_ref, dst_ref, send_sem, recv_sem, local_sem, *, axis, parts, gather):
+    me = lax.axis_index(axis)
+
+    def device(peer):
+        return tuple(peer if name == axis else lax.axis_index(name) for name in AXES)
+
+    barrier = pltpu.get_barrier_semaphore()
+    for k in range(1, parts):
+        peer = lax.rem(me + k, parts)
+        pl.semaphore_signal(barrier, inc=1, device_id=device(peer), device_id_type=MESH)
+    pl.semaphore_wait(barrier, parts - 1)
+
+    local = pltpu.make_async_copy(src_ref if gather else src_ref.at[me], dst_ref.at[me], local_sem)
+    local.start()
+    sends = []
+    for k in range(1, parts):
+        peer = lax.rem(me + k, parts)
+        copy = pltpu.make_async_remote_copy(
+            src_ref=src_ref if gather else src_ref.at[peer],
+            dst_ref=dst_ref.at[me],
+            send_sem=send_sem.at[k],
+            recv_sem=recv_sem.at[k],
+            device_id=device(peer),
+            device_id_type=MESH,
+        )
+        copy.start()
+        sends.append(copy)
+    for k in range(1, parts):
+        source = lax.rem(me + parts - k, parts)
+        incoming = pltpu.make_async_remote_copy(
+            src_ref=src_ref if gather else src_ref.at[source],
+            dst_ref=dst_ref.at[source],
+            send_sem=send_sem.at[k],
+            recv_sem=recv_sem.at[k],
+            device_id=device(source),
+            device_id_type=MESH,
+        )
+        incoming.wait_recv()
+    for copy in sends:
+        copy.wait_send()
+    local.wait()
+
+
+def exchange(values, axis, parts, gather, tag):
+    block = values.shape if gather else values.shape[1:]
+    return pl.pallas_call(
+        functools.partial(exchange_kernel, axis=axis, parts=parts, gather=gather),
+        out_shape=jax.ShapeDtypeStruct((parts,) + block, values.dtype),
+        in_specs=[pl.BlockSpec(memory_space=pl.ANY)],
+        out_specs=pl.BlockSpec(memory_space=pl.ANY),
+        scratch_shapes=[
+            pltpu.SemaphoreType.DMA((parts,)),
+            pltpu.SemaphoreType.DMA((parts,)),
+            pltpu.SemaphoreType.DMA,
+        ],
+        compiler_params=pltpu.CompilerParams(collective_id=tag, has_side_effects=True),
+    )(values)
 
 
 def gather_rows(values, axes, parts):
@@ -148,10 +211,12 @@
     give = lax.dynamic_index_in_dim(by_core, 1 - core, 1, keepdims=False)
     got = lax.ppermute(give, "core", swap)
     chip_sum = (keep.astype(jnp.float32) + got.astype(jnp.float32)).astype(jnp.bfloat16)
-    summed = scatter_sum(chip_sum, "colhi", pair_count)
+    summed = exchange(
+        chip_sum.reshape(pair_count, node_dev, hidden), "colhi", pair_count, False, 0
+    ).astype(jnp.float32).sum(0)
     activated = jax.nn.silu(summed).astype(jnp.bfloat16)
     slope = (cotangent.astype(jnp.float32) * silu_slope(summed)).astype(jnp.bfloat16)
-    slope_pairs = gather_rows(slope, "colhi", pair_count)
+    slope_pairs = exchange(slope, "colhi", pair_count, True, 1).reshape(-1, hidden)
     slope_full = jnp.concatenate([slope_pairs, lax.ppermute(slope_pairs, "core", swap)], axis=0)
     owner = tile_row // per_dev
     slope_index = (

time: 220 us -> 221 us (level)
  blocking collectives: 115 us -> 49.8 us
  Pallas kernels: 29.2 us -> 93.3 us
  other arithmetic: 6.16 us -> 10.8 us
    pallas_call x0 -> x2, Pallas kernels: none -> 62.4 us  [exchange(): pl.pallas_call(functools.partial(exchange_kernel, axis=axis, parts=parts,...]
    all_to_all x3 -> x2, blocking collectives: 85.4 us -> 49.8 us  [scatter_sum(): lax.all_to_all(values.reshape(parts, -1, values.shape[-1]), axes, 0, 0, t...]
    all_to_all x1 -> x0, blocking collectives: 29.9 us -> none  [gather_rows(): lax.all_to_all(copies, axes, 0, 0, tiled=True).reshape(-1, values.shape[-1])]
where the time goes in v8:
time: 221 us; the launch traced here: 220 us
  Pallas kernels  93.3 us (42%)
  blocking collectives  49.8 us (23%)
  waiting for transfers between devices  44.1 us (20%)
  starting transfers between devices  10.9 us (5%)
  other arithmetic  10.8 us (5%)
  local copies, waits for them, and re-layouts  7.28 us (3%)
  matrix products  2.37 us (1%)
    pallas_call x2, Pallas kernels, exchange(): pl.pallas_call(functools.partial(exchange_kernel, axis=axis, parts=parts,...  62.4 us
    all_to_all x2, blocking collectives, scatter_sum(): lax.all_to_all(values.reshape(parts, -1, values.shape[-1]), axes, 0, 0, t...  49.8 us
    all_to_all x2, waiting for transfers between devices, gather_rows(): lax.all_to_all(copies, axes, 0, 0, tiled=True).reshape(-1, values.shape[-1])  35.7 us
    pallas_call x2, Pallas kernels, tile_products(): pl.pallas_call(functools.partial(tile_kernel, forward=forward), grid_spec...  31 us
    all_to_all x2, starting transfers between devices, gather_rows(): lax.all_to_all(copies, axes, 0, 0, tiled=True).reshape(-1, values.shape[-1])  10.3 us
  transfers between devices with their start and end apart: 4, of which 4 were waited for; matrix products, arithmetic and copies ran while one was open for 0% of the time, Pallas kernels for 0%

profile of v8, /device:TPU:1, one launch (start us, length us, event | category | flops | bytes accessed | tf_op | source)
XLA Modules:
  0.0 219.9 jit_solution(3496189324745891183)
XLA Ops:
  0.6 0.0 copy-start
  0.6 0.9 copy-done
  1.6 1.1 convolution_convert_fusion.1
  2.7 1.5 broadcast_in_dim.4
  4.2 0.0 copy-start.1
  4.2 0.0 copy-start.2
  4.2 6.1 %all-to-all-start = ((bf16[8,512,256]{2,1,0:T(8,128)(2,1)}), bf16[8,512,256]{2,1,0:T(8,128)(2,1)S(1)}, u32[]{:S(2)}, u32[]{:S(2)}) async-start(bf16[8,512,256]{2,1,0:T(8,128)(2,1)} %broadcast_in_dim.4), calls=%async_computation | async-start | bytes 4194304 | tf_op jit(solution)/shard_map/all_to_all | solution.py:182
  10.9 25.5 %all-to-all-done = bf16[8,512,256]{2,1,0:T(8,128)(2,1)S(1)} async-done(((bf16[8,512,256]{2,1,0:T(8,128)(2,1)}), bf16[8,512,256]{2,1,0:T(8,128)(2,1)S(1)}, u32[]{:S(2)}, u32[]{:S(2)}) %all-to-all-start) | async-done | bytes 2097184 | tf_op jit(solution)/shard_map/all_to_all | solution.py:182
  36.4 0.0 copy-done.1
  36.4 0.0 copy-done.2
  36.4 15.9 %shard_map.94 = bf16[8192,256]{1,0:T(8,128)(2,1)} custom-call(s32[1]{0:T(128)} %bitcast.20.count_ref, s32[512]{0:T(512)S(1)} %copy-done.2, s32[512]{0:T(512)S(1)} %copy-done.1, bf16[512,128,128]{2,1,0:T(8,128)(2,1)} %tiles_ref.3, bf16[4096,256]{1,0:T(8,128)(2,1)S(1)} %bitcast.22), custom_call_target="tpu_custom_call" | custom-call | flops 4294967296 | bytes 23068672 | tf_op jit(solution)/shard_map/pallas_call | solution.py:102
  52.4 3.0 %dynamic-slice_bitcast_fusion = bf16[8,512,256]{2,1,0:T(8,128)(2,1)} fusion(bf16[8,2,512,256]{3,2,1,0:T(8,128)(2,1)} %bitcast.24, s32[]{:T(128)S(6)} %select_n.27), kind=kLoop, calls=%fused_computation.4 | loop fusion | bytes 4194308 | tf_op jit(solution)/shard_map/jit(dynamic_index_in_dim)/squeeze | solution.py:211
  55.4 0.0 collective-permute-start
  55.4 4.4 %collective-permute-done = bf16[8,512,256]{2,1,0:T(8,128)(2,1)S(1)} collective-permute-done((bf16[8,512,256]{2,1,0:T(8,128)(2,1)}, bf16[8,512,256]{2,1,0:T(8,128)(2,1)S(1)}, u32[]{:S(2)}, u32[]{:S(2)}) %collective-permute-start) | collective-permute-done | bytes 2097184 | tf_op jit(solution)/shard_map/ppermute | solution.py:212
  59.8 3.5 %fusion.src_ref = bf16[8,512,256]{2,1,0:T(8,128)(2,1)} fusion(bf16[8,512,256]{2,1,0:T(8,128)(2,1)S(1)} %collective-permute-done, bf16[8,2,512,256]{3,2,1,0:T(8,128)(2,1)} %bitcast.25, s32[]{:T(128)S(6)} %select_n.26), kind=kLoop, calls=%fused_computation.2 | loop fusion | flops 4194304 | bytes 6291460 | tf_op jit(solution)/shard_map/convert_element_type | solution.py:213
  63.2 32.6 %shard_map.95 = bf16[8,512,256]{2,1,0:T(8,128)(2,1)} custom-call(bf16[8,512,256]{2,1,0:T(8,128)(2,1)} %fusion.src_ref), custom_call_target="tpu_custom_call" | custom-call | tf_op jit(solution)/shard_map/pallas_call | solution.py:166
  95.8 0.0 copy-start.4
  95.8 2.0 convert_reduce_fusion
  97.8 0.0 copy-done.4
  97.8 1.0 multiply_convert_fusion
  98.8 29.8 %shard_map.96 = bf16[8,512,256]{2,1,0:T(8,128)(2,1)} custom-call(bf16[512,256]{1,0:T(8,128)(2,1)} %get-tuple-element.3.src_ref), custom_call_target="tpu_custom_call" | custom-call | tf_op jit(solution)/shard_map/pallas_call | solution.py:166
  128.6 0.6 collective-permute-start.1
  129.2 4.0 %collective-permute-done.1 = bf16[4096,256]{1,0:T(8,128)(2,1)S(1)} collective-permute-done((bf16[4096,256]{1,0:T(8,128)(2,1)}, bf16[4096,256]{1,0:T(8,128)(2,1)S(1)}, u32[]{:S(2)}, u32[]{:S(2)}) %collective-permute-start.1) | collective-permute-done | bytes 2097184 | tf_op jit(solution)/shard_map/ppermute | solution.py:220
  133.2 3.8 %pad_maximum_fusion.src_ref = bf16[8192,256]{1,0:T(8,128)(2,1)} fusion(bf16[4096,256]{1,0:T(8,128)(2,1)S(1)} %collective-permute-done.1, bf16[4096,256]{1,0:T(8,128)(2,1)} %bitcast.27), kind=kLoop, calls=%fused_computation | loop fusion | flops 8388608 | bytes 8388608 | tf_op jit(solution)/shard_map/concatenate | solution.py:220
  137.0 15.0 %shard_map.97 = bf16[4096,256]{1,0:T(8,128)(2,1)S(1)} custom-call(s32[1]{0:T(128)} %bitcast.21.count_ref, s32[512]{0:T(512)S(1)} %copy-done.1, s32[512]{0:T(512)S(1)} %fusion.4.fetch_ref, bf16[512,128,128]{2,1,0:T(8,128)(2,1)} %tiles_ref.3, bf16[8192,256]{1,0:T(8,128)(2,1)} %pad_maximum_fusion.src_ref), custom_call_target="tpu_custom_call" | custom-call | flops 4294967296 | bytes 23068672 | tf_op jit(solution)/shard_map/pallas_call | solution.py:102
  152.0 30.7 %all_to_all.20 = bf16[8,512,256]{2,1,0:T(8,128)(2,1)S(1)} all-to-all(bf16[8,512,256]{2,1,0:T(8,128)(2,1)S(1)} %bitcast.23), channel_id=1, replica_groups=mesh['row'=8,'colhi'=8,'core'=2] {'row'}, dimensions={0} | all-to-all | bytes 4194304 | tf_op jit(solution)/shard_map/all_to_all | solution.py:186
  182.7 0.0 copy-start.3
  182.7 0.4 reduce_sum.31
  183.1 0.3 convolution_bitcast_fusion
  183.4 0.1 reshape.36
  183.5 19.1 %all_to_all.21 = f32[128,2,256]{2,1,0:T(2,128)S(1)} all-to-all(f32[128,2,256]{2,1,0:T(2,128)S(1)} %reshape.36), channel_id=1, replica_groups=mesh['row'=8,'colhi'=8,'core'=2] {'row','colhi','core'}, dimensions={0} | all-to-all | bytes 524288 | tf_op jit(solution)/shard_map/all_to_all | solution.py:186
  202.6 0.1 reduce_sum.32
  202.8 0.8 broadcast_in_dim.5
  203.6 4.2 %all-to-all-start.3 = ((f32[128,2,256]{2,1,0:T(2,128)}), f32[128,2,256]{2,1,0:T(2,128)S(1)}, u32[]{:S(2)}, u32[]{:S(2)}) async-start(f32[128,2,256]{2,1,0:T(2,128)} %broadcast_in_dim.5), calls=%async_computation.3 | async-start | bytes 524288 | tf_op jit(solution)/shard_map/all_to_all | solution.py:182
  207.8 0.0 copy-done.3
  207.8 1.0 convolution_convert_fusion
  208.8 10.2 %all-to-all-done.3 = f32[128,2,256]{2,1,0:T(2,128)S(1)} async-done(((f32[128,2,256]{2,1,0:T(2,128)}), f32[128,2,256]{2,1,0:T(2,128)S(1)}, u32[]{:S(2)}, u32[]{:S(2)}) %all-to-all-start.3) | async-done | bytes 262176 | tf_op jit(solution)/shard_map/all_to_all | solution.py:182
  219.0 0.9 reshape.37
  (1 shorter events, 0.0 us)
Async XLA Ops:
  0.6 1.0 copy-start
  4.2 32.2 %copy-start.1 = (s32[512]{0:T(512)S(1)}, s32[512]{0:T(512)}, u32[]{:S(2)}) copy-start(s32[512]{0:T(512)} %place_ref.3) | copy-start | bytes 6148
  4.2 32.2 %copy-start.2 = (s32[512]{0:T(512)S(1)}, s32[512]{0:T(512)}, u32[]{:S(2)}) copy-start(s32[512]{0:T(512)} %place_ref.2) | copy-start | bytes 6148
  4.2 32.2 %all-to-all-start = ((bf16[8,512,256]{2,1,0:T(8,128)(2,1)}), bf16[8,512,256]{2,1,0:T(8,128)(2,1)S(1)}, u32[]{:S(2)}, u32[]{:S(2)}) async-start(bf16[8,512,256]{2,1,0:T(8,128)(2,1)} %broadcast_in_dim.4), calls=%async_computation | async-start | bytes 4194304 | tf_op jit(solution)/shard_map/all_to_all | solution.py:182
  55.4 4.4 %collective-permute-start = (bf16[8,512,256]{2,1,0:T(8,128)(2,1)}, bf16[8,512,256]{2,1,0:T(8,128)(2,1)S(1)}, u32[]{:S(2)}, u32[]{:S(2)}) collective-permute-start(bf16[8,512,256]{2,1,0:T(8,128)(2,1)} %dynamic-slice_bitcast_fusion), channel_id=1, source_target_pairs={{0,1},{1,0},{2,3},{3,2},{4,5},{5,4},{6,7},{7,6},{8,9},{9,8},{10,11... | collective-permute-start | bytes 6291464 | tf_op jit(solution)/shard_map/ppermute | solution.py:212
  95.8 2.0 copy-start.4
  128.6 4.6 %collective-permute-start.1 = (bf16[4096,256]{1,0:T(8,128)(2,1)}, bf16[4096,256]{1,0:T(8,128)(2,1)S(1)}, u32[]{:S(2)}, u32[]{:S(2)}) collective-permute-start(bf16[4096,256]{1,0:T(8,128)(2,1)} %bitcast.26), channel_id=1, source_target_pairs={{0,1},{1,0},{2,3},{3,2},{4,5},{5,4},{6,7},{7,6},{8,9},{9,8},{10,11... | collective-permute-start | bytes 6291464 | tf_op jit(solution)/shard_map/ppermute | solution.py:220
  182.7 25.1 %copy-start.3 = (bf16[256,256]{1,0:T(8,128)(2,1)S(1)}, bf16[256,256]{1,0:T(8,128)(2,1)}, u32[]{:S(2)}) copy-start(bf16[256,256]{1,0:T(8,128)(2,1)} %param.8) | copy-start | bytes 393220
  203.6 15.5 %all-to-all-start.3 = ((f32[128,2,256]{2,1,0:T(2,128)}), f32[128,2,256]{2,1,0:T(2,128)S(1)}, u32[]{:S(2)}, u32[]{:S(2)}) async-start(f32[128,2,256]{2,1,0:T(2,128)} %broadcast_in_dim.5), calls=%async_computation.3 | async-start | bytes 524288 | tf_op jit(solution)/shard_map/all_to_all | solution.py:182

commit v9 on v7

--- a/solution.py
+++ b/solution.py
@@ -10,7 +10,7 @@
 
 GROUP = 64
 CHUNK = 256
-UNROLL = (32, 8, 1)
+UNROLL = (64, 8, 1)
 
 
 def silu_slope(values):
@@ -18,7 +18,11 @@
     return sigma * (1.0 + values * (1.0 - sigma))
 
 
-def tile_kernel(count_ref, place_ref, fetch_ref, tiles_ref, src_ref, out_ref, acc_ref, *, forward):
+def tile_kernel(count_ref, place_ref, fetch_ref, tiles_ref, src_ref, *refs, forward, block_rows):
+    if block_rows:
+        keep_ref, give_ref, acc_ref = refs
+    else:
+        out_ref, acc_ref = refs
     step = pl.program_id(0)
     tile = tiles_ref.shape[1]
     group = tiles_ref.shape[0]
@@ -70,13 +74,29 @@
     def _():
         def emit(k, carry):
             rows = pl.ds(pl.multiple_of(k * CHUNK, CHUNK), CHUNK)
-            out_ref[rows, :] = acc_ref[rows, :].astype(out_ref.dtype)
+            if not block_rows:
+                out_ref[rows, :] = acc_ref[rows, :].astype(out_ref.dtype)
+                return carry
+            values = acc_ref[rows, :].astype(keep_ref.dtype)
+            block = k * CHUNK // block_rows
+            dst = pl.ds(
+                pl.multiple_of((block // 2) * block_rows + k * CHUNK % block_rows, CHUNK), CHUNK
+            )
+
+            @pl.when(block % 2 == count_ref[1])
+            def _():
+                keep_ref[dst, :] = values
+
+            @pl.when(block % 2 != count_ref[1])
+            def _():
+                give_ref[dst, :] = values
+
             return carry
 
         lax.fori_loop(0, out_rows // CHUNK, emit, 0)
 
 
-def tile_products(tile_values, fetch_index, place_index, count, source, out_tiles, forward):
+def tile_products(tile_values, fetch_index, place_index, count, source, out_tiles, forward, block_rows=0):
     slots, tile, _ = tile_values.shape
     hidden = source.shape[-1]
     src_rows = source.shape[0]
@@ -95,14 +115,18 @@
             pl.BlockSpec((group, tile, tile), tiles_map),
             pl.BlockSpec((src_rows, hidden), lambda i, *_: (0, 0)),
         ],
-        out_specs=pl.BlockSpec((out_rows, hidden), lambda i, *_: (0, 0)),
+        out_specs=[pl.BlockSpec((out_rows // 2, hidden), lambda i, *_: (0, 0))] * 2
+        if block_rows
+        else pl.BlockSpec((out_rows, hidden), lambda i, *_: (0, 0)),
         scratch_shapes=[pltpu.VMEM((out_rows, hidden), jnp.float32)],
     )
     flops = 2 * slots * tile * tile * hidden
     return pl.pallas_call(
-        functools.partial(tile_kernel, forward=forward),
+        functools.partial(tile_kernel, forward=forward, block_rows=block_rows),
         grid_spec=grid_spec,
-        out_shape=jax.ShapeDtypeStruct((out_rows, hidden), jnp.bfloat16),
+        out_shape=[jax.ShapeDtypeStruct((out_rows // 2, hidden), jnp.bfloat16)] * 2
+        if block_rows
+        else jax.ShapeDtypeStruct((out_rows, hidden), jnp.bfloat16),
         compiler_params=pltpu.CompilerParams(
             dimension_semantics=("arbitrary",), vmem_limit_bytes=48 * 1024 * 1024
         ),
@@ -135,19 +159,17 @@
     per_dev = node_dev // tile_size
     row_tiles = node_dev * col_count // tile_size
     col_tiles = node_dev * row_count // tile_size
-    count = tile_count.reshape(1)
+    core = lax.axis_index("core")
+    count = jnp.stack([tile_count.reshape(()), core.astype(jnp.int32)])
     projected = jnp.dot(features, weight, preferred_element_type=jnp.float32).astype(jnp.bfloat16)
     panel_rows = gather_rows(projected, "row", row_count)
-    forward_part = tile_products(
-        tile_values, tile_col, tile_row, count, panel_rows, row_tiles, True
-    )
-    core = lax.axis_index("core")
     swap = [(0, 1), (1, 0)]
-    by_core = forward_part.reshape(pair_count, core_count, node_dev, hidden)
-    keep = lax.dynamic_index_in_dim(by_core, core, 1, keepdims=False)
-    give = lax.dynamic_index_in_dim(by_core, 1 - core, 1, keepdims=False)
+    keep, give = tile_products(
+        tile_values, tile_col, tile_row, count, panel_rows, row_tiles, True, node_dev
+    )
     got = lax.ppermute(give, "core", swap)
     chip_sum = (keep.astype(jnp.float32) + got.astype(jnp.float32)).astype(jnp.bfloat16)
+    chip_sum = chip_sum.reshape(pair_count, node_dev, hidden)
     summed = scatter_sum(chip_sum, "colhi", pair_count)
     activated = jax.nn.silu(summed).astype(jnp.bfloat16)
     slope = (cotangent.astype(jnp.float32) * silu_slope(summed)).astype(jnp.bfloat16)

time: 220 us -> 214 us (0.973)
  blocking collectives: 115 us -> 106 us
  Pallas kernels: 29.2 us -> 35.7 us
    all_to_all x3, blocking collectives: 85.4 us -> 77.1 us  [scatter_sum(): lax.all_to_all(values.reshape(parts, -1, values.shape[-1]), axes, 0, 0, t...]
    pallas_call x2, Pallas kernels: 29.2 us -> 35.7 us  [tile_products(): pl.pallas_call(functools.partial(tile_kernel, forward=forward, block_rows...]
    squeeze x1 -> x0, local copies, waits for them, and re-layouts: 3.04 us -> none  [body(): give = lax.dynamic_index_in_dim(by_core, 1 - core, 1, keepdims=False)]
  transfers between devices with their start and end apart: 4 -> 4, of which waited for: 4 -> 4; matrix products, arithmetic and copies ran while one was open for 0% -> 1% of each run, Pallas kernels for 0% -> 0%
where the time goes in v9:
time: 214 us; the launch traced here: 213 us
  blocking collectives  106 us (50%)
  waiting for transfers between devices  43.6 us (20%)
  Pallas kernels  35.7 us (17%)
  starting transfers between devices  12.8 us (6%)
  local copies, waits for them, and re-layouts  6.37 us (3%)
  other arithmetic  4.74 us (2%)
  matrix products  2.37 us (1%)
    all_to_all x3, blocking collectives, scatter_sum(): lax.all_to_all(values.reshape(parts, -1, values.shape[-1]), axes, 0, 0, t...  77.1 us
    pallas_call x2, Pallas kernels, tile_products(): pl.pallas_call(functools.partial(tile_kernel, forward=forward, block_rows...  35.7 us
    all_to_all x2, waiting for transfers between devices, gather_rows(): lax.all_to_all(copies, axes, 0, 0, tiled=True).reshape(-1, values.shape[-1])  35.7 us
    all_to_all x1, blocking collectives, gather_rows(): lax.all_to_all(copies, axes, 0, 0, tiled=True).reshape(-1, values.shape[-1])  29.4 us
    all_to_all x2, starting transfers between devices, gather_rows(): lax.all_to_all(copies, axes, 0, 0, tiled=True).reshape(-1, values.shape[-1])  10.3 us
  transfers between devices with their start and end apart: 4, of which 4 were waited for; matrix products, arithmetic and copies ran while one was open for 1% of the time, Pallas kernels for 0%

profile of v9, /device:TPU:1, one launch (start us, length us, event | category | flops | bytes accessed | tf_op | source)
XLA Modules:
  0.0 213.4 jit_solution(789732931273420495)
XLA Ops:
  0.6 0.0 copy-start
  0.6 0.9 copy-done
  1.6 1.1 convolution_convert_fusion.1
  2.7 1.5 broadcast_in_dim.6
  4.2 0.0 copy-start.1
  4.2 0.0 copy-start.2
  4.2 6.1 %all-to-all-start = ((bf16[8,512,256]{2,1,0:T(8,128)(2,1)}), bf16[8,512,256]{2,1,0:T(8,128)(2,1)S(1)}, u32[]{:S(2)}, u32[]{:S(2)}) async-start(bf16[8,512,256]{2,1,0:T(8,128)(2,1)} %broadcast_in_dim.6), calls=%async_computation | async-start | bytes 4194304 | tf_op jit(solution)/shard_map/all_to_all | solution.py:143
  10.9 0.1 pad_add_fusion.count_ref
  11.0 25.4 %all-to-all-done = bf16[8,512,256]{2,1,0:T(8,128)(2,1)S(1)} async-done(((bf16[8,512,256]{2,1,0:T(8,128)(2,1)}), bf16[8,512,256]{2,1,0:T(8,128)(2,1)S(1)}, u32[]{:S(2)}, u32[]{:S(2)}) %all-to-all-start) | async-done | bytes 2097184 | tf_op jit(solution)/shard_map/all_to_all | solution.py:143
  36.4 0.0 copy-start.3
  36.4 1.3 copy-done.3
  37.8 0.0 copy-done.1
  37.8 0.0 copy-done.2
  37.8 17.8 %shard_map.94 = (bf16[4096,256]{1,0:T(8,128)(2,1)S(1)}, bf16[4096,256]{1,0:T(8,128)(2,1)S(1)}) custom-call(s32[2]{0:T(128)S(1)} %pad_add_fusion.count_ref, s32[512]{0:T(512)S(1)} %copy-done.2, s32[512]{0:T(512)S(1)} %copy-done.1, bf16[512,128,128]{2,1,0:T(8,128)(2,1)} %tiles_ref.3, bf16[4096,256]{1,0:T(8,128)(2,1)} %bitcast.16), custom_call_target="tpu_custom_call" | custom-call | flops 4294967296 | bytes 23068672 | tf_op jit(solution)/shard_map/pallas_call | solution.py:124
  55.6 0.1 collective-permute-start
  55.7 4.1 %collective-permute-done = bf16[4096,256]{1,0:T(8,128)(2,1)S(1)} collective-permute-done((bf16[4096,256]{1,0:T(8,128)(2,1)S(1)}, bf16[4096,256]{1,0:T(8,128)(2,1)S(1)}, u32[]{:S(2)}, u32[]{:S(2)}) %collective-permute-start) | collective-permute-done | bytes 2097184 | tf_op jit(solution)/shard_map/ppermute | solution.py:170
  59.8 0.7 add_convert_fusion
  60.5 32.7 %all_to_all.30 = bf16[8,512,256]{2,1,0:T(8,128)(2,1)S(1)} all-to-all(bf16[8,512,256]{2,1,0:T(8,128)(2,1)S(1)} %bitcast.17), channel_id=1, replica_groups=mesh['row'=8,'colhi'=8,'core'=2] {'colhi'}, dimensions={0} | all-to-all | bytes 4194304 | tf_op jit(solution)/shard_map/all_to_all | solution.py:147
  93.2 0.0 copy-start.5
  93.2 0.3 convert_reduce_fusion
  93.5 0.7 copy-done.5
  94.2 0.9 multiply_convert_fusion
  95.1 0.1 broadcast_in_dim.7
  95.3 29.4 %all_to_all.31 = bf16[8,512,256]{2,1,0:T(8,128)(2,1)S(1)} all-to-all(bf16[8,512,256]{2,1,0:T(8,128)(2,1)S(1)} %broadcast_in_dim.7), channel_id=1, replica_groups=mesh['row'=8,'colhi'=8,'core'=2] {'colhi'}, dimensions={0} | all-to-all | bytes 4194304 | tf_op jit(solution)/shard_map/all_to_all | solution.py:143
  124.7 2.4 %collective-permute-start.1 = (bf16[4096,256]{1,0:T(8,128)(2,1)S(1)}, bf16[4096,256]{1,0:T(8,128)(2,1)S(1)}, u32[]{:S(2)}, u32[]{:S(2)}) collective-permute-start(bf16[4096,256]{1,0:T(8,128)(2,1)S(1)} %bitcast.18), channel_id=1, source_target_pairs={{0,1},{1,0},{2,3},{3,2},{4,5},{5,4},{6,7},{7,6},{8,9},{9,8},{10,11... | collective-permute-start | bytes 6291464 | tf_op jit(solution)/shard_map/ppermute | solution.py:177
  127.1 3.8 %collective-permute-done.1 = bf16[4096,256]{1,0:T(8,128)(2,1)S(1)} collective-permute-done((bf16[4096,256]{1,0:T(8,128)(2,1)S(1)}, bf16[4096,256]{1,0:T(8,128)(2,1)S(1)}, u32[]{:S(2)}, u32[]{:S(2)}) %collective-permute-start.1) | collective-permute-done | bytes 2097184 | tf_op jit(solution)/shard_map/ppermute | solution.py:177
  130.9 2.2 %pad_maximum_fusion.src_ref = bf16[8192,256]{1,0:T(8,128)(2,1)} fusion(bf16[4096,256]{1,0:T(8,128)(2,1)S(1)} %collective-permute-done.1, bf16[4096,256]{1,0:T(8,128)(2,1)S(1)} %bitcast.19), kind=kLoop, calls=%fused_computation | loop fusion | flops 8388608 | bytes 8388608 | tf_op jit(solution)/shard_map/concatenate | solution.py:177
  133.1 17.9 %shard_map.95 = bf16[4096,256]{1,0:T(8,128)(2,1)S(1)} custom-call(s32[2]{0:T(128)S(1)} %pad_add_fusion.count_ref, s32[512]{0:T(512)S(1)} %copy-done.1, s32[512]{0:T(512)S(1)} %fusion.3.fetch_ref, bf16[512,128,128]{2,1,0:T(8,128)(2,1)} %tiles_ref.3, bf16[8192,256]{1,0:T(8,128)(2,1)} %pad_maximum_fusion.src_ref), custom_call_target="tpu_custom_call" | custom-call | flops 4294967296 | bytes 23068672 | tf_op jit(solution)/shard_map/pallas_call | solution.py:124
  151.0 28.0 %all_to_all.32 = bf16[8,512,256]{2,1,0:T(8,128)(2,1)S(1)} all-to-all(bf16[8,512,256]{2,1,0:T(8,128)(2,1)S(1)} %bitcast.15), channel_id=1, replica_groups=mesh['row'=8,'colhi'=8,'core'=2] {'row'}, dimensions={0} | all-to-all | bytes 4194304 | tf_op jit(solution)/shard_map/all_to_all | solution.py:147
  179.0 0.0 copy-start.4
  179.0 0.4 reduce_sum.31
  179.4 0.3 convolution_bitcast_fusion
  179.7 0.1 reshape.31
  179.8 16.3 %all_to_all.33 = f32[128,2,256]{2,1,0:T(2,128)S(1)} all-to-all(f32[128,2,256]{2,1,0:T(2,128)S(1)} %reshape.31), channel_id=1, replica_groups=mesh['row'=8,'colhi'=8,'core'=2] {'row','colhi','core'}, dimensions={0} | all-to-all | bytes 524288 | tf_op jit(solution)/shard_map/all_to_all | solution.py:147
  196.2 0.1 reduce_sum.32
  196.3 0.8 broadcast_in_dim.8
  197.1 4.2 %all-to-all-start.5 = ((f32[128,2,256]{2,1,0:T(2,128)}), f32[128,2,256]{2,1,0:T(2,128)S(1)}, u32[]{:S(2)}, u32[]{:S(2)}) async-start(f32[128,2,256]{2,1,0:T(2,128)} %broadcast_in_dim.8), calls=%async_computation.5 | async-start | bytes 524288 | tf_op jit(solution)/shard_map/all_to_all | solution.py:143
  201.3 0.0 copy-done.4
  201.3 1.0 convolution_convert_fusion
  202.3 10.2 %all-to-all-done.5 = f32[128,2,256]{2,1,0:T(2,128)S(1)} async-done(((f32[128,2,256]{2,1,0:T(2,128)}), f32[128,2,256]{2,1,0:T(2,128)S(1)}, u32[]{:S(2)}, u32[]{:S(2)}) %all-to-all-start.5) | async-done | bytes 262176 | tf_op jit(solution)/shard_map/all_to_all | solution.py:143
  212.5 0.9 reshape.32
  (1 shorter events, 0.0 us)
Async XLA Ops:
  0.6 1.0 copy-start
  4.2 33.6 %copy-start.1 = (s32[512]{0:T(512)S(1)}, s32[512]{0:T(512)}, u32[]{:S(2)}) copy-start(s32[512]{0:T(512)} %place_ref.3) | copy-start | bytes 6148
  4.2 33.6 %copy-start.2 = (s32[512]{0:T(512)S(1)}, s32[512]{0:T(512)}, u32[]{:S(2)}) copy-start(s32[512]{0:T(512)} %place_ref.2) | copy-start | bytes 6148
  4.2 32.2 %all-to-all-start = ((bf16[8,512,256]{2,1,0:T(8,128)(2,1)}), bf16[8,512,256]{2,1,0:T(8,128)(2,1)S(1)}, u32[]{:S(2)}, u32[]{:S(2)}) async-start(bf16[8,512,256]{2,1,0:T(8,128)(2,1)} %broadcast_in_dim.6), calls=%async_computation | async-start | bytes 4194304 | tf_op jit(solution)/shard_map/all_to_all | solution.py:143
  36.4 1.3 copy-start.3
  55.6 4.2 %collective-permute-start = (bf16[4096,256]{1,0:T(8,128)(2,1)S(1)}, bf16[4096,256]{1,0:T(8,128)(2,1)S(1)}, u32[]{:S(2)}, u32[]{:S(2)}) collective-permute-start(bf16[4096,256]{1,0:T(8,128)(2,1)S(1)} %get-tuple-element.6), channel_id=1, source_target_pairs={{0,1},{1,0},{2,3},{3,2},{4,5},{5,4},{6,7},{7,6},{8,9},{9,8},{10,11... | collective-permute-start | bytes 6291464 | tf_op jit(solution)/shard_map/ppermute | solution.py:170
  93.2 1.0 copy-start.5
  124.7 6.2 %collective-permute-start.1 = (bf16[4096,256]{1,0:T(8,128)(2,1)S(1)}, bf16[4096,256]{1,0:T(8,128)(2,1)S(1)}, u32[]{:S(2)}, u32[]{:S(2)}) collective-permute-start(bf16[4096,256]{1,0:T(8,128)(2,1)S(1)} %bitcast.18), channel_id=1, source_target_pairs={{0,1},{1,0},{2,3},{3,2},{4,5},{5,4},{6,7},{7,6},{8,9},{9,8},{10,11... | collective-permute-start | bytes 6291464 | tf_op jit(solution)/shard_map/ppermute | solution.py:177
  179.0 22.3 %copy-start.4 = (bf16[256,256]{1,0:T(8,128)(2,1)S(1)}, bf16[256,256]{1,0:T(8,128)(2,1)}, u32[]{:S(2)}) copy-start(bf16[256,256]{1,0:T(8,128)(2,1)} %param.8) | copy-start | bytes 393220
  197.1 15.5 %all-to-all-start.5 = ((f32[128,2,256]{2,1,0:T(2,128)}), f32[128,2,256]{2,1,0:T(2,128)S(1)}, u32[]{:S(2)}, u32[]{:S(2)}) async-start(f32[128,2,256]{2,1,0:T(2,128)} %broadcast_in_dim.8), calls=%async_computation.5 | async-start | bytes 524288 | tf_op jit(solution)/shard_map/all_to_all | solution.py:143

commit v10 on v9

--- a/solution.py
+++ b/solution.py
@@ -161,8 +161,10 @@
     col_tiles = node_dev * row_count // tile_size
     core = lax.axis_index("core")
     count = jnp.stack([tile_count.reshape(()), core.astype(jnp.int32)])
-    projected = jnp.dot(features, weight, preferred_element_type=jnp.float32).astype(jnp.bfloat16)
-    panel_rows = gather_rows(projected, "row", row_count)
+    features_block = gather_rows(features, "row", row_count)
+    panel_rows = jnp.dot(features_block, weight, preferred_element_type=jnp.float32).astype(
+        jnp.bfloat16
+    )
     swap = [(0, 1), (1, 0)]
     keep, give = tile_products(
         tile_values, tile_col, tile_row, count, panel_rows, row_tiles, True, node_dev
@@ -184,17 +186,25 @@
     column_part = tile_products(
         tile_values, slope_index, tile_col, count, slope_full, col_tiles, False
     )
-    grad_nodes = scatter_sum(column_part, "row", row_count).astype(jnp.bfloat16)
+    weight_term = lax.dot_general(
+        features_block, column_part, (((0,), (0,)), ((), ())), preferred_element_type=jnp.float32
+    )
+    term_rows = hidden // row_count
+    packed = jnp.concatenate(
+        [
+            column_part.reshape(row_count, node_dev, hidden),
+            weight_term.astype(jnp.bfloat16).reshape(row_count, term_rows, hidden),
+        ],
+        axis=1,
+    )
+    reduced = scatter_sum(packed, "row", row_count)
+    grad_nodes = reduced[:node_dev].astype(jnp.bfloat16)
+    col_terms = gather_rows(reduced[node_dev:], ("colhi", "core"), col_count)
+    weight_rows = col_terms.reshape(col_count, term_rows, hidden).sum(0)
+    grad_weight = gather_rows(weight_rows, "row", row_count)
     grad_features = lax.dot_general(
         grad_nodes, weight, (((1,), (1,)), ((), ())), preferred_element_type=jnp.float32
     ).astype(jnp.bfloat16)
-    weight_term = lax.dot_general(
-        features, grad_nodes, (((0,), (0,)), ((), ())), preferred_element_type=jnp.float32
-    )
-    everyone = ("row", "colhi", "core")
-    devices = row_count * col_count
-    weight_piece = scatter_sum(weight_term, everyone, devices)
-    grad_weight = gather_rows(weight_piece, everyone, devices)
     return (activated, grad_features, grad_weight)
 
 

time: 214 us -> 211 us (0.986)
  blocking collectives: 106 us -> 129 us
  Pallas kernels: 35.7 us -> 14.8 us
  waiting for transfers between devices: 43.6 us -> 38.1 us
    pallas_call x2, Pallas kernels: 35.7 us -> 14.8 us  [tile_products(): pl.pallas_call(functools.partial(tile_kernel, forward=forward, block_rows...]
    all_to_all x1 -> x2, blocking collectives: 29.4 us -> 47.8 us  [gather_rows(): lax.all_to_all(copies, axes, 0, 0, tiled=True).reshape(-1, values.shape[-1])]
    all_to_all x2, waiting for transfers between devices: 35.7 us -> 30.5 us  [gather_rows(): lax.all_to_all(copies, axes, 0, 0, tiled=True).reshape(-1, values.shape[-1])]
    all_to_all x3 -> x2, blocking collectives: 77.1 us -> 81 us  [scatter_sum(): lax.all_to_all(values.reshape(parts, -1, values.shape[-1]), axes, 0, 0, t...]
where the time goes in v10:
time: 211 us; the launch traced here: 210 us
  blocking collectives  129 us (61%)
  waiting for transfers between devices  38.1 us (18%)
  Pallas kernels  14.8 us (7%)
  starting transfers between devices  13.3 us (6%)
  local copies, waits for them, and re-layouts  4.72 us (2%)
  other arithmetic  4.63 us (2%)
  matrix products  3.97 us (2%)
    all_to_all x2, blocking collectives, scatter_sum(): lax.all_to_all(values.reshape(parts, -1, values.shape[-1]), axes, 0, 0, t...  81 us
    all_to_all x2, blocking collectives, gather_rows(): lax.all_to_all(copies, axes, 0, 0, tiled=True).reshape(-1, values.shape[-1])  47.8 us
    all_to_all x2, waiting for transfers between devices, gather_rows(): lax.all_to_all(copies, axes, 0, 0, tiled=True).reshape(-1, values.shape[-1])  30.5 us
    pallas_call x2, Pallas kernels, tile_products(): pl.pallas_call(functools.partial(tile_kernel, forward=forward, block_rows...  14.8 us
    all_to_all x2, starting transfers between devices, gather_rows(): lax.all_to_all(copies, axes, 0, 0, tiled=True).reshape(-1, values.shape[-1])  9.36 us
  transfers between devices with their start and end apart: 4, of which 4 were waited for; matrix products, arithmetic and copies ran while one was open for 1% of the time, Pallas kernels for 0%

profile of v10, /device:TPU:1, one launch (start us, length us, event | category | flops | bytes accessed | tf_op | source)
XLA Modules:
  0.0 209.6 jit_solution(6442616687164678829)
XLA Ops:
  0.6 0.0 copy-start
  0.6 2.5 %broadcast_in_dim.8 = bf16[8,512,256]{2,1,0:T(8,128)(2,1)} broadcast(bf16[512,256]{1,0:T(8,128)(2,1)} %param.7), dimensions={1,2} | broadcast | bytes 2359296 | tf_op jit(solution)/shard_map/broadcast_in_dim | solution.py:142
  3.1 5.9 %all-to-all-start = ((bf16[8,512,256]{2,1,0:T(8,128)(2,1)}), bf16[8,512,256]{2,1,0:T(8,128)(2,1)S(1)}, u32[]{:S(2)}, u32[]{:S(2)}) async-start(bf16[8,512,256]{2,1,0:T(8,128)(2,1)} %broadcast_in_dim.8), calls=%async_computation | async-start | bytes 4194304 | tf_op jit(solution)/shard_map/all_to_all | solution.py:143
  9.7 0.1 pad_add_fusion.count_ref
  9.8 25.4 %all-to-all-done = bf16[8,512,256]{2,1,0:T(8,128)(2,1)S(1)} async-done(((bf16[8,512,256]{2,1,0:T(8,128)(2,1)}), bf16[8,512,256]{2,1,0:T(8,128)(2,1)S(1)}, u32[]{:S(2)}, u32[]{:S(2)}) %all-to-all-start) | async-done | bytes 2097184 | tf_op jit(solution)/shard_map/all_to_all | solution.py:143
  35.2 0.0 copy-done
  35.2 0.0 copy-start.1
  35.2 0.0 copy-start.2
  35.2 2.0 convolution_convert_fusion.src_ref
  37.2 0.0 copy-done.1
  37.2 0.0 copy-done.2
  37.2 7.7 %shard_map.94 = (bf16[4096,256]{1,0:T(8,128)(2,1)S(1)}, bf16[4096,256]{1,0:T(8,128)(2,1)S(1)}) custom-call(s32[2]{0:T(128)S(1)} %pad_add_fusion.count_ref, s32[512]{0:T(512)S(1)} %copy-done.2, s32[512]{0:T(512)S(1)} %copy-done.1, bf16[512,128,128]{2,1,0:T(8,128)(2,1)} %tiles_ref.3, bf16[4096,256]{1,0:T(8,128)(2,1)} %convolution_convert_fusion.src_ref), custom_call_target="tpu_custom_call" | custom-call | flops 4294967296 | bytes 23068672 | tf_op jit(solution)/shard_map/pallas_call | solution.py:124
  44.9 1.6 collective-permute-start
  46.5 3.8 %collective-permute-done = bf16[4096,256]{1,0:T(8,128)(2,1)S(1)} collective-permute-done((bf16[4096,256]{1,0:T(8,128)(2,1)S(1)}, bf16[4096,256]{1,0:T(8,128)(2,1)S(1)}, u32[]{:S(2)}, u32[]{:S(2)}) %collective-permute-start) | collective-permute-done | bytes 2097184 | tf_op jit(solution)/shard_map/ppermute | solution.py:172
  50.3 0.6 add_convert_fusion
  50.9 43.6 %all_to_all.30 = bf16[8,512,256]{2,1,0:T(8,128)(2,1)S(1)} all-to-all(bf16[8,512,256]{2,1,0:T(8,128)(2,1)S(1)} %bitcast.19), channel_id=1, replica_groups=mesh['row'=8,'colhi'=8,'core'=2] {'colhi'}, dimensions={0} | all-to-all | bytes 4194304 | tf_op jit(solution)/shard_map/all_to_all | solution.py:147
  94.5 0.0 copy-start.3
  94.5 0.3 convert_reduce_fusion.1
  94.8 0.6 copy-done.3
  95.4 0.9 multiply_convert_fusion
  96.4 0.1 broadcast_in_dim.9
  96.5 29.9 %all_to_all.31 = bf16[8,512,256]{2,1,0:T(8,128)(2,1)S(1)} all-to-all(bf16[8,512,256]{2,1,0:T(8,128)(2,1)S(1)} %broadcast_in_dim.9), channel_id=1, replica_groups=mesh['row'=8,'colhi'=8,'core'=2] {'colhi'}, dimensions={0} | all-to-all | bytes 4194304 | tf_op jit(solution)/shard_map/all_to_all | solution.py:143
  126.4 2.4 %collective-permute-start.1 = (bf16[4096,256]{1,0:T(8,128)(2,1)S(1)}, bf16[4096,256]{1,0:T(8,128)(2,1)S(1)}, u32[]{:S(2)}, u32[]{:S(2)}) collective-permute-start(bf16[4096,256]{1,0:T(8,128)(2,1)S(1)} %bitcast.20), channel_id=1, source_target_pairs={{0,1},{1,0},{2,3},{3,2},{4,5},{5,4},{6,7},{7,6},{8,9},{9,8},{10,11... | collective-permute-start | bytes 6291464 | tf_op jit(solution)/shard_map/ppermute | solution.py:179
  128.8 3.8 %collective-permute-done.1 = bf16[4096,256]{1,0:T(8,128)(2,1)S(1)} collective-permute-done((bf16[4096,256]{1,0:T(8,128)(2,1)S(1)}, bf16[4096,256]{1,0:T(8,128)(2,1)S(1)}, u32[]{:S(2)}, u32[]{:S(2)}) %collective-permute-start.1) | collective-permute-done | bytes 2097184 | tf_op jit(solution)/shard_map/ppermute | solution.py:179
  132.6 2.2 %pad_maximum_fusion.src_ref = bf16[8192,256]{1,0:T(8,128)(2,1)} fusion(bf16[4096,256]{1,0:T(8,128)(2,1)S(1)} %collective-permute-done.1, bf16[4096,256]{1,0:T(8,128)(2,1)S(1)} %bitcast.21), kind=kLoop, calls=%fused_computation.2 | loop fusion | flops 8388608 | bytes 8388608 | tf_op jit(solution)/shard_map/concatenate | solution.py:179
  134.8 7.1 %shard_map.95 = bf16[4096,256]{1,0:T(8,128)(2,1)S(1)} custom-call(s32[2]{0:T(128)S(1)} %pad_add_fusion.count_ref, s32[512]{0:T(512)S(1)} %copy-done.1, s32[512]{0:T(512)S(1)} %fusion.3.fetch_ref, bf16[512,128,128]{2,1,0:T(8,128)(2,1)} %tiles_ref.3, bf16[8192,256]{1,0:T(8,128)(2,1)} %pad_maximum_fusion.src_ref), custom_call_target="tpu_custom_call" | custom-call | flops 4294967296 | bytes 23068672 | tf_op jit(solution)/shard_map/pallas_call | solution.py:124
  141.9 1.0 convolution_convert_fusion.2
  142.9 0.1 pad_maximum_fusion.1
  143.0 37.4 %all_to_all.32 = bf16[8,544,256]{2,1,0:T(8,128)(2,1)S(1)} all-to-all(bf16[8,544,256]{2,1,0:T(8,128)(2,1)S(1)} %pad_maximum_fusion.1), channel_id=1, replica_groups=mesh['row'=8,'colhi'=8,'core'=2] {'row'}, dimensions={0} | all-to-all | bytes 4456448 | tf_op jit(solution)/shard_map/all_to_all | solution.py:147
  180.4 0.3 convert_reduce_fusion
  180.8 17.9 %all_to_all.33 = f32[16,32,256]{2,1,0:T(8,128)S(1)} all-to-all(f32[16,32,256]{2,1,0:T(8,128)S(1)} %broadcast_in_dim.10), channel_id=1, replica_groups=mesh['row'=8,'colhi'=8,'core'=2] {'colhi','core'}, dimensions={0} | all-to-all | bytes 1048576 | tf_op jit(solution)/shard_map/all_to_all | solution.py:143
  198.7 0.7 broadcast_in_dim.11
  199.5 3.4 %all-to-all-start.5 = ((f32[8,32,256]{2,1,0:T(8,128)}), f32[8,32,256]{2,1,0:T(8,128)S(1)}, u32[]{:S(2)}, u32[]{:S(2)}) async-start(f32[8,32,256]{2,1,0:T(8,128)} %broadcast_in_dim.11), calls=%async_computation.5 | async-start | bytes 524288 | tf_op jit(solution)/shard_map/all_to_all | solution.py:143
  202.9 1.0 convolution_convert_fusion.1
  203.8 5.1 %all-to-all-done.5 = f32[8,32,256]{2,1,0:T(8,128)S(1)} async-done(((f32[8,32,256]{2,1,0:T(8,128)}), f32[8,32,256]{2,1,0:T(8,128)S(1)}, u32[]{:S(2)}, u32[]{:S(2)}) %all-to-all-start.5) | async-done | bytes 262176 | tf_op jit(solution)/shard_map/all_to_all | solution.py:143
  208.9 0.7 copy.12
  (4 shorter events, 0.1 us)
Async XLA Ops:
  0.6 34.6 %copy-start = (bf16[256,256]{1,0:T(8,128)(2,1)S(1)}, bf16[256,256]{1,0:T(8,128)(2,1)}, u32[]{:S(2)}) copy-start(bf16[256,256]{1,0:T(8,128)(2,1)} %param.8) | copy-start | bytes 393220
  3.1 32.1 %all-to-all-start = ((bf16[8,512,256]{2,1,0:T(8,128)(2,1)}), bf16[8,512,256]{2,1,0:T(8,128)(2,1)S(1)}, u32[]{:S(2)}, u32[]{:S(2)}) async-start(bf16[8,512,256]{2,1,0:T(8,128)(2,1)} %broadcast_in_dim.8), calls=%async_computation | async-start | bytes 4194304 | tf_op jit(solution)/shard_map/all_to_all | solution.py:143
  35.2 2.0 copy-start.1
  35.2 2.0 copy-start.2
  44.9 5.4 %collective-permute-start = (bf16[4096,256]{1,0:T(8,128)(2,1)S(1)}, bf16[4096,256]{1,0:T(8,128)(2,1)S(1)}, u32[]{:S(2)}, u32[]{:S(2)}) collective-permute-start(bf16[4096,256]{1,0:T(8,128)(2,1)S(1)} %get-tuple-element.6), channel_id=1, source_target_pairs={{0,1},{1,0},{2,3},{3,2},{4,5},{5,4},{6,7},{7,6},{8,9},{9,8},{10,11... | collective-permute-start | bytes 6291464 | tf_op jit(solution)/shard_map/ppermute | solution.py:172
  94.5 1.0 copy-start.3
  126.4 6.2 %collective-permute-start.1 = (bf16[4096,256]{1,0:T(8,128)(2,1)S(1)}, bf16[4096,256]{1,0:T(8,128)(2,1)S(1)}, u32[]{:S(2)}, u32[]{:S(2)}) collective-permute-start(bf16[4096,256]{1,0:T(8,128)(2,1)S(1)} %bitcast.20), channel_id=1, source_target_pairs={{0,1},{1,0},{2,3},{3,2},{4,5},{5,4},{6,7},{7,6},{8,9},{9,8},{10,11... | collective-permute-start | bytes 6291464 | tf_op jit(solution)/shard_map/ppermute | solution.py:179
  199.5 9.5 %all-to-all-start.5 = ((f32[8,32,256]{2,1,0:T(8,128)}), f32[8,32,256]{2,1,0:T(8,128)S(1)}, u32[]{:S(2)}, u32[]{:S(2)}) async-start(f32[8,32,256]{2,1,0:T(8,128)} %broadcast_in_dim.11), calls=%async_computation.5 | async-start | bytes 524288 | tf_op jit(solution)/shard_map/all_to_all | solution.py:143

commit v11 on v10

--- a/solution.py
+++ b/solution.py
@@ -138,6 +138,69 @@
     )(count, place_index, fetch_index, tile_values, source)
 
 
+MESH = pl.DeviceIdType.MESH
+AXES = ("row", "colhi", "core")
+
+
+def exchange_kernel(src_ref, dst_ref, send_sem, recv_sem, local_sem, *, axis, parts, gather):
+    me = lax.axis_index(axis)
+
+    def device(peer):
+        return tuple(peer if name == axis else lax.axis_index(name) for name in AXES)
+
+    barrier = pltpu.get_barrier_semaphore()
+    for k in range(1, parts):
+        peer = lax.rem(me + k, parts)
+        pl.semaphore_signal(barrier, inc=1, device_id=device(peer), device_id_type=MESH)
+    pl.semaphore_wait(barrier, parts - 1)
+
+    local = pltpu.make_async_copy(src_ref if gather else src_ref.at[me], dst_ref.at[me], local_sem)
+    local.start()
+    sends = []
+    for k in range(1, parts):
+        peer = lax.rem(me + k, parts)
+        copy = pltpu.make_async_remote_copy(
+            src_ref=src_ref if gather else src_ref.at[peer],
+            dst_ref=dst_ref.at[me],
+            send_sem=send_sem.at[k],
+            recv_sem=recv_sem.at[k],
+            device_id=device(peer),
+            device_id_type=MESH,
+        )
+        copy.start()
+        sends.append(copy)
+    for k in range(1, parts):
+        source = lax.rem(me + parts - k, parts)
+        incoming = pltpu.make_async_remote_copy(
+            src_ref=src_ref if gather else src_ref.at[source],
+            dst_ref=dst_ref.at[source],
+            send_sem=send_sem.at[k],
+            recv_sem=recv_sem.at[k],
+            device_id=device(source),
+            device_id_type=MESH,
+        )
+        incoming.wait_recv()
+    for copy in sends:
+        copy.wait_send()
+    local.wait()
+
+
+def exchange(values, axis, parts, gather, tag):
+    block = values.shape if gather else values.shape[1:]
+    return pl.pallas_call(
+        functools.partial(exchange_kernel, axis=axis, parts=parts, gather=gather),
+        out_shape=jax.ShapeDtypeStruct((parts,) + block, values.dtype),
+        in_specs=[pl.BlockSpec(memory_space=pl.ANY)],
+        out_specs=pl.BlockSpec(memory_space=pl.ANY),
+        scratch_shapes=[
+            pltpu.SemaphoreType.DMA((parts,)),
+            pltpu.SemaphoreType.DMA((parts,)),
+            pltpu.SemaphoreType.DMA,
+        ],
+        compiler_params=pltpu.CompilerParams(collective_id=tag, has_side_effects=True),
+    )(values)
+
+
 def gather_rows(values, axes, parts):
     copies = jnp.broadcast_to(values[None], (parts,) + values.shape)
     return lax.all_to_all(copies, axes, 0, 0, tiled=True).reshape(-1, values.shape[-1])
@@ -161,7 +224,7 @@
     col_tiles = node_dev * row_count // tile_size
     core = lax.axis_index("core")
     count = jnp.stack([tile_count.reshape(()), core.astype(jnp.int32)])
-    features_block = gather_rows(features, "row", row_count)
+    features_block = exchange(features, "row", row_count, True, 0).reshape(-1, hidden)
     panel_rows = jnp.dot(features_block, weight, preferred_element_type=jnp.float32).astype(
         jnp.bfloat16
     )

time: 211 us -> 214 us (1.014)
  Pallas kernels: 14.8 us -> 55.1 us
  waiting for transfers between devices: 38.1 us -> 12.6 us
  blocking collectives: 129 us -> 120 us
  starting transfers between devices: 13.3 us -> 10.6 us
  local copies, waits for them, and re-layouts: 4.72 us -> 2.27 us
    pallas_call x0 -> x1, Pallas kernels: none -> 30.9 us  [exchange(): pl.pallas_call(functools.partial(exchange_kernel, axis=axis, parts=parts,...]
    all_to_all x2 -> x1, waiting for transfers between devices: 30.5 us -> 5.08 us  [gather_rows(): lax.all_to_all(copies, axes, 0, 0, tiled=True).reshape(-1, values.shape[-1])]
    all_to_all x2, blocking collectives: 81 us -> 69 us  [scatter_sum(): lax.all_to_all(values.reshape(parts, -1, values.shape[-1]), axes, 0, 0, t...]
    pallas_call x2, Pallas kernels: 14.8 us -> 24.2 us  [tile_products(): pl.pallas_call(functools.partial(tile_kernel, forward=forward, block_rows...]
    all_to_all x2 -> x1, starting transfers between devices: 9.36 us -> 3.41 us  [gather_rows(): lax.all_to_all(copies, axes, 0, 0, tiled=True).reshape(-1, values.shape[-1])]
    all_to_all x2, blocking collectives: 47.8 us -> 51 us  [gather_rows(): lax.all_to_all(copies, axes, 0, 0, tiled=True).reshape(-1, values.shape[-1])]
    ppermute x1, starting transfers between devices: 1.61 us -> 4.82 us  [body(): got = lax.ppermute(give, 'core', swap)]
    broadcast_in_dim x4 -> x3, local copies, waits for them, and re-layouts: 3.36 us -> 0.91 us  [gather_rows(): copies = jnp.broadcast_to(values[None], (parts,) + values.shape)]
  transfers between devices with their start and end apart: 4 -> 3, of which waited for: 4 -> 3; matrix products, arithmetic and copies ran while one was open for 1% -> 0% of each run, Pallas kernels for 0% -> 0%
where the time goes in v11:
time: 214 us; the launch traced here: 212 us
  blocking collectives  120 us (56%)
  Pallas kernels  55.1 us (26%)
  waiting for transfers between devices  12.6 us (6%)
  starting transfers between devices  10.6 us (5%)
  matrix products  5.58 us (3%)
  other arithmetic  4.68 us (2%)
  local copies, waits for them, and re-layouts  2.27 us (1%)
    all_to_all x2, blocking collectives, scatter_sum(): lax.all_to_all(values.reshape(parts, -1, values.shape[-1]), axes, 0, 0, t...  69 us
    all_to_all x2, blocking collectives, gather_rows(): lax.all_to_all(copies, axes, 0, 0, tiled=True).reshape(-1, values.shape[-1])  51 us
    pallas_call x1, Pallas kernels, exchange(): pl.pallas_call(functools.partial(exchange_kernel, axis=axis, parts=parts,...  30.9 us
    pallas_call x2, Pallas kernels, tile_products(): pl.pallas_call(functools.partial(tile_kernel, forward=forward, block_rows...  24.2 us
    all_to_all x1, waiting for transfers between devices, gather_rows(): lax.all_to_all(copies, axes, 0, 0, tiled=True).reshape(-1, values.shape[-1])  5.08 us
    ppermute x1, starting transfers between devices, body(): got = lax.ppermute(give, 'core', swap)  4.82 us
  transfers between devices with their start and end apart: 3, of which 3 were waited for; matrix products, arithmetic and copies ran while one was open for 0% of the time, Pallas kernels for 0%

profile of v11, /device:TPU:1, one launch (start us, length us, event | category | flops | bytes accessed | tf_op | source)
XLA Modules:
  0.0 212.3 jit_solution(12597948784855930435)
XLA Ops:
  0.6 0.0 copy-start
  1.3 30.9 %shard_map.94 = bf16[8,512,256]{2,1,0:T(8,128)(2,1)} custom-call(bf16[512,256]{1,0:T(8,128)(2,1)} %src_ref.1), custom_call_target="tpu_custom_call" | custom-call | tf_op jit(solution)/shard_map/pallas_call | solution.py:190
  32.3 0.1 pad_add_fusion.count_ref
  32.3 0.0 copy-done
  32.3 0.0 copy-start.1
  32.4 0.0 copy-start.2
  32.4 3.7 %convolution_convert_fusion.src_ref = bf16[4096,256]{1,0:T(8,128)(2,1)} fusion(bf16[4096,256]{1,0:T(8,128)(2,1)} %bitcast.17, bf16[256,256]{1,0:T(8,128)(2,1)S(1)} %copy-done), kind=kOutput, calls=%fused_computation | convolution fusion | flops 537919488 | bytes 4325376 | tf_op jit(solution)/shard_map/dot_general | solution.py:228
  36.0 0.0 copy-done.1
  36.0 0.0 copy-done.2
  36.0 12.2 %shard_map.95 = (bf16[4096,256]{1,0:T(8,128)(2,1)S(1)}, bf16[4096,256]{1,0:T(8,128)(2,1)S(1)}) custom-call(s32[2]{0:T(128)S(1)} %pad_add_fusion.count_ref, s32[512]{0:T(512)S(1)} %copy-done.2, s32[512]{0:T(512)S(1)} %copy-done.1, bf16[512,128,128]{2,1,0:T(8,128)(2,1)} %tiles_ref.3, bf16[4096,256]{1,0:T(8,128)(2,1)} %convolution_convert_fusion.src_ref), custom_call_target="tpu_custom_call" | custom-call | flops 4294967296 | bytes 23068672 | tf_op jit(solution)/shard_map/pallas_call | solution.py:124
  48.2 4.8 %collective-permute-start = (bf16[4096,256]{1,0:T(8,128)(2,1)S(1)}, bf16[4096,256]{1,0:T(8,128)(2,1)S(1)}, u32[]{:S(2)}, u32[]{:S(2)}) collective-permute-start(bf16[4096,256]{1,0:T(8,128)(2,1)S(1)} %get-tuple-element.6), channel_id=1, source_target_pairs={{0,1},{1,0},{2,3},{3,2},{4,5},{5,4},{6,7},{7,6},{8,9},{9,8},{10,11... | collective-permute-start | bytes 6291464 | tf_op jit(solution)/shard_map/ppermute | solution.py:235
  53.0 3.8 %collective-permute-done = bf16[4096,256]{1,0:T(8,128)(2,1)S(1)} collective-permute-done((bf16[4096,256]{1,0:T(8,128)(2,1)S(1)}, bf16[4096,256]{1,0:T(8,128)(2,1)S(1)}, u32[]{:S(2)}, u32[]{:S(2)}) %collective-permute-start) | collective-permute-done | bytes 2097184 | tf_op jit(solution)/shard_map/ppermute | solution.py:235
  56.8 0.6 add_convert_fusion
  57.5 34.8 %all_to_all.25 = bf16[8,512,256]{2,1,0:T(8,128)(2,1)S(1)} all-to-all(bf16[8,512,256]{2,1,0:T(8,128)(2,1)S(1)} %bitcast.19), channel_id=1, replica_groups=mesh['row'=8,'colhi'=8,'core'=2] {'colhi'}, dimensions={0} | all-to-all | bytes 4194304 | tf_op jit(solution)/shard_map/all_to_all | solution.py:210
  92.3 0.0 copy-start.4
  92.3 0.3 convert_reduce_fusion.1
  92.6 0.6 copy-done.4
  93.2 0.9 multiply_convert_fusion
  94.2 0.1 broadcast_in_dim.6
  94.3 29.9 %all_to_all.26 = bf16[8,512,256]{2,1,0:T(8,128)(2,1)S(1)} all-to-all(bf16[8,512,256]{2,1,0:T(8,128)(2,1)S(1)} %broadcast_in_dim.6), channel_id=1, replica_groups=mesh['row'=8,'colhi'=8,'core'=2] {'colhi'}, dimensions={0} | all-to-all | bytes 4194304 | tf_op jit(solution)/shard_map/all_to_all | solution.py:206
  124.2 2.4 %collective-permute-start.1 = (bf16[4096,256]{1,0:T(8,128)(2,1)S(1)}, bf16[4096,256]{1,0:T(8,128)(2,1)S(1)}, u32[]{:S(2)}, u32[]{:S(2)}) collective-permute-start(bf16[4096,256]{1,0:T(8,128)(2,1)S(1)} %bitcast.20), channel_id=1, source_target_pairs={{0,1},{1,0},{2,3},{3,2},{4,5},{5,4},{6,7},{7,6},{8,9},{9,8},{10,11... | collective-permute-start | bytes 6291464 | tf_op jit(solution)/shard_map/ppermute | solution.py:242
  126.6 3.8 %collective-permute-done.1 = bf16[4096,256]{1,0:T(8,128)(2,1)S(1)} collective-permute-done((bf16[4096,256]{1,0:T(8,128)(2,1)S(1)}, bf16[4096,256]{1,0:T(8,128)(2,1)S(1)}, u32[]{:S(2)}, u32[]{:S(2)}) %collective-permute-start.1) | collective-permute-done | bytes 2097184 | tf_op jit(solution)/shard_map/ppermute | solution.py:242
  130.4 2.2 %pad_maximum_fusion.src_ref = bf16[8192,256]{1,0:T(8,128)(2,1)} fusion(bf16[4096,256]{1,0:T(8,128)(2,1)S(1)} %collective-permute-done.1, bf16[4096,256]{1,0:T(8,128)(2,1)S(1)} %bitcast.21), kind=kLoop, calls=%fused_computation.2 | loop fusion | flops 8388608 | bytes 8388608 | tf_op jit(solution)/shard_map/concatenate | solution.py:242
  132.6 0.0 copy-start.3
  132.6 12.0 %shard_map.96 = bf16[4096,256]{1,0:T(8,128)(2,1)S(1)} custom-call(s32[2]{0:T(128)S(1)} %pad_add_fusion.count_ref, s32[512]{0:T(512)S(1)} %copy-done.1, s32[512]{0:T(512)S(1)} %fusion.3.fetch_ref, bf16[512,128,128]{2,1,0:T(8,128)(2,1)} %tiles_ref.3, bf16[8192,256]{1,0:T(8,128)(2,1)} %pad_maximum_fusion.src_ref), custom_call_target="tpu_custom_call" | custom-call | flops 4294967296 | bytes 23068672 | tf_op jit(solution)/shard_map/pallas_call | solution.py:124
  144.6 0.0 copy-done.3
  144.6 1.0 convolution_convert_fusion.2
  145.6 0.1 pad_maximum_fusion.1
  145.7 34.2 %all_to_all.27 = bf16[8,544,256]{2,1,0:T(8,128)(2,1)S(1)} all-to-all(bf16[8,544,256]{2,1,0:T(8,128)(2,1)S(1)} %pad_maximum_fusion.1), channel_id=1, replica_groups=mesh['row'=8,'colhi'=8,'core'=2] {'row'}, dimensions={0} | all-to-all | bytes 4456448 | tf_op jit(solution)/shard_map/all_to_all | solution.py:210
  179.9 0.3 convert_reduce_fusion
  180.3 21.1 %all_to_all.28 = f32[16,32,256]{2,1,0:T(8,128)S(1)} all-to-all(f32[16,32,256]{2,1,0:T(8,128)S(1)} %broadcast_in_dim.7), channel_id=1, replica_groups=mesh['row'=8,'colhi'=8,'core'=2] {'colhi','core'}, dimensions={0} | all-to-all | bytes 1048576 | tf_op jit(solution)/shard_map/all_to_all | solution.py:206
  201.4 0.7 broadcast_in_dim.8
  202.1 3.4 %all-to-all-start.4 = ((f32[8,32,256]{2,1,0:T(8,128)}), f32[8,32,256]{2,1,0:T(8,128)S(1)}, u32[]{:S(2)}, u32[]{:S(2)}) async-start(f32[8,32,256]{2,1,0:T(8,128)} %broadcast_in_dim.8), calls=%async_computation.4 | async-start | bytes 524288 | tf_op jit(solution)/shard_map/all_to_all | solution.py:206
  205.6 1.0 convolution_convert_fusion.1
  206.5 5.1 %all-to-all-done.4 = f32[8,32,256]{2,1,0:T(8,128)S(1)} async-done(((f32[8,32,256]{2,1,0:T(8,128)}), f32[8,32,256]{2,1,0:T(8,128)S(1)}, u32[]{:S(2)}, u32[]{:S(2)}) %all-to-all-start.4) | async-done | bytes 262176 | tf_op jit(solution)/shard_map/all_to_all | solution.py:206
  211.6 0.7 copy.12
  (4 shorter events, 0.1 us)
Async XLA Ops:
  0.6 31.7 %copy-start = (bf16[256,256]{1,0:T(8,128)(2,1)S(1)}, bf16[256,256]{1,0:T(8,128)(2,1)}, u32[]{:S(2)}) copy-start(bf16[256,256]{1,0:T(8,128)(2,1)} %param.8) | copy-start | bytes 393220
  32.3 3.7 %copy-start.1 = (s32[512]{0:T(512)S(1)}, s32[512]{0:T(512)}, u32[]{:S(2)}) copy-start(s32[512]{0:T(512)} %place_ref.3) | copy-start | bytes 6148
  32.4 3.7 %copy-start.2 = (s32[512]{0:T(512)S(1)}, s32[512]{0:T(512)}, u32[]{:S(2)}) copy-start(s32[512]{0:T(512)} %place_ref.2) | copy-start | bytes 6148
  48.2 8.6 %collective-permute-start = (bf16[4096,256]{1,0:T(8,128)(2,1)S(1)}, bf16[4096,256]{1,0:T(8,128)(2,1)S(1)}, u32[]{:S(2)}, u32[]{:S(2)}) collective-permute-start(bf16[4096,256]{1,0:T(8,128)(2,1)S(1)} %get-tuple-element.6), channel_id=1, source_target_pairs={{0,1},{1,0},{2,3},{3,2},{4,5},{5,4},{6,7},{7,6},{8,9},{9,8},{10,11... | collective-permute-start | bytes 6291464 | tf_op jit(solution)/shard_map/ppermute | solution.py:235
  92.3 1.0 copy-start.4
  124.2 6.2 %collective-permute-start.1 = (bf16[4096,256]{1,0:T(8,128)(2,1)S(1)}, bf16[4096,256]{1,0:T(8,128)(2,1)S(1)}, u32[]{:S(2)}, u32[]{:S(2)}) collective-permute-start(bf16[4096,256]{1,0:T(8,128)(2,1)S(1)} %bitcast.20), channel_id=1, source_target_pairs={{0,1},{1,0},{2,3},{3,2},{4,5},{5,4},{6,7},{7,6},{8,9},{9,8},{10,11... | collective-permute-start | bytes 6291464 | tf_op jit(solution)/shard_map/ppermute | solution.py:242
  132.6 12.0 %copy-start.3 = (bf16[8,512,256]{2,1,0:T(8,128)(2,1)S(1)}, bf16[8,512,256]{2,1,0:T(8,128)(2,1)}, u32[]{:S(2)}) copy-start(bf16[8,512,256]{2,1,0:T(8,128)(2,1)} %shard_map.94) | copy-start | bytes 6291460
  202.1 9.5 %all-to-all-start.4 = ((f32[8,32,256]{2,1,0:T(8,128)}), f32[8,32,256]{2,1,0:T(8,128)S(1)}, u32[]{:S(2)}, u32[]{:S(2)}) async-start(f32[8,32,256]{2,1,0:T(8,128)} %broadcast_in_dim.8), calls=%async_computation.4 | async-start | bytes 524288 | tf_op jit(solution)/shard_map/all_to_all | solution.py:206

commit v12 on v10

--- a/solution.py
+++ b/solution.py
@@ -199,8 +199,9 @@
     )
     reduced = scatter_sum(packed, "row", row_count)
     grad_nodes = reduced[:node_dev].astype(jnp.bfloat16)
-    col_terms = gather_rows(reduced[node_dev:], ("colhi", "core"), col_count)
-    weight_rows = col_terms.reshape(col_count, term_rows, hidden).sum(0)
+    chip_terms = reduced[node_dev:] + lax.ppermute(reduced[node_dev:], "core", swap)
+    col_terms = gather_rows(chip_terms, "colhi", pair_count)
+    weight_rows = col_terms.reshape(pair_count, term_rows, hidden).sum(0)
     grad_weight = gather_rows(weight_rows, "row", row_count)
     grad_features = lax.dot_general(
         grad_nodes, weight, (((1,), (1,)), ((), ())), preferred_element_type=jnp.float32

time: 211 us -> 208 us (0.986)
  blocking collectives: 129 us -> 108 us
  starting transfers between devices: 13.3 us -> 21.5 us
  Pallas kernels: 14.8 us -> 22.8 us
    all_to_all x2, blocking collectives: 81 us -> 66.5 us  [scatter_sum(): lax.all_to_all(values.reshape(parts, -1, values.shape[-1]), axes, 0, 0, t...]
    pallas_call x2, Pallas kernels: 14.8 us -> 22.8 us  [tile_products(): pl.pallas_call(functools.partial(tile_kernel, forward=forward, block_rows...]
    all_to_all x2, blocking collectives: 47.8 us -> 41.3 us  [gather_rows(): lax.all_to_all(copies, axes, 0, 0, tiled=True).reshape(-1, values.shape[-1])]
    ppermute x1, starting transfers between devices: 1.61 us -> 6.67 us  [body(): got = lax.ppermute(give, 'core', swap)]
    ppermute x0 -> x1, starting transfers between devices: none -> 3.1 us  [body(): lax.ppermute(reduced[node_dev:], 'core', swap)]
  transfers between devices with their start and end apart: 4 -> 5, of which waited for: 4 -> 5; matrix products, arithmetic and copies ran while one was open for 1% -> 1% of each run, Pallas kernels for 0% -> 0%
where the time goes in v12:
time: 208 us; the launch traced here: 206 us
  blocking collectives  108 us (52%)
  waiting for transfers between devices  38.9 us (19%)
  Pallas kernels  22.8 us (11%)
  starting transfers between devices  21.5 us (10%)
  local copies, waits for them, and re-layouts  4.69 us (2%)
  other arithmetic  4.62 us (2%)
  matrix products  3.98 us (2%)
    all_to_all x2, blocking collectives, scatter_sum(): lax.all_to_all(values.reshape(parts, -1, values.shape[-1]), axes, 0, 0, t...  66.5 us
    all_to_all x2, blocking collectives, gather_rows(): lax.all_to_all(copies, axes, 0, 0, tiled=True).reshape(-1, values.shape[-1])  41.3 us
    all_to_all x2, waiting for transfers between devices, gather_rows(): lax.all_to_all(copies, axes, 0, 0, tiled=True).reshape(-1, values.shape[-1])  30.5 us
    pallas_call x2, Pallas kernels, tile_products(): pl.pallas_call(functools.partial(tile_kernel, forward=forward, block_rows...  22.8 us
    all_to_all x2, starting transfers between devices, gather_rows(): lax.all_to_all(copies, axes, 0, 0, tiled=True).reshape(-1, values.shape[-1])  9.36 us
    ppermute x1, starting transfers between devices, body(): got = lax.ppermute(give, 'core', swap)  6.67 us
  transfers between devices with their start and end apart: 5, of which 5 were waited for; matrix products, arithmetic and copies ran while one was open for 1% of the time, Pallas kernels for 0%

profile of v12, /device:TPU:1, one launch (start us, length us, event | category | flops | bytes accessed | tf_op | source)
XLA Modules:
  0.0 205.7 jit_solution(8387028543473030807)
XLA Ops:
  0.6 0.0 copy-start
  0.6 2.4 %broadcast_in_dim.8 = bf16[8,512,256]{2,1,0:T(8,128)(2,1)} broadcast(bf16[512,256]{1,0:T(8,128)(2,1)} %param.7), dimensions={1,2} | broadcast | bytes 2359296 | tf_op jit(solution)/shard_map/broadcast_in_dim | solution.py:142
  3.1 5.9 %all-to-all-start = ((bf16[8,512,256]{2,1,0:T(8,128)(2,1)}), bf16[8,512,256]{2,1,0:T(8,128)(2,1)S(1)}, u32[]{:S(2)}, u32[]{:S(2)}) async-start(bf16[8,512,256]{2,1,0:T(8,128)(2,1)} %broadcast_in_dim.8), calls=%async_computation | async-start | bytes 4194304 | tf_op jit(solution)/shard_map/all_to_all | solution.py:143
  9.7 0.1 pad_add_fusion.count_ref
  9.8 25.4 %all-to-all-done = bf16[8,512,256]{2,1,0:T(8,128)(2,1)S(1)} async-done(((bf16[8,512,256]{2,1,0:T(8,128)(2,1)}), bf16[8,512,256]{2,1,0:T(8,128)(2,1)S(1)}, u32[]{:S(2)}, u32[]{:S(2)}) %all-to-all-start) | async-done | bytes 2097184 | tf_op jit(solution)/shard_map/all_to_all | solution.py:143
  35.2 0.0 copy-done
  35.2 0.0 copy-start.1
  35.2 0.0 copy-start.2
  35.2 2.0 convolution_convert_fusion.src_ref
  37.2 0.0 copy-done.1
  37.2 0.0 copy-done.2
  37.2 11.5 %shard_map.94 = (bf16[4096,256]{1,0:T(8,128)(2,1)S(1)}, bf16[4096,256]{1,0:T(8,128)(2,1)S(1)}) custom-call(s32[2]{0:T(128)S(1)} %pad_add_fusion.count_ref, s32[512]{0:T(512)S(1)} %copy-done.2, s32[512]{0:T(512)S(1)} %copy-done.1, bf16[512,128,128]{2,1,0:T(8,128)(2,1)} %tiles_ref.3, bf16[4096,256]{1,0:T(8,128)(2,1)} %convolution_convert_fusion.src_ref), custom_call_target="tpu_custom_call" | custom-call | flops 4294967296 | bytes 23068672 | tf_op jit(solution)/shard_map/pallas_call | solution.py:124
  48.7 6.7 %collective-permute-start = (bf16[4096,256]{1,0:T(8,128)(2,1)S(1)}, bf16[4096,256]{1,0:T(8,128)(2,1)S(1)}, u32[]{:S(2)}, u32[]{:S(2)}) collective-permute-start(bf16[4096,256]{1,0:T(8,128)(2,1)S(1)} %get-tuple-element.6), channel_id=1, source_target_pairs={{0,1},{1,0},{2,3},{3,2},{4,5},{5,4},{6,7},{7,6},{8,9},{9,8},{10,11... | collective-permute-start | bytes 6291464 | tf_op jit(solution)/shard_map/ppermute | solution.py:172
  55.4 3.8 %collective-permute-done = bf16[4096,256]{1,0:T(8,128)(2,1)S(1)} collective-permute-done((bf16[4096,256]{1,0:T(8,128)(2,1)S(1)}, bf16[4096,256]{1,0:T(8,128)(2,1)S(1)}, u32[]{:S(2)}, u32[]{:S(2)}) %collective-permute-start) | collective-permute-done | bytes 2097184 | tf_op jit(solution)/shard_map/ppermute | solution.py:172
  59.2 0.6 add_convert_fusion
  59.8 33.4 %all_to_all.30 = bf16[8,512,256]{2,1,0:T(8,128)(2,1)S(1)} all-to-all(bf16[8,512,256]{2,1,0:T(8,128)(2,1)S(1)} %bitcast.19), channel_id=1, replica_groups=mesh['row'=8,'colhi'=8,'core'=2] {'colhi'}, dimensions={0} | all-to-all | bytes 4194304 | tf_op jit(solution)/shard_map/all_to_all | solution.py:147
  93.1 0.0 copy-start.3
  93.1 0.3 convert_reduce_fusion.1
  93.4 0.6 copy-done.3
  94.1 0.9 multiply_convert_fusion
  95.0 0.1 broadcast_in_dim.9
  95.2 29.9 %all_to_all.31 = bf16[8,512,256]{2,1,0:T(8,128)(2,1)S(1)} all-to-all(bf16[8,512,256]{2,1,0:T(8,128)(2,1)S(1)} %broadcast_in_dim.9), channel_id=1, replica_groups=mesh['row'=8,'colhi'=8,'core'=2] {'colhi'}, dimensions={0} | all-to-all | bytes 4194304 | tf_op jit(solution)/shard_map/all_to_all | solution.py:143
  125.1 2.4 %collective-permute-start.1 = (bf16[4096,256]{1,0:T(8,128)(2,1)S(1)}, bf16[4096,256]{1,0:T(8,128)(2,1)S(1)}, u32[]{:S(2)}, u32[]{:S(2)}) collective-permute-start(bf16[4096,256]{1,0:T(8,128)(2,1)S(1)} %bitcast.20), channel_id=1, source_target_pairs={{0,1},{1,0},{2,3},{3,2},{4,5},{5,4},{6,7},{7,6},{8,9},{9,8},{10,11... | collective-permute-start | bytes 6291464 | tf_op jit(solution)/shard_map/ppermute | solution.py:179
  127.5 3.8 %collective-permute-done.1 = bf16[4096,256]{1,0:T(8,128)(2,1)S(1)} collective-permute-done((bf16[4096,256]{1,0:T(8,128)(2,1)S(1)}, bf16[4096,256]{1,0:T(8,128)(2,1)S(1)}, u32[]{:S(2)}, u32[]{:S(2)}) %collective-permute-start.1) | collective-permute-done | bytes 2097184 | tf_op jit(solution)/shard_map/ppermute | solution.py:179
  131.2 2.2 %pad_maximum_fusion.src_ref = bf16[8192,256]{1,0:T(8,128)(2,1)} fusion(bf16[4096,256]{1,0:T(8,128)(2,1)S(1)} %collective-permute-done.1, bf16[4096,256]{1,0:T(8,128)(2,1)S(1)} %bitcast.21), kind=kLoop, calls=%fused_computation.2 | loop fusion | flops 8388608 | bytes 8388608 | tf_op jit(solution)/shard_map/concatenate | solution.py:179
  133.5 11.4 %shard_map.95 = bf16[4096,256]{1,0:T(8,128)(2,1)S(1)} custom-call(s32[2]{0:T(128)S(1)} %pad_add_fusion.count_ref, s32[512]{0:T(512)S(1)} %copy-done.1, s32[512]{0:T(512)S(1)} %fusion.3.fetch_ref, bf16[512,128,128]{2,1,0:T(8,128)(2,1)} %tiles_ref.3, bf16[8192,256]{1,0:T(8,128)(2,1)} %pad_maximum_fusion.src_ref), custom_call_target="tpu_custom_call" | custom-call | flops 4294967296 | bytes 23068672 | tf_op jit(solution)/shard_map/pallas_call | solution.py:124
  144.8 1.0 convolution_convert_fusion.2
  145.8 0.1 pad_maximum_fusion.1
  146.0 33.1 %all_to_all.32 = bf16[8,544,256]{2,1,0:T(8,128)(2,1)S(1)} all-to-all(bf16[8,544,256]{2,1,0:T(8,128)(2,1)S(1)} %pad_maximum_fusion.1), channel_id=1, replica_groups=mesh['row'=8,'colhi'=8,'core'=2] {'row'}, dimensions={0} | all-to-all | bytes 4456448 | tf_op jit(solution)/shard_map/all_to_all | solution.py:147
  179.1 0.3 convert_reduce_fusion
  179.4 3.1 %collective-permute-start.2 = (f32[32,256]{1,0:T(8,128)S(1)}, f32[32,256]{1,0:T(8,128)S(1)}, u32[]{:S(2)}, u32[]{:S(2)}) collective-permute-start(f32[32,256]{1,0:T(8,128)S(1)} %slice.11), channel_id=1, source_target_pairs={{0,1},{1,0},{2,3},{3,2},{4,5},{5,4},{6,7},{7,6},{8,9},{9,8},{10,11... | collective-permute-start | bytes 98312 | tf_op jit(solution)/shard_map/ppermute | solution.py:202
  182.5 0.9 collective-permute-done.2
  183.4 11.4 %all_to_all.33 = f32[8,32,256]{2,1,0:T(8,128)S(1)} all-to-all(f32[8,32,256]{2,1,0:T(8,128)S(1)} %broadcast_in_dim.10), channel_id=1, replica_groups=mesh['row'=8,'colhi'=8,'core'=2] {'colhi'}, dimensions={0} | all-to-all | bytes 524288 | tf_op jit(solution)/shard_map/all_to_all | solution.py:143
  194.8 0.7 broadcast_in_dim.11
  195.6 3.4 %all-to-all-start.5 = ((f32[8,32,256]{2,1,0:T(8,128)}), f32[8,32,256]{2,1,0:T(8,128)S(1)}, u32[]{:S(2)}, u32[]{:S(2)}) async-start(f32[8,32,256]{2,1,0:T(8,128)} %broadcast_in_dim.11), calls=%async_computation.5 | async-start | bytes 524288 | tf_op jit(solution)/shard_map/all_to_all | solution.py:143
  199.0 1.0 convolution_convert_fusion.1
  199.9 5.1 %all-to-all-done.5 = f32[8,32,256]{2,1,0:T(8,128)S(1)} async-done(((f32[8,32,256]{2,1,0:T(8,128)}), f32[8,32,256]{2,1,0:T(8,128)S(1)}, u32[]{:S(2)}, u32[]{:S(2)}) %all-to-all-start.5) | async-done | bytes 262176 | tf_op jit(solution)/shard_map/all_to_all | solution.py:143
  205.0 0.7 copy.12
  (5 shorter events, 0.1 us)
Async XLA Ops:
  0.6 34.6 %copy-start = (bf16[256,256]{1,0:T(8,128)(2,1)S(1)}, bf16[256,256]{1,0:T(8,128)(2,1)}, u32[]{:S(2)}) copy-start(bf16[256,256]{1,0:T(8,128)(2,1)} %param.8) | copy-start | bytes 393220
  3.1 32.1 %all-to-all-start = ((bf16[8,512,256]{2,1,0:T(8,128)(2,1)}), bf16[8,512,256]{2,1,0:T(8,128)(2,1)S(1)}, u32[]{:S(2)}, u32[]{:S(2)}) async-start(bf16[8,512,256]{2,1,0:T(8,128)(2,1)} %broadcast_in_dim.8), calls=%async_computation | async-start | bytes 4194304 | tf_op jit(solution)/shard_map/all_to_all | solution.py:143
  35.2 2.0 copy-start.1
  35.2 2.0 copy-start.2
  48.7 10.5 %collective-permute-start = (bf16[4096,256]{1,0:T(8,128)(2,1)S(1)}, bf16[4096,256]{1,0:T(8,128)(2,1)S(1)}, u32[]{:S(2)}, u32[]{:S(2)}) collective-permute-start(bf16[4096,256]{1,0:T(8,128)(2,1)S(1)} %get-tuple-element.6), channel_id=1, source_target_pairs={{0,1},{1,0},{2,3},{3,2},{4,5},{5,4},{6,7},{7,6},{8,9},{9,8},{10,11... | collective-permute-start | bytes 6291464 | tf_op jit(solution)/shard_map/ppermute | solution.py:172
  93.1 1.0 copy-start.3
  125.1 6.2 %collective-permute-start.1 = (bf16[4096,256]{1,0:T(8,128)(2,1)S(1)}, bf16[4096,256]{1,0:T(8,128)(2,1)S(1)}, u32[]{:S(2)}, u32[]{:S(2)}) collective-permute-start(bf16[4096,256]{1,0:T(8,128)(2,1)S(1)} %bitcast.20), channel_id=1, source_target_pairs={{0,1},{1,0},{2,3},{3,2},{4,5},{5,4},{6,7},{7,6},{8,9},{9,8},{10,11... | collective-permute-start | bytes 6291464 | tf_op jit(solution)/shard_map/ppermute | solution.py:179
  179.4 4.0 %collective-permute-start.2 = (f32[32,256]{1,0:T(8,128)S(1)}, f32[32,256]{1,0:T(8,128)S(1)}, u32[]{:S(2)}, u32[]{:S(2)}) collective-permute-start(f32[32,256]{1,0:T(8,128)S(1)} %slice.11), channel_id=1, source_target_pairs={{0,1},{1,0},{2,3},{3,2},{4,5},{5,4},{6,7},{7,6},{8,9},{9,8},{10,11... | collective-permute-start | bytes 98312 | tf_op jit(solution)/shard_map/ppermute | solution.py:202
  195.6 9.5 %all-to-all-start.5 = ((f32[8,32,256]{2,1,0:T(8,128)}), f32[8,32,256]{2,1,0:T(8,128)S(1)}, u32[]{:S(2)}, u32[]{:S(2)}) async-start(f32[8,32,256]{2,1,0:T(8,128)} %broadcast_in_dim.11), calls=%async_computation.5 | async-start | bytes 524288 | tf_op jit(solution)/shard_map/all_to_all | solution.py:143

commit v13 on v12

--- a/solution.py
+++ b/solution.py
@@ -8,9 +8,9 @@
 from jax.sharding import Mesh, PartitionSpec as P
 
 
-GROUP = 64
+GROUP = 128
 CHUNK = 256
-UNROLL = (64, 8, 1)
+UNROLL = (128, 8, 1)
 
 
 def silu_slope(values):

time: 208 us -> 209 us (level)
  blocking collectives: 108 us -> 117 us
  Pallas kernels: 22.8 us -> 15.2 us
    pallas_call x2, Pallas kernels: 22.8 us -> 15.2 us  [tile_products(): pl.pallas_call(functools.partial(tile_kernel, forward=forward, block_rows...]
    all_to_all x2, blocking collectives: 66.5 us -> 73.9 us  [scatter_sum(): lax.all_to_all(values.reshape(parts, -1, values.shape[-1]), axes, 0, 0, t...]
where the time goes in v13:
time: 209 us; the launch traced here: 207 us
  blocking collectives  117 us (56%)
  waiting for transfers between devices  38.9 us (19%)
  starting transfers between devices  21.5 us (10%)
  Pallas kernels  15.2 us (7%)
  local copies, waits for them, and re-layouts  4.69 us (2%)
  other arithmetic  4.62 us (2%)
  matrix products  3.97 us (2%)
    all_to_all x2, blocking collectives, scatter_sum(): lax.all_to_all(values.reshape(parts, -1, values.shape[-1]), axes, 0, 0, t...  73.9 us
    all_to_all x2, blocking collectives, gather_rows(): lax.all_to_all(copies, axes, 0, 0, tiled=True).reshape(-1, values.shape[-1])  43.3 us
    all_to_all x2, waiting for transfers between devices, gather_rows(): lax.all_to_all(copies, axes, 0, 0, tiled=True).reshape(-1, values.shape[-1])  30.5 us
    pallas_call x2, Pallas kernels, tile_products(): pl.pallas_call(functools.partial(tile_kernel, forward=forward, block_rows...  15.2 us
    all_to_all x2, starting transfers between devices, gather_rows(): lax.all_to_all(copies, axes, 0, 0, tiled=True).reshape(-1, values.shape[-1])  9.36 us
    ppermute x1, starting transfers between devices, body(): got = lax.ppermute(give, 'core', swap)  6.27 us
  transfers between devices with their start and end apart: 5, of which 5 were waited for; matrix products, arithmetic and copies ran while one was open for 1% of the time, Pallas kernels for 0%

profile of v13, /device:TPU:1, one launch (start us, length us, event | category | flops | bytes accessed | tf_op | source)
XLA Modules:
  0.0 207.4 jit_solution(3310355095519535516)
XLA Ops:
  0.6 0.0 copy-start
  0.6 2.4 %broadcast_in_dim.8 = bf16[8,512,256]{2,1,0:T(8,128)(2,1)} broadcast(bf16[512,256]{1,0:T(8,128)(2,1)} %param.7), dimensions={1,2} | broadcast | bytes 2359296 | tf_op jit(solution)/shard_map/broadcast_in_dim | solution.py:142
  3.1 5.9 %all-to-all-start = ((bf16[8,512,256]{2,1,0:T(8,128)(2,1)}), bf16[8,512,256]{2,1,0:T(8,128)(2,1)S(1)}, u32[]{:S(2)}, u32[]{:S(2)}) async-start(bf16[8,512,256]{2,1,0:T(8,128)(2,1)} %broadcast_in_dim.8), calls=%async_computation | async-start | bytes 4194304 | tf_op jit(solution)/shard_map/all_to_all | solution.py:143
  9.7 0.1 pad_add_fusion.count_ref
  9.8 25.4 %all-to-all-done = bf16[8,512,256]{2,1,0:T(8,128)(2,1)S(1)} async-done(((bf16[8,512,256]{2,1,0:T(8,128)(2,1)}), bf16[8,512,256]{2,1,0:T(8,128)(2,1)S(1)}, u32[]{:S(2)}, u32[]{:S(2)}) %all-to-all-start) | async-done | bytes 2097184 | tf_op jit(solution)/shard_map/all_to_all | solution.py:143
  35.2 0.0 copy-done
  35.2 0.0 copy-start.1
  35.2 0.0 copy-start.2
  35.2 2.0 convolution_convert_fusion.src_ref
  37.2 0.0 copy-done.1
  37.2 0.0 copy-done.2
  37.2 7.9 %shard_map.94 = (bf16[4096,256]{1,0:T(8,128)(2,1)S(1)}, bf16[4096,256]{1,0:T(8,128)(2,1)S(1)}) custom-call(s32[2]{0:T(128)S(1)} %pad_add_fusion.count_ref, s32[512]{0:T(512)S(1)} %copy-done.2, s32[512]{0:T(512)S(1)} %copy-done.1, bf16[512,128,128]{2,1,0:T(8,128)(2,1)} %tiles_ref.3, bf16[4096,256]{1,0:T(8,128)(2,1)} %convolution_convert_fusion.src_ref), custom_call_target="tpu_custom_call" | custom-call | flops 4294967296 | bytes 23068672 | tf_op jit(solution)/shard_map/pallas_call | solution.py:124
  45.1 6.3 %collective-permute-start = (bf16[4096,256]{1,0:T(8,128)(2,1)S(1)}, bf16[4096,256]{1,0:T(8,128)(2,1)S(1)}, u32[]{:S(2)}, u32[]{:S(2)}) collective-permute-start(bf16[4096,256]{1,0:T(8,128)(2,1)S(1)} %get-tuple-element.6), channel_id=1, source_target_pairs={{0,1},{1,0},{2,3},{3,2},{4,5},{5,4},{6,7},{7,6},{8,9},{9,8},{10,11... | collective-permute-start | bytes 6291464 | tf_op jit(solution)/shard_map/ppermute | solution.py:172
  51.4 3.8 %collective-permute-done = bf16[4096,256]{1,0:T(8,128)(2,1)S(1)} collective-permute-done((bf16[4096,256]{1,0:T(8,128)(2,1)S(1)}, bf16[4096,256]{1,0:T(8,128)(2,1)S(1)}, u32[]{:S(2)}, u32[]{:S(2)}) %collective-permute-start) | collective-permute-done | bytes 2097184 | tf_op jit(solution)/shard_map/ppermute | solution.py:172
  55.2 0.6 add_convert_fusion
  55.8 39.1 %all_to_all.30 = bf16[8,512,256]{2,1,0:T(8,128)(2,1)S(1)} all-to-all(bf16[8,512,256]{2,1,0:T(8,128)(2,1)S(1)} %bitcast.19), channel_id=1, replica_groups=mesh['row'=8,'colhi'=8,'core'=2] {'colhi'}, dimensions={0} | all-to-all | bytes 4194304 | tf_op jit(solution)/shard_map/all_to_all | solution.py:147
  94.8 0.0 copy-start.3
  94.8 0.3 convert_reduce_fusion.1
  95.2 0.6 copy-done.3
  95.8 0.9 multiply_convert_fusion
  96.7 0.1 broadcast_in_dim.9
  96.9 29.4 %all_to_all.31 = bf16[8,512,256]{2,1,0:T(8,128)(2,1)S(1)} all-to-all(bf16[8,512,256]{2,1,0:T(8,128)(2,1)S(1)} %broadcast_in_dim.9), channel_id=1, replica_groups=mesh['row'=8,'colhi'=8,'core'=2] {'colhi'}, dimensions={0} | all-to-all | bytes 4194304 | tf_op jit(solution)/shard_map/all_to_all | solution.py:143
  126.3 2.4 %collective-permute-start.1 = (bf16[4096,256]{1,0:T(8,128)(2,1)S(1)}, bf16[4096,256]{1,0:T(8,128)(2,1)S(1)}, u32[]{:S(2)}, u32[]{:S(2)}) collective-permute-start(bf16[4096,256]{1,0:T(8,128)(2,1)S(1)} %bitcast.20), channel_id=1, source_target_pairs={{0,1},{1,0},{2,3},{3,2},{4,5},{5,4},{6,7},{7,6},{8,9},{9,8},{10,11... | collective-permute-start | bytes 6291464 | tf_op jit(solution)/shard_map/ppermute | solution.py:179
  128.8 3.8 %collective-permute-done.1 = bf16[4096,256]{1,0:T(8,128)(2,1)S(1)} collective-permute-done((bf16[4096,256]{1,0:T(8,128)(2,1)S(1)}, bf16[4096,256]{1,0:T(8,128)(2,1)S(1)}, u32[]{:S(2)}, u32[]{:S(2)}) %collective-permute-start.1) | collective-permute-done | bytes 2097184 | tf_op jit(solution)/shard_map/ppermute | solution.py:179
  132.5 2.2 %pad_maximum_fusion.src_ref = bf16[8192,256]{1,0:T(8,128)(2,1)} fusion(bf16[4096,256]{1,0:T(8,128)(2,1)S(1)} %collective-permute-done.1, bf16[4096,256]{1,0:T(8,128)(2,1)S(1)} %bitcast.21), kind=kLoop, calls=%fused_computation.2 | loop fusion | flops 8388608 | bytes 8388608 | tf_op jit(solution)/shard_map/concatenate | solution.py:179
  134.7 7.3 %shard_map.95 = bf16[4096,256]{1,0:T(8,128)(2,1)S(1)} custom-call(s32[2]{0:T(128)S(1)} %pad_add_fusion.count_ref, s32[512]{0:T(512)S(1)} %copy-done.1, s32[512]{0:T(512)S(1)} %fusion.3.fetch_ref, bf16[512,128,128]{2,1,0:T(8,128)(2,1)} %tiles_ref.3, bf16[8192,256]{1,0:T(8,128)(2,1)} %pad_maximum_fusion.src_ref), custom_call_target="tpu_custom_call" | custom-call | flops 4294967296 | bytes 23068672 | tf_op jit(solution)/shard_map/pallas_call | solution.py:124
  142.0 1.0 convolution_convert_fusion.2
  143.0 0.1 pad_maximum_fusion.1
  143.2 34.8 %all_to_all.32 = bf16[8,544,256]{2,1,0:T(8,128)(2,1)S(1)} all-to-all(bf16[8,544,256]{2,1,0:T(8,128)(2,1)S(1)} %pad_maximum_fusion.1), channel_id=1, replica_groups=mesh['row'=8,'colhi'=8,'core'=2] {'row'}, dimensions={0} | all-to-all | bytes 4456448 | tf_op jit(solution)/shard_map/all_to_all | solution.py:147
  178.0 0.3 convert_reduce_fusion
  178.3 3.4 %collective-permute-start.2 = (f32[32,256]{1,0:T(8,128)S(1)}, f32[32,256]{1,0:T(8,128)S(1)}, u32[]{:S(2)}, u32[]{:S(2)}) collective-permute-start(f32[32,256]{1,0:T(8,128)S(1)} %slice.11), channel_id=1, source_target_pairs={{0,1},{1,0},{2,3},{3,2},{4,5},{5,4},{6,7},{7,6},{8,9},{9,8},{10,11... | collective-permute-start | bytes 98312 | tf_op jit(solution)/shard_map/ppermute | solution.py:202
  181.7 0.9 collective-permute-done.2
  182.6 13.9 %all_to_all.33 = f32[8,32,256]{2,1,0:T(8,128)S(1)} all-to-all(f32[8,32,256]{2,1,0:T(8,128)S(1)} %broadcast_in_dim.10), channel_id=1, replica_groups=mesh['row'=8,'colhi'=8,'core'=2] {'colhi'}, dimensions={0} | all-to-all | bytes 524288 | tf_op jit(solution)/shard_map/all_to_all | solution.py:143
  196.6 0.7 broadcast_in_dim.11
  197.3 3.4 %all-to-all-start.5 = ((f32[8,32,256]{2,1,0:T(8,128)}), f32[8,32,256]{2,1,0:T(8,128)S(1)}, u32[]{:S(2)}, u32[]{:S(2)}) async-start(f32[8,32,256]{2,1,0:T(8,128)} %broadcast_in_dim.11), calls=%async_computation.5 | async-start | bytes 524288 | tf_op jit(solution)/shard_map/all_to_all | solution.py:143
  200.7 1.0 convolution_convert_fusion.1
  201.7 5.0 %all-to-all-done.5 = f32[8,32,256]{2,1,0:T(8,128)S(1)} async-done(((f32[8,32,256]{2,1,0:T(8,128)}), f32[8,32,256]{2,1,0:T(8,128)S(1)}, u32[]{:S(2)}, u32[]{:S(2)}) %all-to-all-start.5) | async-done | bytes 262176 | tf_op jit(solution)/shard_map/all_to_all | solution.py:143
  206.7 0.7 copy.12
  (5 shorter events, 0.1 us)
Async XLA Ops:
  0.6 34.6 %copy-start = (bf16[256,256]{1,0:T(8,128)(2,1)S(1)}, bf16[256,256]{1,0:T(8,128)(2,1)}, u32[]{:S(2)}) copy-start(bf16[256,256]{1,0:T(8,128)(2,1)} %param.8) | copy-start | bytes 393220
  3.1 32.1 %all-to-all-start = ((bf16[8,512,256]{2,1,0:T(8,128)(2,1)}), bf16[8,512,256]{2,1,0:T(8,128)(2,1)S(1)}, u32[]{:S(2)}, u32[]{:S(2)}) async-start(bf16[8,512,256]{2,1,0:T(8,128)(2,1)} %broadcast_in_dim.8), calls=%async_computation | async-start | bytes 4194304 | tf_op jit(solution)/shard_map/all_to_all | solution.py:143
  35.2 2.0 copy-start.1
  35.2 2.0 copy-start.2
  45.1 10.1 %collective-permute-start = (bf16[4096,256]{1,0:T(8,128)(2,1)S(1)}, bf16[4096,256]{1,0:T(8,128)(2,1)S(1)}, u32[]{:S(2)}, u32[]{:S(2)}) collective-permute-start(bf16[4096,256]{1,0:T(8,128)(2,1)S(1)} %get-tuple-element.6), channel_id=1, source_target_pairs={{0,1},{1,0},{2,3},{3,2},{4,5},{5,4},{6,7},{7,6},{8,9},{9,8},{10,11... | collective-permute-start | bytes 6291464 | tf_op jit(solution)/shard_map/ppermute | solution.py:172
  94.8 1.0 copy-start.3
  126.3 6.2 %collective-permute-start.1 = (bf16[4096,256]{1,0:T(8,128)(2,1)S(1)}, bf16[4096,256]{1,0:T(8,128)(2,1)S(1)}, u32[]{:S(2)}, u32[]{:S(2)}) collective-permute-start(bf16[4096,256]{1,0:T(8,128)(2,1)S(1)} %bitcast.20), channel_id=1, source_target_pairs={{0,1},{1,0},{2,3},{3,2},{4,5},{5,4},{6,7},{7,6},{8,9},{9,8},{10,11... | collective-permute-start | bytes 6291464 | tf_op jit(solution)/shard_map/ppermute | solution.py:179
  178.3 4.3 %collective-permute-start.2 = (f32[32,256]{1,0:T(8,128)S(1)}, f32[32,256]{1,0:T(8,128)S(1)}, u32[]{:S(2)}, u32[]{:S(2)}) collective-permute-start(f32[32,256]{1,0:T(8,128)S(1)} %slice.11), channel_id=1, source_target_pairs={{0,1},{1,0},{2,3},{3,2},{4,5},{5,4},{6,7},{7,6},{8,9},{9,8},{10,11... | collective-permute-start | bytes 98312 | tf_op jit(solution)/shard_map/ppermute | solution.py:202
  197.3 9.4 %all-to-all-start.5 = ((f32[8,32,256]{2,1,0:T(8,128)}), f32[8,32,256]{2,1,0:T(8,128)S(1)}, u32[]{:S(2)}, u32[]{:S(2)}) async-start(f32[8,32,256]{2,1,0:T(8,128)} %broadcast_in_dim.11), calls=%async_computation.5 | async-start | bytes 524288 | tf_op jit(solution)/shard_map/all_to_all | solution.py:143

commit v14 on v12

--- a/solution.py
+++ b/solution.py
@@ -18,11 +18,12 @@
     return sigma * (1.0 + values * (1.0 - sigma))
 
 
-def tile_kernel(count_ref, place_ref, fetch_ref, tiles_ref, src_ref, *refs, forward, block_rows):
+def tile_kernel(count_ref, place_ref, fetch_ref, tiles_ref, feed_ref, *refs, forward, block_rows):
     if block_rows:
-        keep_ref, give_ref, acc_ref = refs
+        weight_ref, keep_ref, give_ref, acc_ref, src_ref = refs
     else:
         out_ref, acc_ref = refs
+        src_ref = feed_ref
     step = pl.program_id(0)
     tile = tiles_ref.shape[1]
     group = tiles_ref.shape[0]
@@ -36,6 +37,17 @@
             return carry
 
         lax.fori_loop(0, out_rows // CHUNK, zero, 0)
+
+        if block_rows:
+
+            def project(k, carry):
+                rows = pl.ds(pl.multiple_of(k * CHUNK, CHUNK), CHUNK)
+                src_ref[rows, :] = jnp.dot(
+                    feed_ref[rows, :], weight_ref[...], preferred_element_type=jnp.float32
+                ).astype(src_ref.dtype)
+                return carry
+
+            lax.fori_loop(0, src_ref.shape[0] // CHUNK, project, 0)
 
     base = step * group
     live = jnp.clip(count_ref[0] - base, 0, group)
@@ -96,7 +108,9 @@
         lax.fori_loop(0, out_rows // CHUNK, emit, 0)
 
 
-def tile_products(tile_values, fetch_index, place_index, count, source, out_tiles, forward, block_rows=0):
+def tile_products(
+    tile_values, fetch_index, place_index, count, source, out_tiles, forward, block_rows=0, weight=None
+):
     slots, tile, _ = tile_values.shape
     hidden = source.shape[-1]
     src_rows = source.shape[0]
@@ -114,11 +128,13 @@
         in_specs=[
             pl.BlockSpec((group, tile, tile), tiles_map),
             pl.BlockSpec((src_rows, hidden), lambda i, *_: (0, 0)),
-        ],
+        ]
+        + ([pl.BlockSpec((hidden, hidden), lambda i, *_: (0, 0))] if block_rows else []),
         out_specs=[pl.BlockSpec((out_rows // 2, hidden), lambda i, *_: (0, 0))] * 2
         if block_rows
         else pl.BlockSpec((out_rows, hidden), lambda i, *_: (0, 0)),
-        scratch_shapes=[pltpu.VMEM((out_rows, hidden), jnp.float32)],
+        scratch_shapes=[pltpu.VMEM((out_rows, hidden), jnp.float32)]
+        + ([pltpu.VMEM((src_rows, hidden), jnp.bfloat16)] if block_rows else []),
     )
     flops = 2 * slots * tile * tile * hidden
     return pl.pallas_call(
@@ -135,7 +151,7 @@
             bytes_accessed=slots * tile * tile * 2 + src_rows * hidden * 2 + out_rows * hidden * 2,
             transcendentals=0,
         ),
-    )(count, place_index, fetch_index, tile_values, source)
+    )(count, place_index, fetch_index, tile_values, source, *([weight] if block_rows else []))
 
 
 def gather_rows(values, axes, parts):
@@ -162,12 +178,9 @@
     core = lax.axis_index("core")
     count = jnp.stack([tile_count.reshape(()), core.astype(jnp.int32)])
     features_block = gather_rows(features, "row", row_count)
-    panel_rows = jnp.dot(features_block, weight, preferred_element_type=jnp.float32).astype(
-        jnp.bfloat16
-    )
     swap = [(0, 1), (1, 0)]
     keep, give = tile_products(
-        tile_values, tile_col, tile_row, count, panel_rows, row_tiles, True, node_dev
+        tile_values, tile_col, tile_row, count, features_block, row_tiles, True, node_dev, weight
     )
     got = lax.ppermute(give, "core", swap)
     chip_sum = (keep.astype(jnp.float32) + got.astype(jnp.float32)).astype(jnp.bfloat16)

time: 208 us -> 210 us (level)
  Pallas kernels: 22.8 us -> 29.9 us
  starting transfers between devices: 21.5 us -> 15 us
    pallas_call x2, Pallas kernels: 22.8 us -> 29.9 us  [tile_products(): pl.pallas_call(functools.partial(tile_kernel, forward=forward, block_rows...]
    ppermute x1, starting transfers between devices: 6.67 us -> 0.09 us  [body(): got = lax.ppermute(give, 'core', swap)]
    all_to_all x2, blocking collectives: 66.5 us -> 69.2 us  [scatter_sum(): lax.all_to_all(values.reshape(parts, -1, values.shape[-1]), axes, 0, 0, t...]
where the time goes in v14:
time: 210 us; the launch traced here: 208 us
  blocking collectives  110 us (52%)
  waiting for transfers between devices  39.2 us (19%)
  Pallas kernels  29.9 us (14%)
  starting transfers between devices  15 us (7%)
  local copies, waits for them, and re-layouts  6.02 us (3%)
  other arithmetic  4.56 us (2%)
    all_to_all x2, blocking collectives, scatter_sum(): lax.all_to_all(values.reshape(parts, -1, values.shape[-1]), axes, 0, 0, t...  69.2 us
    all_to_all x2, blocking collectives, gather_rows(): lax.all_to_all(copies, axes, 0, 0, tiled=True).reshape(-1, values.shape[-1])  40.8 us
    all_to_all x2, waiting for transfers between devices, gather_rows(): lax.all_to_all(copies, axes, 0, 0, tiled=True).reshape(-1, values.shape[-1])  30.5 us
    pallas_call x2, Pallas kernels, tile_products(): pl.pallas_call(functools.partial(tile_kernel, forward=forward, block_rows...  29.9 us
    all_to_all x2, starting transfers between devices, gather_rows(): lax.all_to_all(copies, axes, 0, 0, tiled=True).reshape(-1, values.shape[-1])  9.49 us
  transfers between devices with their start and end apart: 5, of which 5 were waited for; matrix products, arithmetic and copies ran while one was open for 1% of the time, Pallas kernels for 0%

profile of v14, /device:TPU:1, one launch (start us, length us, event | category | flops | bytes accessed | tf_op | source)
XLA Modules:
  0.0 207.9 jit_solution(5053919823141363254)
XLA Ops:
  0.6 2.4 %broadcast_in_dim.8 = bf16[8,512,256]{2,1,0:T(8,128)(2,1)} broadcast(bf16[512,256]{1,0:T(8,128)(2,1)} %param.7), dimensions={1,2} | broadcast | bytes 2359296 | tf_op jit(solution)/shard_map/broadcast_in_dim | solution.py:158
  3.1 0.0 copy-start
  3.1 0.0 copy-start.1
  3.1 0.0 copy-start.2
  3.1 6.1 %all-to-all-start = ((bf16[8,512,256]{2,1,0:T(8,128)(2,1)}), bf16[8,512,256]{2,1,0:T(8,128)(2,1)S(1)}, u32[]{:S(2)}, u32[]{:S(2)}) async-start(bf16[8,512,256]{2,1,0:T(8,128)(2,1)} %broadcast_in_dim.8), calls=%async_computation | async-start | bytes 4194304 | tf_op jit(solution)/shard_map/all_to_all | solution.py:159
  9.8 0.1 pad_add_fusion.count_ref
  9.9 25.4 %all-to-all-done = bf16[8,512,256]{2,1,0:T(8,128)(2,1)S(1)} async-done(((bf16[8,512,256]{2,1,0:T(8,128)(2,1)}), bf16[8,512,256]{2,1,0:T(8,128)(2,1)S(1)}, u32[]{:S(2)}, u32[]{:S(2)}) %all-to-all-start) | async-done | bytes 2097184 | tf_op jit(solution)/shard_map/all_to_all | solution.py:159
  35.3 0.0 copy-start.3
  35.3 1.3 copy-done.3
  36.6 0.0 copy-done
  36.6 0.0 copy-done.1
  36.6 0.0 copy-done.2
  36.6 16.6 %shard_map.94 = (bf16[4096,256]{1,0:T(8,128)(2,1)S(1)}, bf16[4096,256]{1,0:T(8,128)(2,1)S(1)}) custom-call(s32[2]{0:T(128)S(1)} %pad_add_fusion.count_ref, s32[512]{0:T(512)S(1)} %copy-done.2, s32[512]{0:T(512)S(1)} %copy-done.1, bf16[512,128,128]{2,1,0:T(8,128)(2,1)} %tiles_ref.3, bf16[4096,256]{1,0:T(8,128)(2,1)} %bitcast.15, bf16[256,256]{1,0:T(8,128)(2,1)S(1)} %copy-done), custom_call_target="tpu_custom_call" | custom-call | flops 4294967296 | bytes 23068672 | tf_op jit(solution)/shard_map/pallas_call | solution.py:140
  53.2 0.1 collective-permute-start
  53.3 4.1 %collective-permute-done = bf16[4096,256]{1,0:T(8,128)(2,1)S(1)} collective-permute-done((bf16[4096,256]{1,0:T(8,128)(2,1)S(1)}, bf16[4096,256]{1,0:T(8,128)(2,1)S(1)}, u32[]{:S(2)}, u32[]{:S(2)}) %collective-permute-start) | collective-permute-done | bytes 2097184 | tf_op jit(solution)/shard_map/ppermute | solution.py:185
  57.4 0.5 add_convert_fusion
  58.0 37.5 %all_to_all.30 = bf16[8,512,256]{2,1,0:T(8,128)(2,1)S(1)} all-to-all(bf16[8,512,256]{2,1,0:T(8,128)(2,1)S(1)} %bitcast.17), channel_id=1, replica_groups=mesh['row'=8,'colhi'=8,'core'=2] {'colhi'}, dimensions={0} | all-to-all | bytes 4194304 | tf_op jit(solution)/shard_map/all_to_all | solution.py:163
  95.5 0.0 copy-start.5
  95.5 0.3 convert_reduce_fusion.1
  95.8 0.7 copy-done.5
  96.5 0.9 multiply_convert_fusion
  97.4 0.1 broadcast_in_dim.9
  97.5 29.9 %all_to_all.31 = bf16[8,512,256]{2,1,0:T(8,128)(2,1)S(1)} all-to-all(bf16[8,512,256]{2,1,0:T(8,128)(2,1)S(1)} %broadcast_in_dim.9), channel_id=1, replica_groups=mesh['row'=8,'colhi'=8,'core'=2] {'colhi'}, dimensions={0} | all-to-all | bytes 4194304 | tf_op jit(solution)/shard_map/all_to_all | solution.py:159
  127.5 2.4 %collective-permute-start.1 = (bf16[4096,256]{1,0:T(8,128)(2,1)S(1)}, bf16[4096,256]{1,0:T(8,128)(2,1)S(1)}, u32[]{:S(2)}, u32[]{:S(2)}) collective-permute-start(bf16[4096,256]{1,0:T(8,128)(2,1)S(1)} %bitcast.18), channel_id=1, source_target_pairs={{0,1},{1,0},{2,3},{3,2},{4,5},{5,4},{6,7},{7,6},{8,9},{9,8},{10,11... | collective-permute-start | bytes 6291464 | tf_op jit(solution)/shard_map/ppermute | solution.py:192
  129.9 3.8 %collective-permute-done.1 = bf16[4096,256]{1,0:T(8,128)(2,1)S(1)} collective-permute-done((bf16[4096,256]{1,0:T(8,128)(2,1)S(1)}, bf16[4096,256]{1,0:T(8,128)(2,1)S(1)}, u32[]{:S(2)}, u32[]{:S(2)}) %collective-permute-start.1) | collective-permute-done | bytes 2097184 | tf_op jit(solution)/shard_map/ppermute | solution.py:192
  133.6 2.2 %pad_maximum_fusion.feed_ref = bf16[8192,256]{1,0:T(8,128)(2,1)} fusion(bf16[4096,256]{1,0:T(8,128)(2,1)S(1)} %collective-permute-done.1, bf16[4096,256]{1,0:T(8,128)(2,1)S(1)} %bitcast.19), kind=kLoop, calls=%fused_computation.1 | loop fusion | flops 8388608 | bytes 8388608 | tf_op jit(solution)/shard_map/concatenate | solution.py:192
  135.8 0.0 copy-start.4
  135.8 13.3 %shard_map.95 = bf16[4096,256]{1,0:T(8,128)(2,1)S(1)} custom-call(s32[2]{0:T(128)S(1)} %pad_add_fusion.count_ref, s32[512]{0:T(512)S(1)} %copy-done.1, s32[512]{0:T(512)S(1)} %fusion.3.fetch_ref, bf16[512,128,128]{2,1,0:T(8,128)(2,1)} %tiles_ref.3, bf16[8192,256]{1,0:T(8,128)(2,1)} %pad_maximum_fusion.feed_ref), custom_call_target="tpu_custom_call" | custom-call | flops 4294967296 | bytes 23068672 | tf_op jit(solution)/shard_map/pallas_call | solution.py:140
  149.1 0.0 copy-done.4
  149.2 1.0 convolution_convert_fusion.1
  150.1 0.1 pad_maximum_fusion.1
  150.3 31.6 %all_to_all.32 = bf16[8,544,256]{2,1,0:T(8,128)(2,1)S(1)} all-to-all(bf16[8,544,256]{2,1,0:T(8,128)(2,1)S(1)} %pad_maximum_fusion.1), channel_id=1, replica_groups=mesh['row'=8,'colhi'=8,'core'=2] {'row'}, dimensions={0} | all-to-all | bytes 4456448 | tf_op jit(solution)/shard_map/all_to_all | solution.py:163
  181.9 0.3 convert_reduce_fusion
  182.2 3.0 %collective-permute-start.2 = (f32[32,256]{1,0:T(8,128)S(1)}, f32[32,256]{1,0:T(8,128)S(1)}, u32[]{:S(2)}, u32[]{:S(2)}) collective-permute-start(f32[32,256]{1,0:T(8,128)S(1)} %slice.11), channel_id=1, source_target_pairs={{0,1},{1,0},{2,3},{3,2},{4,5},{5,4},{6,7},{7,6},{8,9},{9,8},{10,11... | collective-permute-start | bytes 98312 | tf_op jit(solution)/shard_map/ppermute | solution.py:215
  185.3 0.9 collective-permute-done.2
  186.2 10.9 %all_to_all.33 = f32[8,32,256]{2,1,0:T(8,128)S(1)} all-to-all(f32[8,32,256]{2,1,0:T(8,128)S(1)} %broadcast_in_dim.10), channel_id=1, replica_groups=mesh['row'=8,'colhi'=8,'core'=2] {'colhi'}, dimensions={0} | all-to-all | bytes 524288 | tf_op jit(solution)/shard_map/all_to_all | solution.py:159
  197.1 0.7 broadcast_in_dim.11
  197.8 3.4 %all-to-all-start.5 = ((f32[8,32,256]{2,1,0:T(8,128)}), f32[8,32,256]{2,1,0:T(8,128)S(1)}, u32[]{:S(2)}, u32[]{:S(2)}) async-start(f32[8,32,256]{2,1,0:T(8,128)} %broadcast_in_dim.11), calls=%async_computation.5 | async-start | bytes 524288 | tf_op jit(solution)/shard_map/all_to_all | solution.py:159
  201.2 1.0 convolution_convert_fusion
  202.2 5.0 %all-to-all-done.5 = f32[8,32,256]{2,1,0:T(8,128)S(1)} async-done(((f32[8,32,256]{2,1,0:T(8,128)}), f32[8,32,256]{2,1,0:T(8,128)S(1)}, u32[]{:S(2)}, u32[]{:S(2)}) %all-to-all-start.5) | async-done | bytes 262176 | tf_op jit(solution)/shard_map/all_to_all | solution.py:159
  207.2 0.7 copy.12
  (5 shorter events, 0.1 us)
Async XLA Ops:
  3.1 33.5 %copy-start = (bf16[256,256]{1,0:T(8,128)(2,1)S(1)}, bf16[256,256]{1,0:T(8,128)(2,1)}, u32[]{:S(2)}) copy-start(bf16[256,256]{1,0:T(8,128)(2,1)} %refs_0_.1) | copy-start | bytes 393220
  3.1 33.5 %copy-start.1 = (s32[512]{0:T(512)S(1)}, s32[512]{0:T(512)}, u32[]{:S(2)}) copy-start(s32[512]{0:T(512)} %place_ref.3) | copy-start | bytes 6148
  3.1 33.5 %copy-start.2 = (s32[512]{0:T(512)S(1)}, s32[512]{0:T(512)}, u32[]{:S(2)}) copy-start(s32[512]{0:T(512)} %place_ref.2) | copy-start | bytes 6148
  3.1 32.2 %all-to-all-start = ((bf16[8,512,256]{2,1,0:T(8,128)(2,1)}), bf16[8,512,256]{2,1,0:T(8,128)(2,1)S(1)}, u32[]{:S(2)}, u32[]{:S(2)}) async-start(bf16[8,512,256]{2,1,0:T(8,128)(2,1)} %broadcast_in_dim.8), calls=%async_computation | async-start | bytes 4194304 | tf_op jit(solution)/shard_map/all_to_all | solution.py:159
  35.3 1.3 copy-start.3
  53.2 4.2 %collective-permute-start = (bf16[4096,256]{1,0:T(8,128)(2,1)S(1)}, bf16[4096,256]{1,0:T(8,128)(2,1)S(1)}, u32[]{:S(2)}, u32[]{:S(2)}) collective-permute-start(bf16[4096,256]{1,0:T(8,128)(2,1)S(1)} %get-tuple-element.6), channel_id=1, source_target_pairs={{0,1},{1,0},{2,3},{3,2},{4,5},{5,4},{6,7},{7,6},{8,9},{9,8},{10,11... | collective-permute-start | bytes 6291464 | tf_op jit(solution)/shard_map/ppermute | solution.py:185
  95.5 1.0 copy-start.5
  127.5 6.2 %collective-permute-start.1 = (bf16[4096,256]{1,0:T(8,128)(2,1)S(1)}, bf16[4096,256]{1,0:T(8,128)(2,1)S(1)}, u32[]{:S(2)}, u32[]{:S(2)}) collective-permute-start(bf16[4096,256]{1,0:T(8,128)(2,1)S(1)} %bitcast.18), channel_id=1, source_target_pairs={{0,1},{1,0},{2,3},{3,2},{4,5},{5,4},{6,7},{7,6},{8,9},{9,8},{10,11... | collective-permute-start | bytes 6291464 | tf_op jit(solution)/shard_map/ppermute | solution.py:192
  135.8 13.3 %copy-start.4 = (bf16[8,512,256]{2,1,0:T(8,128)(2,1)S(1)}, bf16[8,512,256]{2,1,0:T(8,128)(2,1)}, u32[]{:S(2)}) copy-start(bf16[8,512,256]{2,1,0:T(8,128)(2,1)} %copy-done.3) | copy-start | bytes 6291460
  182.2 3.9 %collective-permute-start.2 = (f32[32,256]{1,0:T(8,128)S(1)}, f32[32,256]{1,0:T(8,128)S(1)}, u32[]{:S(2)}, u32[]{:S(2)}) collective-permute-start(f32[32,256]{1,0:T(8,128)S(1)} %slice.11), channel_id=1, source_target_pairs={{0,1},{1,0},{2,3},{3,2},{4,5},{5,4},{6,7},{7,6},{8,9},{9,8},{10,11... | collective-permute-start | bytes 98312 | tf_op jit(solution)/shard_map/ppermute | solution.py:215
  197.8 9.4 %all-to-all-start.5 = ((f32[8,32,256]{2,1,0:T(8,128)}), f32[8,32,256]{2,1,0:T(8,128)S(1)}, u32[]{:S(2)}, u32[]{:S(2)}) async-start(f32[8,32,256]{2,1,0:T(8,128)} %broadcast_in_dim.11), calls=%async_computation.5 | async-start | bytes 524288 | tf_op jit(solution)/shard_map/all_to_all | solution.py:159

commit v15 on v12

--- a/solution.py
+++ b/solution.py
@@ -9,7 +9,7 @@
 
 
 GROUP = 64
-CHUNK = 256
+CHUNK = 512
 UNROLL = (64, 8, 1)
 
 

time: 208 us -> 207 us (level)
  Pallas kernels: 22.8 us -> 33 us
  starting transfers between devices: 21.5 us -> 13.4 us
  blocking collectives: 108 us -> 105 us
    pallas_call x2, Pallas kernels: 22.8 us -> 33 us  [tile_products(): pl.pallas_call(functools.partial(tile_kernel, forward=forward, block_rows...]
    ppermute x1, starting transfers between devices: 6.67 us -> 0.09 us  [body(): got = lax.ppermute(give, 'core', swap)]
where the time goes in v15:
time: 207 us; the launch traced here: 205 us
  blocking collectives  105 us (51%)
  waiting for transfers between devices  39.2 us (19%)
  Pallas kernels  33 us (16%)
  starting transfers between devices  13.4 us (6%)
  local copies, waits for them, and re-layouts  4.69 us (2%)
  other arithmetic  4.62 us (2%)
  matrix products  3.98 us (2%)
    all_to_all x2, blocking collectives, scatter_sum(): lax.all_to_all(values.reshape(parts, -1, values.shape[-1]), axes, 0, 0, t...  64.4 us
    all_to_all x2, blocking collectives, gather_rows(): lax.all_to_all(copies, axes, 0, 0, tiled=True).reshape(-1, values.shape[-1])  40.4 us
    pallas_call x2, Pallas kernels, tile_products(): pl.pallas_call(functools.partial(tile_kernel, forward=forward, block_rows...  33 us
    all_to_all x2, waiting for transfers between devices, gather_rows(): lax.all_to_all(copies, axes, 0, 0, tiled=True).reshape(-1, values.shape[-1])  30.5 us
    all_to_all x2, starting transfers between devices, gather_rows(): lax.all_to_all(copies, axes, 0, 0, tiled=True).reshape(-1, values.shape[-1])  9.36 us
    ppermute x1, waiting for transfers between devices, body(): got = lax.ppermute(give, 'core', swap)  4.15 us
  transfers between devices with their start and end apart: 5, of which 5 were waited for; matrix products, arithmetic and copies ran while one was open for 1% of the time, Pallas kernels for 0%

profile of v15, /device:TPU:1, one launch (start us, length us, event | category | flops | bytes accessed | tf_op | source)
XLA Modules:
  0.0 205.2 jit_solution(1060156716735450497)
XLA Ops:
  0.6 0.0 copy-start
  0.6 2.4 %broadcast_in_dim.8 = bf16[8,512,256]{2,1,0:T(8,128)(2,1)} broadcast(bf16[512,256]{1,0:T(8,128)(2,1)} %param.7), dimensions={1,2} | broadcast | bytes 2359296 | tf_op jit(solution)/shard_map/broadcast_in_dim | solution.py:142
  3.1 5.9 %all-to-all-start = ((bf16[8,512,256]{2,1,0:T(8,128)(2,1)}), bf16[8,512,256]{2,1,0:T(8,128)(2,1)S(1)}, u32[]{:S(2)}, u32[]{:S(2)}) async-start(bf16[8,512,256]{2,1,0:T(8,128)(2,1)} %broadcast_in_dim.8), calls=%async_computation | async-start | bytes 4194304 | tf_op jit(solution)/shard_map/all_to_all | solution.py:143
  9.7 0.1 pad_add_fusion.count_ref
  9.8 25.4 %all-to-all-done = bf16[8,512,256]{2,1,0:T(8,128)(2,1)S(1)} async-done(((bf16[8,512,256]{2,1,0:T(8,128)(2,1)}), bf16[8,512,256]{2,1,0:T(8,128)(2,1)S(1)}, u32[]{:S(2)}, u32[]{:S(2)}) %all-to-all-start) | async-done | bytes 2097184 | tf_op jit(solution)/shard_map/all_to_all | solution.py:143
  35.2 0.0 copy-done
  35.2 0.0 copy-start.1
  35.2 0.0 copy-start.2
  35.2 2.0 convolution_convert_fusion.src_ref
  37.2 0.0 copy-done.1
  37.2 0.0 copy-done.2
  37.2 16.6 %shard_map.94 = (bf16[4096,256]{1,0:T(8,128)(2,1)S(1)}, bf16[4096,256]{1,0:T(8,128)(2,1)S(1)}) custom-call(s32[2]{0:T(128)S(1)} %pad_add_fusion.count_ref, s32[512]{0:T(512)S(1)} %copy-done.2, s32[512]{0:T(512)S(1)} %copy-done.1, bf16[512,128,128]{2,1,0:T(8,128)(2,1)} %tiles_ref.3, bf16[4096,256]{1,0:T(8,128)(2,1)} %convolution_convert_fusion.src_ref), custom_call_target="tpu_custom_call" | custom-call | flops 4294967296 | bytes 23068672 | tf_op jit(solution)/shard_map/pallas_call | solution.py:124
  53.8 0.1 collective-permute-start
  53.9 4.1 %collective-permute-done = bf16[4096,256]{1,0:T(8,128)(2,1)S(1)} collective-permute-done((bf16[4096,256]{1,0:T(8,128)(2,1)S(1)}, bf16[4096,256]{1,0:T(8,128)(2,1)S(1)}, u32[]{:S(2)}, u32[]{:S(2)}) %collective-permute-start) | collective-permute-done | bytes 2097184 | tf_op jit(solution)/shard_map/ppermute | solution.py:172
  58.1 0.6 add_convert_fusion
  58.6 34.2 %all_to_all.30 = bf16[8,512,256]{2,1,0:T(8,128)(2,1)S(1)} all-to-all(bf16[8,512,256]{2,1,0:T(8,128)(2,1)S(1)} %bitcast.19), channel_id=1, replica_groups=mesh['row'=8,'colhi'=8,'core'=2] {'colhi'}, dimensions={0} | all-to-all | bytes 4194304 | tf_op jit(solution)/shard_map/all_to_all | solution.py:147
  92.8 0.0 copy-start.3
  92.8 0.3 convert_reduce_fusion.1
  93.1 0.6 copy-done.3
  93.7 0.9 multiply_convert_fusion
  94.7 0.1 broadcast_in_dim.9
  94.8 29.9 %all_to_all.31 = bf16[8,512,256]{2,1,0:T(8,128)(2,1)S(1)} all-to-all(bf16[8,512,256]{2,1,0:T(8,128)(2,1)S(1)} %broadcast_in_dim.9), channel_id=1, replica_groups=mesh['row'=8,'colhi'=8,'core'=2] {'colhi'}, dimensions={0} | all-to-all | bytes 4194304 | tf_op jit(solution)/shard_map/all_to_all | solution.py:143
  124.7 2.4 %collective-permute-start.1 = (bf16[4096,256]{1,0:T(8,128)(2,1)S(1)}, bf16[4096,256]{1,0:T(8,128)(2,1)S(1)}, u32[]{:S(2)}, u32[]{:S(2)}) collective-permute-start(bf16[4096,256]{1,0:T(8,128)(2,1)S(1)} %bitcast.20), channel_id=1, source_target_pairs={{0,1},{1,0},{2,3},{3,2},{4,5},{5,4},{6,7},{7,6},{8,9},{9,8},{10,11... | collective-permute-start | bytes 6291464 | tf_op jit(solution)/shard_map/ppermute | solution.py:179
  127.1 3.8 %collective-permute-done.1 = bf16[4096,256]{1,0:T(8,128)(2,1)S(1)} collective-permute-done((bf16[4096,256]{1,0:T(8,128)(2,1)S(1)}, bf16[4096,256]{1,0:T(8,128)(2,1)S(1)}, u32[]{:S(2)}, u32[]{:S(2)}) %collective-permute-start.1) | collective-permute-done | bytes 2097184 | tf_op jit(solution)/shard_map/ppermute | solution.py:179
  130.9 2.2 %pad_maximum_fusion.src_ref = bf16[8192,256]{1,0:T(8,128)(2,1)} fusion(bf16[4096,256]{1,0:T(8,128)(2,1)S(1)} %collective-permute-done.1, bf16[4096,256]{1,0:T(8,128)(2,1)S(1)} %bitcast.21), kind=kLoop, calls=%fused_computation.2 | loop fusion | flops 8388608 | bytes 8388608 | tf_op jit(solution)/shard_map/concatenate | solution.py:179
  133.1 16.5 %shard_map.95 = bf16[4096,256]{1,0:T(8,128)(2,1)S(1)} custom-call(s32[2]{0:T(128)S(1)} %pad_add_fusion.count_ref, s32[512]{0:T(512)S(1)} %copy-done.1, s32[512]{0:T(512)S(1)} %fusion.3.fetch_ref, bf16[512,128,128]{2,1,0:T(8,128)(2,1)} %tiles_ref.3, bf16[8192,256]{1,0:T(8,128)(2,1)} %pad_maximum_fusion.src_ref), custom_call_target="tpu_custom_call" | custom-call | flops 4294967296 | bytes 23068672 | tf_op jit(solution)/shard_map/pallas_call | solution.py:124
  149.6 1.0 convolution_convert_fusion.2
  150.6 0.1 pad_maximum_fusion.1
  150.7 30.3 %all_to_all.32 = bf16[8,544,256]{2,1,0:T(8,128)(2,1)S(1)} all-to-all(bf16[8,544,256]{2,1,0:T(8,128)(2,1)S(1)} %pad_maximum_fusion.1), channel_id=1, replica_groups=mesh['row'=8,'colhi'=8,'core'=2] {'row'}, dimensions={0} | all-to-all | bytes 4456448 | tf_op jit(solution)/shard_map/all_to_all | solution.py:147
  181.0 0.3 convert_reduce_fusion
  181.3 1.6 collective-permute-start.2
  182.9 0.9 collective-permute-done.2
  183.8 10.5 %all_to_all.33 = f32[8,32,256]{2,1,0:T(8,128)S(1)} all-to-all(f32[8,32,256]{2,1,0:T(8,128)S(1)} %broadcast_in_dim.10), channel_id=1, replica_groups=mesh['row'=8,'colhi'=8,'core'=2] {'colhi'}, dimensions={0} | all-to-all | bytes 524288 | tf_op jit(solution)/shard_map/all_to_all | solution.py:143
  194.3 0.7 broadcast_in_dim.11
  195.0 3.4 %all-to-all-start.5 = ((f32[8,32,256]{2,1,0:T(8,128)}), f32[8,32,256]{2,1,0:T(8,128)S(1)}, u32[]{:S(2)}, u32[]{:S(2)}) async-start(f32[8,32,256]{2,1,0:T(8,128)} %broadcast_in_dim.11), calls=%async_computation.5 | async-start | bytes 524288 | tf_op jit(solution)/shard_map/all_to_all | solution.py:143
  198.5 1.0 convolution_convert_fusion.1
  199.4 5.1 %all-to-all-done.5 = f32[8,32,256]{2,1,0:T(8,128)S(1)} async-done(((f32[8,32,256]{2,1,0:T(8,128)}), f32[8,32,256]{2,1,0:T(8,128)S(1)}, u32[]{:S(2)}, u32[]{:S(2)}) %all-to-all-start.5) | async-done | bytes 262176 | tf_op jit(solution)/shard_map/all_to_all | solution.py:143
  204.5 0.7 copy.12
  (5 shorter events, 0.1 us)
Async XLA Ops:
  0.6 34.6 %copy-start = (bf16[256,256]{1,0:T(8,128)(2,1)S(1)}, bf16[256,256]{1,0:T(8,128)(2,1)}, u32[]{:S(2)}) copy-start(bf16[256,256]{1,0:T(8,128)(2,1)} %param.8) | copy-start | bytes 393220
  3.1 32.1 %all-to-all-start = ((bf16[8,512,256]{2,1,0:T(8,128)(2,1)}), bf16[8,512,256]{2,1,0:T(8,128)(2,1)S(1)}, u32[]{:S(2)}, u32[]{:S(2)}) async-start(bf16[8,512,256]{2,1,0:T(8,128)(2,1)} %broadcast_in_dim.8), calls=%async_computation | async-start | bytes 4194304 | tf_op jit(solution)/shard_map/all_to_all | solution.py:143
  35.2 2.0 copy-start.1
  35.2 2.0 copy-start.2
  53.8 4.2 %collective-permute-start = (bf16[4096,256]{1,0:T(8,128)(2,1)S(1)}, bf16[4096,256]{1,0:T(8,128)(2,1)S(1)}, u32[]{:S(2)}, u32[]{:S(2)}) collective-permute-start(bf16[4096,256]{1,0:T(8,128)(2,1)S(1)} %get-tuple-element.6), channel_id=1, source_target_pairs={{0,1},{1,0},{2,3},{3,2},{4,5},{5,4},{6,7},{7,6},{8,9},{9,8},{10,11... | collective-permute-start | bytes 6291464 | tf_op jit(solution)/shard_map/ppermute | solution.py:172
  92.8 1.0 copy-start.3
  124.7 6.2 %collective-permute-start.1 = (bf16[4096,256]{1,0:T(8,128)(2,1)S(1)}, bf16[4096,256]{1,0:T(8,128)(2,1)S(1)}, u32[]{:S(2)}, u32[]{:S(2)}) collective-permute-start(bf16[4096,256]{1,0:T(8,128)(2,1)S(1)} %bitcast.20), channel_id=1, source_target_pairs={{0,1},{1,0},{2,3},{3,2},{4,5},{5,4},{6,7},{7,6},{8,9},{9,8},{10,11... | collective-permute-start | bytes 6291464 | tf_op jit(solution)/shard_map/ppermute | solution.py:179
  181.3 2.4 %collective-permute-start.2 = (f32[32,256]{1,0:T(8,128)S(1)}, f32[32,256]{1,0:T(8,128)S(1)}, u32[]{:S(2)}, u32[]{:S(2)}) collective-permute-start(f32[32,256]{1,0:T(8,128)S(1)} %slice.11), channel_id=1, source_target_pairs={{0,1},{1,0},{2,3},{3,2},{4,5},{5,4},{6,7},{7,6},{8,9},{9,8},{10,11... | collective-permute-start | bytes 98312 | tf_op jit(solution)/shard_map/ppermute | solution.py:202
  195.0 9.4 %all-to-all-start.5 = ((f32[8,32,256]{2,1,0:T(8,128)}), f32[8,32,256]{2,1,0:T(8,128)S(1)}, u32[]{:S(2)}, u32[]{:S(2)}) async-start(f32[8,32,256]{2,1,0:T(8,128)} %broadcast_in_dim.11), calls=%async_computation.5 | async-start | bytes 524288 | tf_op jit(solution)/shard_map/all_to_all | solution.py:143
